TPU v7x, 32 devices: a whole 2x2x4 slice. The times are simulated.
32 devices in a mesh: tmpl: 4 (over z), chan: 4 (over y, core), tm: 2 (over x).
Axes of the slice: x: 2, y: 2, z: 4, core: 2. Of those that a mesh axis runs over, the one named last changes fastest.
Arguments:
- raw: bfloat16 [256, 4096], P('chan', ('tmpl', 'tm')), may hold values from -6 to 6
- dead_mask: int32 [256], P('chan'), may hold values 0 or 1
- templates: bfloat16 [16, 256, 512], P('tmpl', 'chan'), may hold values from -0.015625 to 0.015625
- assign: int32 [16], P('tmpl'), may hold values from 0 to 15, as said below
- w_enc: bfloat16 [16, 1, 3, 3], replicated, may hold values from -2 to 2
- b_enc: float32 [16], replicated, may hold values from -3 to 3
- w_mid: bfloat16 [32, 16, 3, 3], replicated, may hold values from -0.5 to 0.5
- b_mid: float32 [32], replicated, may hold values from -3 to 3
- w_dec: bfloat16 [16, 48, 3, 3], replicated, may hold values from -0.3125 to 0.3125
- b_dec: float32 [16], replicated, may hold values from -3 to 3
- w_out: bfloat16 [16], replicated, may hold values from -1.5 to 1.5
- b_out: float32 [1], replicated, may hold values from -3 to 3
Outputs:
- denoised: bfloat16 [256, 4096], P('chan', ('tmpl', 'tm'))
- corr: float32 [16, 4, 2, 512], P('tmpl', None, 'tm', 'chan')
Inputs may be any that keep to these rules, and one draw needn't show every extreme that they name: `assign`: for each j, entries 4 * j to 4 * j + 3 hold exactly those numbers in some order.
All inputs are finite; a program needn't handle non-finite values. No bound on the sum of `dead_mask` on one device may be relied on, other than what follows from the above.
Results may differ from a plain program's by a relative error of at most 0.018.
Values may be sent and summed in bfloat16 or wider, within the bound.
No kernel may reach another device: no remote copies, remote signals or barrier semaphores. Data moves between devices by JAX's collectives and lax.ppermute only.
A program may use at most 128 MiB of HBM per device.

v0:
```python
import functools
import math

import jax
import jax.numpy as jnp
import numpy as np
from jax import lax
from jax.experimental import pallas as pl
from jax.experimental.pallas import tpu as pltpu
from jax.sharding import PartitionSpec as P

BF = jnp.bfloat16
F32 = jnp.float32
EDGE = 8
ENC_ROWS = 8
MID_ROWS = 7
DEC_ROWS = 8
OFF = -1e30


def frequency_order(patch_len):
    return np.concatenate([np.arange(0, patch_len, 2), np.arange(1, patch_len, 2)])


def forward_table(patch_len):
    s = np.arange(patch_len)[:, None]
    f = frequency_order(patch_len)[None, :]
    phase = ((s * f) % (2 * patch_len)).astype(np.float64) * (math.pi / patch_len)
    table = np.concatenate([np.cos(phase), np.sin(phase)], axis=1)
    table[:, patch_len] = 1.0 - 2.0 * (np.arange(patch_len) % 2)
    return table.astype(jnp.bfloat16)


def inverse_table(patch_len):
    table = forward_table(patch_len).astype(np.float32).T.copy()
    table[0] *= 0.5
    table[patch_len] *= 0.5
    return table.astype(jnp.bfloat16)


def dot(a, b):
    return jnp.dot(a, b, preferred_element_type=F32)


def iota(shape, dim):
    return lax.broadcasted_iota(jnp.int32, shape, dim)


def column(row, count):
    m = row.shape[1]
    pick = iota((count, m), 0) % m == iota((count, m), 1)
    return jnp.sum(jnp.where(pick, row, 0.0), axis=1, keepdims=True)


def prep_kernel(
    we_ref, wm_ref, ws_ref, wu_ref, be_ref, bm_ref, bd_ref, wo_ref,
    enc_ref, mid_ref, dec_ref, out_ref, benc_ref, bmid_ref, bdec_ref, wide_ref,
):
    maps = we_ref.shape[0]
    half = benc_ref.shape[1]
    rows, cols = enc_ref.shape
    window = ENC_ROWS + EDGE
    spread = jnp.where(iota((rows, maps), 0) % maps == iota((rows, maps), 1), 1.0, 0.0).astype(BF)
    taps = dot(spread, we_ref[...])
    row_id = iota((rows, cols), 0)
    col_id = iota((rows, cols), 1)
    dy = col_id % window - row_id // (4 * maps) - (EDGE // 2 - 1)
    dx = col_id // window - row_id // maps % 4
    tap = jnp.where((dy >= 0) & (dy < 3) & (dx >= 0) & (dx < 3), dy * 3 + dx, -1)
    acc = jnp.zeros((rows, cols), F32)
    for t in range(9):
        acc = jnp.where(tap == t, taps[:, t : t + 1], acc)
    enc_ref[...] = acc.astype(BF)
    wide_ref[...] = jnp.zeros(wide_ref.shape, F32)
    wm = wm_ref[...].astype(F32)
    for r in range(MID_ROWS):
        wide_ref[r * 2 * maps : (r + 1) * 2 * maps, r * 3 * maps : r * 3 * maps + 9 * maps] = wm
    mid_ref[...] = wide_ref[: mid_ref.shape[0], : mid_ref.shape[1]].astype(BF)
    wide_ref[...] = jnp.zeros(wide_ref.shape, F32)
    ws = ws_ref[...].astype(F32)
    wu = wu_ref[...].astype(F32)
    skip_cols = (DEC_ROWS + 2) * 4 * maps
    k = [[wu[:, (y * 3 + x) * 2 * maps : (y * 3 + x + 1) * 2 * maps] for x in range(3)] for y in range(3)]
    for r in range(DEC_ROWS):
        ys = ((0,), (1, 2)) if r % 2 == 0 else ((0, 1), (2,))
        for q in range(2):
            top = (r * 2 + q) * maps
            for y in range(3):
                left = ((r + y) * 4 + q) * maps
                wide_ref[top : top + maps, left : left + 3 * maps] = ws[:, y * 3 * maps : (y + 1) * 3 * maps]
            xs = ((0,), (1, 2)) if q == 0 else ((0, 1), (2,))
            for a in range(2):
                for b in range(2):
                    value = sum(k[y][x] for y in ys[a] for x in xs[b])
                    left = skip_cols + ((r + 1) // 2 + a) * 6 * maps + (q + b) * 2 * maps
                    wide_ref[top : top + maps, left : left + 2 * maps] = value
    dec_ref[...] = wide_ref[...].astype(BF)
    n = out_ref.shape[1]
    repeat = jnp.where(iota((maps, n), 1) % maps == iota((maps, n), 0), 1.0, 0.0).astype(BF)
    weights = dot(wo_ref[...], repeat)
    r_id = iota(out_ref.shape, 0)
    c_id = iota(out_ref.shape, 1)
    same = (c_id // (2 * maps) == r_id % DEC_ROWS) & (c_id // maps % 2 == r_id // DEC_ROWS)
    out_ref[...] = jnp.where(same, weights, 0.0).astype(BF)
    lane = iota((4 * maps, half), 1)
    q = iota((4 * maps, half), 0) // maps
    outside = ((q == 0) & (lane == 0)) | ((q == 3) & (lane == half - 1))
    benc_ref[...] = jnp.where(outside, OFF, column(be_ref[...], 4 * maps))
    bmid_ref[...] = jnp.broadcast_to(column(bm_ref[...], 2 * maps), bmid_ref.shape)
    bdec_ref[...] = jnp.broadcast_to(column(bd_ref[...], 2 * maps), bdec_ref.shape)


def shifted(x, by):
    width = x.shape[1]
    lane = iota(x.shape, 1)
    edge = 0 if by < 0 else width - 1
    return jnp.where(lane == edge, 0.0, pltpu.roll(x, (-by) % width, 1))


def unet_kernel(
    raw_ref, mask_ref, r1_ref, r2_ref, enc_ref, mid_ref, dec_ref, wout_ref, benc_ref, bmid_ref, bdec_ref, bout_ref,
    out_ref, xs_ref, e4_ref, p3_ref, m3_ref, de_ref, do_ref,
):
    rows, length = raw_ref.shape
    half = length // 2
    maps = benc_ref.shape[0] // 4
    here = lax.axis_index("chan")
    last = lax.axis_size("chan") - 1
    odd = here % 2 == 1
    keep_top = jnp.where(here == 0, 0.0, 1.0)
    keep_bottom = jnp.where(here == last, 0.0, 1.0)
    alive = column(mask_ref[...].astype(F32), rows)
    r1 = r1_ref[...].astype(F32)
    r2 = r2_ref[...].astype(F32)
    cleaned = raw_ref[...].astype(F32) * alive
    x = jnp.concatenate([jnp.where(odd, r1, r2), cleaned, jnp.where(odd, r2, r1)], axis=0).astype(BF)
    s = iota((length, half), 0)
    t = iota((length, half), 1)
    even = dot(x, jnp.where(s == 2 * t, 1.0, 0.0).astype(BF))
    uneven = dot(x, jnp.where(s == 2 * t + 1, 1.0, 0.0).astype(BF))
    for d, piece in enumerate((shifted(even, -1), shifted(uneven, -1), even, uneven, shifted(even, 1), shifted(uneven, 1))):
        xs_ref[d] = piece
    span = 4 * maps
    groups = (rows + EDGE) // ENC_ROWS
    margin = EDGE // 2
    p3_ref[...] = jnp.zeros(p3_ref.shape, BF)
    for g in range(groups):
        start = g * ENC_ROWS
        window = jnp.concatenate([xs_ref[d, start : start + ENC_ROWS + EDGE, :] for d in range(6)], axis=0).astype(BF)
        y = dot(enc_ref[...], window).reshape(ENC_ROWS, span, half)
        y = jnp.maximum(y + benc_ref[...][None], 0.0)
        pieces = []
        for r in range(ENC_ROWS):
            row = start + r - margin
            piece = y[r]
            if row < 0:
                piece = piece * keep_top
            if row >= rows:
                piece = piece * keep_bottom
            piece = piece.astype(BF)
            e4_ref[(start + r) * span : (start + r + 1) * span, :] = piece
            pieces.append(piece[maps : 3 * maps].astype(F32))
        for r in range(0, ENC_ROWS, 2):
            both = pieces[r] + pieces[r + 1]
            pooled = ((both[:maps] + both[maps:]) * 0.25).astype(BF).astype(F32)
            at = (start + r) // 2 * 3 * maps
            p3_ref[at : at + 3 * maps, :] = jnp.concatenate([shifted(pooled, -1), pooled, shifted(pooled, 1)], axis=0).astype(BF)
    span_p = 3 * maps
    span_m = 6 * maps
    mid_total = rows // 2 + 2
    for g in range(-(-mid_total // MID_ROWS)):
        start = g * MID_ROWS
        y = dot(mid_ref[...], p3_ref[start * span_p : (start + MID_ROWS + 2) * span_p, :]).reshape(MID_ROWS, 2 * maps, half)
        y = jnp.maximum(y + bmid_ref[...][None], 0.0)
        for r in range(MID_ROWS):
            row = start + r - 1
            if row > rows // 2:
                continue
            piece = y[r]
            if row < 0:
                piece = piece * keep_top
            if row >= rows // 2:
                piece = piece * keep_bottom
            piece = piece.astype(BF).astype(F32)
            m3_ref[(start + r) * span_m : (start + r + 1) * span_m, :] = jnp.concatenate(
                [shifted(piece, -1), piece, shifted(piece, 1)], axis=0
            ).astype(BF)
    for g in range(rows // DEC_ROWS):
        start = g * DEC_ROWS
        skip = e4_ref[(start + margin - 1) * span : (start + margin + DEC_ROWS + 1) * span, :]
        up = m3_ref[start // 2 * span_m : (start // 2 + DEC_ROWS // 2 + 2) * span_m, :]
        y = dot(dec_ref[...], jnp.concatenate([skip, up], axis=0)).reshape(DEC_ROWS, 2 * maps, half)
        y = jnp.maximum(y + bdec_ref[...][None], 0.0).astype(BF).reshape(DEC_ROWS * 2 * maps, half)
        branch = dot(wout_ref[...], y)
        live = alive[start : start + DEC_ROWS]
        at = start + EDGE
        for q, ref in ((0, de_ref), (1, do_ref)):
            own = xs_ref[2 + q, at : at + DEC_ROWS, :]
            ref[start : start + DEC_ROWS, :] = live * (own + branch[q * DEC_ROWS : (q + 1) * DEC_ROWS] + bout_ref[0])
    s = iota((half, length), 1)
    t = iota((half, length), 0)
    out_ref[...] = (
        dot(de_ref[...].astype(BF), jnp.where(s == 2 * t, 1.0, 0.0).astype(BF))
        + dot(do_ref[...].astype(BF), jnp.where(s == 2 * t + 1, 1.0, 0.0).astype(BF))
    ).astype(BF)


def template_kernel(t_ref, table_ref, a_ref, b_ref, first_ref):
    count, rows, length = t_ref.shape
    for k in range(count):
        y = dot(t_ref[k], table_ref[...]).astype(BF).astype(F32)
        a = y[:, :length]
        b = y[:, length:]
        lane = iota(a.shape, 1)
        a_ref[k] = a
        b_ref[k] = jnp.where(lane == 0, 0.0, b)
        first_ref[k] = jnp.where(lane == 0, b, a)[:, :128]


def corr_kernel(count, *refs):
    x_refs = refs[:count]
    ta_ref, tb_ref, tf_ref, table_ref, inverse_ref, assign_ref = refs[count : count + 6]
    outs = refs[count + 6 : -3]
    sa_ref, p_ref, share_ref = refs[-3:]
    rows, length = x_refs[0].shape
    tmpl = ta_ref.shape[0]
    here = lax.axis_index("tmpl")
    for k in range(count):
        sa_ref[(here - k) % count] = dot(x_refs[k][...], table_ref[...]).astype(BF).astype(F32)
    picks = [assign_ref[r] % tmpl for r in range(tmpl)]
    for lane in range(0, length, 128):
        real = [[None] * count for _ in range(tmpl)]
        imag = [[None] * count for _ in range(tmpl)]
        for c in range(0, rows, 8):
            at = [ta_ref[picks[r], c : c + 8, lane : lane + 128] for r in range(tmpl)]
            bt = [tb_ref[picks[r], c : c + 8, lane : lane + 128] for r in range(tmpl)]
            af = at if lane else [tf_ref[picks[r], c : c + 8, :] for r in range(tmpl)]
            for i in range(count):
                ax = sa_ref[i, c : c + 8, lane : lane + 128]
                bx = sa_ref[i, c : c + 8, length + lane : length + lane + 128]
                for r in range(tmpl):
                    re = ax * at[r] + bx * bt[r]
                    im = bx * af[r] - ax * bt[r]
                    real[r][i] = re if c == 0 else real[r][i] + re
                    imag[r][i] = im if c == 0 else imag[r][i] + im
        for r in range(tmpl):
            for i in range(count):
                row = r * count + i
                p_ref[row : row + 1, lane : lane + 128] = jnp.sum(real[r][i], axis=0, keepdims=True)
                p_ref[row : row + 1, length + lane : length + lane + 128] = jnp.sum(imag[r][i], axis=0, keepdims=True)
    p = p_ref[...]
    high = p.astype(BF)
    low = (p - high.astype(F32)).astype(BF)
    pairs = tmpl * count
    both = jnp.concatenate([high, low], axis=0)
    half = length // 2

    def part(first):
        y = dot(both[:, first : first + half], inverse_ref[first : first + half, :]) + dot(
            both[:, length + first : length + first + half], inverse_ref[length + first : length + first + half, :]
        )
        return (y[:pairs] + y[pairs:]) * (1.0 / length)

    even = part(0)
    uneven = part(half)
    near = even + uneven
    far = even - uneven
    block = iota(far.shape, 0) % count
    later = jnp.where(block == count - 1, 0.0, pltpu.roll(far, pairs - 1, 0))
    parity = lax.axis_index("tm")
    far = jnp.where(parity == 1, far, later)
    width = share_ref.shape[3]
    chans = share_ref.shape[1]
    for c in range(chans):
        share_ref[0, c] = near[:, c * width : (c + 1) * width]
        share_ref[1, c] = far[:, c * width : (c + 1) * width]
    chan = lax.axis_index("chan")
    for k, out in enumerate(outs):
        to = (chan * 2 + parity + k) % (2 * chans)
        out[...] = share_ref[(to + parity) % 2, to // 2].astype(BF)


def call(kernel, outs, scratch=(), smem=(), inputs=0, name=None):
    return pl.pallas_call(
        kernel,
        out_shape=tuple(jax.ShapeDtypeStruct(s, d) for s, d in outs),
        in_specs=[
            pl.BlockSpec(memory_space=pltpu.SMEM if i in smem else pltpu.VMEM) for i in range(inputs)
        ],
        out_specs=tuple(pl.BlockSpec(memory_space=pltpu.VMEM) for _ in outs),
        scratch_shapes=scratch,
        name=name,
        compiler_params=pltpu.CompilerParams(vmem_limit_bytes=48 * 1024 * 1024),
    )


def rotated(x, axes, by):
    count = lax.axis_size(axes)
    return lax.ppermute(x, axes, [(i, (i + by) % count) for i in range(count)])


def body(raw, dead_mask, templates, assign, w_enc, b_enc, w_mid, b_mid, w_dec, b_dec, w_out, b_out):
    rows, length = raw.shape
    half = length // 2
    maps = w_enc.shape[0]
    chans = lax.axis_size("chan")
    blocks = lax.axis_size("tmpl")
    tmpl = templates.shape[0]
    odd = lax.axis_index("chan") % 2 == 1
    alive = dead_mask.astype(BF)[:, None]
    head = raw[:EDGE] * alive[:EDGE]
    tail = raw[-EDGE:] * alive[-EDGE:]
    r1 = lax.ppermute(jnp.where(odd, head, tail), "chan", [(i, i ^ 1) for i in range(chans) if i ^ 1 < chans])
    links = [(i, i + 1) for i in range(1, chans - 1, 2)]
    r2 = lax.ppermute(jnp.where(odd, tail, head), "chan", links + [(b, a) for a, b in links])

    dec_cols = (DEC_ROWS + 2) * 4 * maps + (DEC_ROWS // 2 + 2) * 6 * maps
    weights = call(
        prep_kernel,
        [
            ((ENC_ROWS * 4 * maps, 6 * (ENC_ROWS + EDGE)), BF),
            ((MID_ROWS * 2 * maps, (MID_ROWS + 2) * 3 * maps), BF),
            ((DEC_ROWS * 2 * maps, dec_cols), BF),
            ((2 * DEC_ROWS, DEC_ROWS * 2 * maps), BF),
            ((4 * maps, half), F32),
            ((2 * maps, half), F32),
            ((2 * maps, half), F32),
        ],
        [pltpu.VMEM((DEC_ROWS * 2 * maps, dec_cols), F32)],
        inputs=8,
        name="prep",
    )(
        w_enc.reshape(maps, 9),
        w_mid.transpose(0, 2, 3, 1).reshape(2 * maps, 9 * maps),
        w_dec[:, 2 * maps :].transpose(0, 2, 3, 1).reshape(maps, 9 * maps),
        w_dec[:, : 2 * maps].transpose(0, 2, 3, 1).reshape(maps, 18 * maps),
        b_enc[None],
        b_mid[None],
        b_dec[None],
        w_out[None],
    )
    mid_groups = -(-(rows // 2 + 2) // MID_ROWS)
    (denoised,) = call(
        unet_kernel,
        [((rows, length), BF)],
        [
            pltpu.VMEM((6, rows + 2 * EDGE, half), F32),
            pltpu.VMEM(((rows + EDGE) * 4 * maps, half), BF),
            pltpu.VMEM(((mid_groups * MID_ROWS + 2) * 3 * maps, half), BF),
            pltpu.VMEM(((rows // 2 + 2) * 6 * maps, half), BF),
            pltpu.VMEM((rows, half), F32),
            pltpu.VMEM((rows, half), F32),
        ],
        smem=(11,),
        inputs=12,
        name="unet",
    )(raw, dead_mask[None], r1, r2, *weights, b_out)

    forward = jnp.asarray(forward_table(length))
    inverse = jnp.asarray(inverse_table(length))
    spectra_t = call(
        template_kernel,
        [((tmpl, rows, length), F32), ((tmpl, rows, length), F32), ((tmpl, rows, 128), F32)],
        inputs=2,
        name="tspectra",
    )(templates, forward)
    gathered = [denoised] + [rotated(denoised, "tmpl", k) for k in range(1, blocks)]
    width = length // chans
    pairs = tmpl * blocks
    sent = call(
        functools.partial(corr_kernel, blocks),
        [((pairs, width), BF)] * (2 * chans),
        [
            pltpu.VMEM((blocks, rows, 2 * length), F32),
            pltpu.VMEM((pairs, 2 * length), F32),
            pltpu.VMEM((2, chans, pairs, width), F32),
        ],
        smem=(blocks + 5,),
        inputs=blocks + 6,
        name="corr",
    )(*gathered, *spectra_t, forward, inverse, assign)
    total = sent[0].astype(F32)
    for k in range(1, 2 * chans):
        total = total + rotated(sent[k], ("chan", "tm"), k).astype(F32)
    return denoised, total.reshape(tmpl, blocks, 1, width)


def solution(mesh):
    return jax.shard_map(
        body,
        mesh=mesh,
        in_specs=(
            P("chan", ("tmpl", "tm")),
            P("chan"),
            P("tmpl", "chan", None),
            P("tmpl"),
            P(),
            P(),
            P(),
            P(),
            P(),
            P(),
            P(),
            P(),
        ),
        out_specs=(P("chan", ("tmpl", "tm")), P("tmpl", None, "tm", "chan")),
        check_vma=False,
    )
```

profile of v0, /device:TPU:0, one launch (start us, length us, event | category | flops | bytes accessed | tf_op | source)
XLA Modules:
  0.0 46.2 jit_solution(10757380070291699924)
XLA Ops:
  0.7 0.7 %convert_element_type.27 = bf16[64]{0:T(256)(128)(2,1)S(1)} convert(s32[64]{0:T(128)} %param.15) | non-fusion elementwise | flops 64 | bytes 384 | tf_op jit(solution)/shard_map/convert_element_type | solution.py:310
  1.5 0.8 %broadcast_select_fusion = (bf16[8,512]{1,0:T(8,128)(2,1)S(1)}, bf16[8,512]{1,0:T(8,128)(2,1)S(1)}) fusion(pred[]{:T(512)S(6)} %eq.5, bf16[64,512]{1,0:T(8,128)(2,1)} %raw_ref.1, bf16[8]{0:T(256)(128)(2,1)S(1)} %get-tuple-element.45, bf16[8]{0:T(256)(128)(2,1)S(1)} %get-tuple-element.44), kind=kLoop, calls=%fused_computation.5 | loop fusion | flops 16384 | bytes 32801 | tf_op jit(solution)/shard_map/jit(_where)/select_n | solution.py:315
  2.9 4.4 %collective-permute-start = (bf16[8,512]{1,0:T(8,128)(2,1)S(1)}, bf16[8,512]{1,0:T(8,128)(2,1)S(1)}, u32[]{:S(2)}, u32[]{:S(2)}) collective-permute-start(bf16[8,512]{1,0:T(8,128)(2,1)S(1)} %get-tuple-element.43), channel_id=1, source_target_pairs={{0,2},{2,0},{4,6},{6,4},{1,3},{3,1},{5,7},{7,5},{8,10},{10,8},{12,... | collective-permute-start | bytes 24584 | tf_op jit(solution)/shard_map/ppermute | solution.py:313
  7.3 0.8 %slice_bitcast_fusion = bf16[16,3,3,32]{3,0,2,1:T(8,128)(2,1)S(1)} fusion(bf16[16,48,3,3]{1,0,3,2:T(8,128)(2,1)} %param.22), kind=kLoop, calls=%fused_computation | loop fusion | bytes 18432 | tf_op jit(solution)/shard_map/transpose | solution.py:336
  8.1 0.8 %slice_bitcast_fusion.1 = bf16[16,3,3,16]{3,0,2,1:T(8,128)(2,1)S(1)} fusion(bf16[16,48,3,3]{1,0,3,2:T(8,128)(2,1)} %param.22), kind=kLoop, calls=%fused_computation.1 | loop fusion | bytes 9216 | tf_op jit(solution)/shard_map/transpose | solution.py:335
  9.6 0.7 %reshape.23 = bf16[16,9]{0,1:T(8,128)(2,1)S(1)} reshape(bf16[16,1,3,3]{0,3,2,1:T(4,128)(2,1)} %param.18) | data formatting | bytes 576 | tf_op jit(solution)/shard_map/reshape | solution.py:333
  10.4 0.8 %copy.24.wm_ref = bf16[32,144]{1,0:T(8,128)(2,1)S(1)} copy(bf16[32,144]{0,1:T(8,128)(2,1)} %bitcast.22) | data formatting | bytes 18432 | tf_op jit(solution)/shard_map/reshape | solution.py:334
  11.5 0.7 %copy-done.5 = f32[16]{0:T(128)S(1)} copy-done((f32[16]{0:T(128)S(1)}, f32[16]{0:T(128)}, u32[]{:S(2)}) %copy-start.5) | copy-done | bytes 88
  12.2 0.7 %copy-done.6 = f32[32]{0:T(128)S(1)} copy-done((f32[32]{0:T(128)S(1)}, f32[32]{0:T(128)}, u32[]{:S(2)}) %copy-start.6) | copy-done | bytes 152
  14.1 1.1 %prep.1 = (bf16[512,96]{1,0:T(8,128)(2,1)S(1)}, bf16[224,432]{1,0:T(8,128)(2,1)S(1)}, bf16[256,1216]{1,0:T(8,128)(2,1)S(1)}, bf16[16,256]{1,0:T(8,128)(2,1)S(1)}...) custom-call(bf16[16,9]{1,0:T(8,128)(2,1)S(1)} %copy.23.we_ref, ...), custom_call_target="tpu_custom_call" | custom-call | tf_op jit(solution)/shard_map/prep/pallas_call | solution.py:318
  15.2 0.8 %copy-done.4 = bf16[64,512]{1,0:T(8,128)(2,1)S(1)} copy-done((bf16[64,512]{1,0:T(8,128)(2,1)S(1)}, bf16[64,512]{1,0:T(8,128)(2,1)}, u32[]{:S(2)}) %copy-start.4) | copy-done | bytes 65560
  16.7 6.1 %unet.1.refs_0_ = bf16[64,512]{1,0:T(8,128)(2,1)} custom-call(bf16[64,512]{1,0:T(8,128)(2,1)S(1)} %copy-done.4, s32[1,64]{1,0:T(1,128)S(1)} %bitcast.21, bf16[8,512]{1,0:T(8,128)(2,1)S(1)} %collective-permute-done.r1_ref, bf16[8,512]{1,0:T(8,128)(2,1)S(1)} %collective-permute-done.1.r2_ref, bf16[512,96]{1,0:T(8,128)(2,1)S(1)} %get-tuple-element.20.enc_ref, ...), custom_call_target="tpu_custom_call" | custom-call | tf_op jit(solution)/shard_map/unet/pallas_call | solution.py:343
  22.8 3.6 %collective-permute-start.4 = (bf16[64,512]{1,0:T(8,128)(2,1)}, bf16[64,512]{1,0:T(8,128)(2,1)S(1)}, u32[]{:S(2)}, u32[]{:S(2)}) collective-permute-start(bf16[64,512]{1,0:T(8,128)(2,1)} %unet.1.refs_0_), channel_id=1, source_target_pairs={{0,24},{8,0},{16,8},{24,16},{1,25},{9,1},{17,9},{25,17},{2,26},{10... | collective-permute-start | bytes 196616 | tf_op jit(solution)/shard_map/ppermute | solution.py:299
  26.4 1.0 %collective-permute-start.2 = (bf16[64,512]{1,0:T(8,128)(2,1)}, bf16[64,512]{1,0:T(8,128)(2,1)S(1)}, u32[]{:S(2)}, u32[]{:S(2)}) collective-permute-start(bf16[64,512]{1,0:T(8,128)(2,1)} %unet.1.refs_0_), channel_id=1, source_target_pairs={{0,8},{8,16},{16,24},{24,0},{1,9},{9,17},{17,25},{25,1},{2,10},{10... | collective-permute-start | bytes 196616 | tf_op jit(solution)/shard_map/ppermute | solution.py:299
  27.5 0.8 %tspectra.1 = (f32[4,64,512]{2,1,0:T(8,128)S(1)}, f32[4,64,512]{2,1,0:T(8,128)S(1)}, f32[4,64,128]{2,1,0:T(8,128)S(1)}) custom-call(bf16[4,64,512]{2,1,0:T(8,128)(2,1)S(1)} %copy-done.2, bf16[512,1024]{1,0:T(8,128)(2,1)S(1)} %copy-done), custom_call_target="tpu_custom_call" | custom-call | tf_op jit(solution)/shard_map/tspectra/pallas_call | solution.py:361
  28.3 0.9 %collective-permute-done.4.refs_3_ = bf16[64,512]{1,0:T(8,128)(2,1)S(1)} collective-permute-done((bf16[64,512]{1,0:T(8,128)(2,1)}, bf16[64,512]{1,0:T(8,128)(2,1)S(1)}, u32[]{:S(2)}, u32[]{:S(2)}) %collective-permute-start.4) | collective-permute-done | bytes 65568 | tf_op jit(solution)/shard_map/ppermute | solution.py:299
  29.2 4.1 %collective-permute-done.3.refs_2_ = bf16[64,512]{1,0:T(8,128)(2,1)S(1)} collective-permute-done((bf16[64,512]{1,0:T(8,128)(2,1)}, bf16[64,512]{1,0:T(8,128)(2,1)S(1)}, u32[]{:S(2)}, u32[]{:S(2)}) %collective-permute-start.3) | collective-permute-done | bytes 65568 | tf_op jit(solution)/shard_map/ppermute | solution.py:299
  34.0 2.3 %corr.1 = (bf16[16,128]{1,0:T(8,128)(2,1)S(1)}, bf16[16,128]{1,0:T(8,128)(2,1)S(1)}, bf16[16,128]{1,0:T(8,128)(2,1)S(1)}, bf16[16,128]{1,0:T(8,128)(2,1)S(1)}, b...) custom-call(bf16[64,512]{1,0:T(8,128)(2,1)S(1)} %copy-done.3, ...), custom_call_target="tpu_custom_call" | custom-call | tf_op jit(solution)/shard_map/corr/pallas_call | solution.py:370
  36.2 1.6 %collective-permute-start.5 = (bf16[16,128]{1,0:T(8,128)(2,1)S(1)}, bf16[16,128]{1,0:T(8,128)(2,1)S(1)}, u32[]{:S(2)}, u32[]{:S(2)}) collective-permute-start(bf16[16,128]{1,0:T(8,128)(2,1)S(1)} %get-tuple-element.31), channel_id=1, source_target_pairs={{0,1},{1,2},{2,3},{3,4},{4,5},{5,6},{6,7},{7,0},{8,9},{9,10},{10,1... | collective-permute-start | bytes 12296 | tf_op jit(solution)/shard_map/ppermute | solution.py:299
  38.0 1.6 %collective-permute-start.8 = (bf16[16,128]{1,0:T(8,128)(2,1)S(1)}, bf16[16,128]{1,0:T(8,128)(2,1)S(1)}, u32[]{:S(2)}, u32[]{:S(2)}) collective-permute-start(bf16[16,128]{1,0:T(8,128)(2,1)S(1)} %get-tuple-element.34), channel_id=1, source_target_pairs={{0,4},{1,5},{2,6},{3,7},{4,0},{5,1},{6,2},{7,3},{8,12},{9,13},{10,... | collective-permute-start | bytes 12296 | tf_op jit(solution)/shard_map/ppermute | solution.py:299
  39.6 1.5 %collective-permute-start.9 = (bf16[16,128]{1,0:T(8,128)(2,1)S(1)}, bf16[16,128]{1,0:T(8,128)(2,1)S(1)}, u32[]{:S(2)}, u32[]{:S(2)}) collective-permute-start(bf16[16,128]{1,0:T(8,128)(2,1)S(1)} %get-tuple-element.35), channel_id=1, source_target_pairs={{0,5},{1,6},{2,7},{3,0},{4,1},{5,2},{6,3},{7,4},{8,13},{9,14},{10,... | collective-permute-start | bytes 12296 | tf_op jit(solution)/shard_map/ppermute | solution.py:299
  41.1 0.9 %collective-permute-start.10 = (bf16[16,128]{1,0:T(8,128)(2,1)S(1)}, bf16[16,128]{1,0:T(8,128)(2,1)S(1)}, u32[]{:S(2)}, u32[]{:S(2)}) collective-permute-start(bf16[16,128]{1,0:T(8,128)(2,1)S(1)} %get-tuple-element.36), channel_id=1, source_target_pairs={{0,6},{1,7},{2,0},{3,1},{4,2},{5,3},{6,4},{7,5},{8,14},{9,15},{10,... | collective-permute-start | bytes 12296 | tf_op jit(solution)/shard_map/ppermute | solution.py:299
  42.6 0.7 %collective-permute-done.10 = bf16[16,128]{1,0:T(8,128)(2,1)S(1)} collective-permute-done((bf16[16,128]{1,0:T(8,128)(2,1)S(1)}, bf16[16,128]{1,0:T(8,128)(2,1)S(1)}, u32[]{:S(2)}, u32[]{:S(2)}) %collective-permute-start.10) | collective-permute-done | bytes 4128 | tf_op jit(solution)/shard_map/ppermute | solution.py:299
  43.3 2.3 %collective-permute-done.11 = bf16[16,128]{1,0:T(8,128)(2,1)S(1)} collective-permute-done((bf16[16,128]{1,0:T(8,128)(2,1)S(1)}, bf16[16,128]{1,0:T(8,128)(2,1)S(1)}, u32[]{:S(2)}, u32[]{:S(2)}) %collective-permute-start.11) | collective-permute-done | bytes 4128 | tf_op jit(solution)/shard_map/ppermute | solution.py:299
  (39 shorter events, 5.2 us)
Async XLA Ops:
  0.6 26.8 %copy-start = (bf16[512,1024]{1,0:T(8,128)(2,1)S(1)}, bf16[512,1024]{1,0:T(8,128)(2,1)}, u32[]{:S(2)}) copy-start(bf16[512,1024]{1,0:T(8,128)(2,1)} %constant.24.clone.table_ref.refs_7_) | copy-start | bytes 3145732
  2.3 12.9 %collective-permute-start.1 = (bf16[8,512]{1,0:T(8,128)(2,1)S(1)}, bf16[8,512]{1,0:T(8,128)(2,1)S(1)}, u32[]{:S(2)}, u32[]{:S(2)}) collective-permute-start(bf16[8,512]{1,0:T(8,128)(2,1)S(1)} %get-tuple-element.42), channel_id=1, source_target_pairs={{2,4},{4,2},{3,5},{5,3},{10,12},{12,10},{11,13},{13,11},{18,20},{2... | collective-permute-start | bytes 24584 | tf_op jit(solution)/shard_map/ppermute | solution.py:315
  2.9 12.3 %collective-permute-start = (bf16[8,512]{1,0:T(8,128)(2,1)S(1)}, bf16[8,512]{1,0:T(8,128)(2,1)S(1)}, u32[]{:S(2)}, u32[]{:S(2)}) collective-permute-start(bf16[8,512]{1,0:T(8,128)(2,1)S(1)} %get-tuple-element.43), channel_id=1, source_target_pairs={{0,2},{2,0},{4,6},{6,4},{1,3},{3,1},{5,7},{7,5},{8,10},{10,8},{12,... | collective-permute-start | bytes 24584 | tf_op jit(solution)/shard_map/ppermute | solution.py:313
  11.5 0.7 %copy-start.5 = (f32[16]{0:T(128)S(1)}, f32[16]{0:T(128)}, u32[]{:S(2)}) copy-start(f32[16]{0:T(128)} %param.19) | copy-start | bytes 196
  12.2 0.7 %copy-start.6 = (f32[32]{0:T(128)S(1)}, f32[32]{0:T(128)}, u32[]{:S(2)}) copy-start(f32[32]{0:T(128)} %param.21) | copy-start | bytes 388
  12.8 0.7 %copy-start.7 = (f32[16]{0:T(128)S(1)}, f32[16]{0:T(128)}, u32[]{:S(2)}) copy-start(f32[16]{0:T(128)} %param.23) | copy-start | bytes 196
  13.5 0.7 %copy-start.8 = (bf16[16]{0:T(256)(128)(2,1)S(1)}, bf16[16]{0:T(256)(128)(2,1)}, u32[]{:S(2)}) copy-start(bf16[16]{0:T(256)(128)(2,1)} %param.24) | copy-start | bytes 100
  14.1 13.3 %copy-start.2 = (bf16[4,64,512]{2,1,0:T(8,128)(2,1)S(1)}, bf16[4,64,512]{2,1,0:T(8,128)(2,1)}, u32[]{:S(2)}) copy-start(bf16[4,64,512]{2,1,0:T(8,128)(2,1)} %t_ref.1) | copy-start | bytes 786436
  15.2 0.8 %copy-start.4 = (bf16[64,512]{1,0:T(8,128)(2,1)S(1)}, bf16[64,512]{1,0:T(8,128)(2,1)}, u32[]{:S(2)}) copy-start(bf16[64,512]{1,0:T(8,128)(2,1)} %raw_ref.1) | copy-start | bytes 196612
  16.1 0.7 %copy-start.9 = (s32[64]{0:T(128)S(1)}, s32[64]{0:T(128)}, u32[]{:S(2)}) copy-start(s32[64]{0:T(128)} %param.15) | copy-start | bytes 772
  16.7 16.6 %copy-start.1 = (bf16[1024,512]{1,0:T(8,128)(2,1)S(1)}, bf16[1024,512]{1,0:T(8,128)(2,1)}, u32[]{:S(2)}) copy-start(bf16[1024,512]{1,0:T(8,128)(2,1)} %constant.25.clone.refs_8_) | copy-start | bytes 3145732
  22.8 10.5 %copy-start.3 = (bf16[64,512]{1,0:T(8,128)(2,1)S(1)}, bf16[64,512]{1,0:T(8,128)(2,1)}, u32[]{:S(2)}) copy-start(bf16[64,512]{1,0:T(8,128)(2,1)} %unet.1.refs_0_) | copy-start | bytes 196612
  22.8 6.4 %collective-permute-start.4 = (bf16[64,512]{1,0:T(8,128)(2,1)}, bf16[64,512]{1,0:T(8,128)(2,1)S(1)}, u32[]{:S(2)}, u32[]{:S(2)}) collective-permute-start(bf16[64,512]{1,0:T(8,128)(2,1)} %unet.1.refs_0_), channel_id=1, source_target_pairs={{0,24},{8,0},{16,8},{24,16},{1,25},{9,1},{17,9},{25,17},{2,26},{10... | collective-permute-start | bytes 196616 | tf_op jit(solution)/shard_map/ppermute | solution.py:299
  26.4 6.9 %collective-permute-start.3 = (bf16[64,512]{1,0:T(8,128)(2,1)}, bf16[64,512]{1,0:T(8,128)(2,1)S(1)}, u32[]{:S(2)}, u32[]{:S(2)}) collective-permute-start(bf16[64,512]{1,0:T(8,128)(2,1)} %unet.1.refs_0_), channel_id=1, source_target_pairs={{0,16},{8,24},{16,0},{24,8},{1,17},{9,25},{17,1},{25,9},{2,18},{10... | collective-permute-start | bytes 196616 | tf_op jit(solution)/shard_map/ppermute | solution.py:299
  26.4 6.9 %collective-permute-start.2 = (bf16[64,512]{1,0:T(8,128)(2,1)}, bf16[64,512]{1,0:T(8,128)(2,1)S(1)}, u32[]{:S(2)}, u32[]{:S(2)}) collective-permute-start(bf16[64,512]{1,0:T(8,128)(2,1)} %unet.1.refs_0_), channel_id=1, source_target_pairs={{0,8},{8,16},{16,24},{24,0},{1,9},{9,17},{17,25},{25,1},{2,10},{10... | collective-permute-start | bytes 196616 | tf_op jit(solution)/shard_map/ppermute | solution.py:299
  33.3 0.7 %copy-start.10 = (s32[4]{0:T(128)S(1)}, s32[4]{0:T(128)}, u32[]{:S(2)}) copy-start(s32[4]{0:T(128)} %refs_9_.1) | copy-start | bytes 52
  36.2 4.9 %collective-permute-start.5 = (bf16[16,128]{1,0:T(8,128)(2,1)S(1)}, bf16[16,128]{1,0:T(8,128)(2,1)S(1)}, u32[]{:S(2)}, u32[]{:S(2)}) collective-permute-start(bf16[16,128]{1,0:T(8,128)(2,1)S(1)} %get-tuple-element.31), channel_id=1, source_target_pairs={{0,1},{1,2},{2,3},{3,4},{4,5},{5,6},{6,7},{7,0},{8,9},{9,10},{10,1... | collective-permute-start | bytes 12296 | tf_op jit(solution)/shard_map/ppermute | solution.py:299
  37.8 4.2 %collective-permute-start.6 = (bf16[16,128]{1,0:T(8,128)(2,1)S(1)}, bf16[16,128]{1,0:T(8,128)(2,1)S(1)}, u32[]{:S(2)}, u32[]{:S(2)}) collective-permute-start(bf16[16,128]{1,0:T(8,128)(2,1)S(1)} %get-tuple-element.32), channel_id=1, source_target_pairs={{0,2},{1,3},{2,4},{3,5},{4,6},{5,7},{6,0},{7,1},{8,10},{9,11},{10,... | collective-permute-start | bytes 12296 | tf_op jit(solution)/shard_map/ppermute | solution.py:299
  37.8 4.5 %collective-permute-start.7 = (bf16[16,128]{1,0:T(8,128)(2,1)S(1)}, bf16[16,128]{1,0:T(8,128)(2,1)S(1)}, u32[]{:S(2)}, u32[]{:S(2)}) collective-permute-start(bf16[16,128]{1,0:T(8,128)(2,1)S(1)} %get-tuple-element.33), channel_id=1, source_target_pairs={{0,3},{1,4},{2,5},{3,6},{4,7},{5,0},{6,1},{7,2},{8,11},{9,12},{10,... | collective-permute-start | bytes 12296 | tf_op jit(solution)/shard_map/ppermute | solution.py:299
  38.0 4.3 %collective-permute-start.8 = (bf16[16,128]{1,0:T(8,128)(2,1)S(1)}, bf16[16,128]{1,0:T(8,128)(2,1)S(1)}, u32[]{:S(2)}, u32[]{:S(2)}) collective-permute-start(bf16[16,128]{1,0:T(8,128)(2,1)S(1)} %get-tuple-element.34), channel_id=1, source_target_pairs={{0,4},{1,5},{2,6},{3,7},{4,0},{5,1},{6,2},{7,3},{8,12},{9,13},{10,... | collective-permute-start | bytes 12296 | tf_op jit(solution)/shard_map/ppermute | solution.py:299
  39.6 3.0 %collective-permute-start.9 = (bf16[16,128]{1,0:T(8,128)(2,1)S(1)}, bf16[16,128]{1,0:T(8,128)(2,1)S(1)}, u32[]{:S(2)}, u32[]{:S(2)}) collective-permute-start(bf16[16,128]{1,0:T(8,128)(2,1)S(1)} %get-tuple-element.35), channel_id=1, source_target_pairs={{0,5},{1,6},{2,7},{3,0},{4,1},{5,2},{6,3},{7,4},{8,13},{9,14},{10,... | collective-permute-start | bytes 12296 | tf_op jit(solution)/shard_map/ppermute | solution.py:299
  41.1 2.2 %collective-permute-start.10 = (bf16[16,128]{1,0:T(8,128)(2,1)S(1)}, bf16[16,128]{1,0:T(8,128)(2,1)S(1)}, u32[]{:S(2)}, u32[]{:S(2)}) collective-permute-start(bf16[16,128]{1,0:T(8,128)(2,1)S(1)} %get-tuple-element.36), channel_id=1, source_target_pairs={{0,6},{1,7},{2,0},{3,1},{4,2},{5,3},{6,4},{7,5},{8,14},{9,15},{10,... | collective-permute-start | bytes 12296 | tf_op jit(solution)/shard_map/ppermute | solution.py:299
  42.0 3.6 %collective-permute-start.11 = (bf16[16,128]{1,0:T(8,128)(2,1)S(1)}, bf16[16,128]{1,0:T(8,128)(2,1)S(1)}, u32[]{:S(2)}, u32[]{:S(2)}) collective-permute-start(bf16[16,128]{1,0:T(8,128)(2,1)S(1)} %get-tuple-element.37), channel_id=1, source_target_pairs={{0,7},{1,0},{2,1},{3,2},{4,3},{5,4},{6,5},{7,6},{8,15},{9,8},{10,9... | collective-permute-start | bytes 12296 | tf_op jit(solution)/shard_map/ppermute | solution.py:299
where the time goes:
time: 46.7 us; the launch traced here: 46.2 us
  starting transfers between devices  15.7 us (34%)
  Pallas kernels  10.3 us (22%)
  local copies, waits for them, and re-layouts  8.34 us (18%)
  waiting for transfers between devices  8.32 us (18%)
  other arithmetic  2.14 us (5%)
  between operations  1.41 us (3%)
    ppermute x10, starting transfers between devices, rotated(): return lax.ppermute(x, axes, [(i, (i + by) % count) for i in range(count)])  10.7 us
    ppermute x10, waiting for transfers between devices, rotated(): return lax.ppermute(x, axes, [(i, (i + by) % count) for i in range(count)])  8.31 us
    pallas_call x1, Pallas kernels, body(): call(unet_kernel, [((rows, length), BF)], [pltpu.VMEM((6, rows + 2 * EDGE...  6.11 us
    unnamed x22, local copies, waits for them, and re-layouts  4.77 us
    ppermute x1, starting transfers between devices, body(): lax.ppermute(jnp.where(odd, head, tail), 'chan', [(i, i ^ 1) for i in ran...  4.42 us
    pallas_call x1, Pallas kernels, body(): call(functools.partial(corr_kernel, blocks), [((pairs, width), BF)] * (2...  2.26 us
    pallas_call x1, Pallas kernels, body(): call(prep_kernel, [((ENC_ROWS * 4 * maps, 6 * (ENC_ROWS + EDGE)), BF), ((...  1.05 us
  transfers between devices with their start and end apart: 12, of which 5 were waited for; matrix products, arithmetic and copies ran while one was open for 8% of the time, Pallas kernels for 4%

commit v1 on v0

--- a/solution.py
+++ b/solution.py
@@ -52,16 +52,39 @@
     return jnp.sum(jnp.where(pick, row, 0.0), axis=1, keepdims=True)
 
 
+def load_kernel(*refs):
+    count = (len(refs) - 3) // 2
+    sources = refs[:count]
+    copies = refs[count : 2 * count]
+    first_ref, second_ref, sems = refs[2 * count :]
+    moves = [pltpu.make_async_copy(src, dst, sems.at[i]) for i, (src, dst) in enumerate(zip(sources, copies))]
+    for move in moves:
+        move.start()
+    moves[0].wait()
+    moves[1].wait()
+    raw_ref, mask_ref = copies[:2]
+    rows = raw_ref.shape[0]
+    alive = column(mask_ref[...].astype(F32), rows)
+    head = raw_ref[:EDGE].astype(F32) * alive[:EDGE]
+    tail = raw_ref[rows - EDGE :].astype(F32) * alive[rows - EDGE :]
+    odd = lax.axis_index("chan") % 2 == 1
+    first_ref[...] = jnp.where(odd, head, tail).astype(BF)
+    second_ref[...] = jnp.where(odd, tail, head).astype(BF)
+    for move in moves[2:]:
+        move.wait()
+
+
 def prep_kernel(
-    we_ref, wm_ref, ws_ref, wu_ref, be_ref, bm_ref, bd_ref, wo_ref,
+    we_ref, wm_ref, wd_ref, be_ref, bm_ref, bd_ref, wo_ref,
     enc_ref, mid_ref, dec_ref, out_ref, benc_ref, bmid_ref, bdec_ref, wide_ref,
 ):
-    maps = we_ref.shape[0]
+    maps = we_ref.shape[3]
     half = benc_ref.shape[1]
     rows, cols = enc_ref.shape
     window = ENC_ROWS + EDGE
     spread = jnp.where(iota((rows, maps), 0) % maps == iota((rows, maps), 1), 1.0, 0.0).astype(BF)
-    taps = dot(spread, we_ref[...])
+    we = jnp.concatenate([we_ref[0, y].astype(F32) for y in range(3)], axis=0).astype(BF)
+    taps = lax.dot_general(spread, we, (((1,), (1,)), ((), ())), preferred_element_type=F32)
     row_id = iota((rows, cols), 0)
     col_id = iota((rows, cols), 1)
     dy = col_id % window - row_id // (4 * maps) - (EDGE // 2 - 1)
@@ -72,28 +95,31 @@
         acc = jnp.where(tap == t, taps[:, t : t + 1], acc)
     enc_ref[...] = acc.astype(BF)
     wide_ref[...] = jnp.zeros(wide_ref.shape, F32)
-    wm = wm_ref[...].astype(F32)
+    wm = wm_ref[...].astype(F32).reshape(9 * maps, 2 * maps).T
     for r in range(MID_ROWS):
         wide_ref[r * 2 * maps : (r + 1) * 2 * maps, r * 3 * maps : r * 3 * maps + 9 * maps] = wm
     mid_ref[...] = wide_ref[: mid_ref.shape[0], : mid_ref.shape[1]].astype(BF)
     wide_ref[...] = jnp.zeros(wide_ref.shape, F32)
-    ws = ws_ref[...].astype(F32)
-    wu = wu_ref[...].astype(F32)
     skip_cols = (DEC_ROWS + 2) * 4 * maps
-    k = [[wu[:, (y * 3 + x) * 2 * maps : (y * 3 + x + 1) * 2 * maps] for x in range(3)] for y in range(3)]
+    k = [[wd_ref[y, x].astype(F32) for x in range(3)] for y in range(3)]
+    ws = [jnp.concatenate([k[y][x][:, 2 * maps :] for x in range(3)], axis=1) for y in range(3)]
+    split = ((0,), (1, 2)), ((0, 1), (2,))
+    wu = {}
+    for r in range(2):
+        for q in range(2):
+            for a in range(2):
+                wu[r, q, a] = jnp.concatenate(
+                    [sum(k[y][x][:, : 2 * maps] for y in split[r][a] for x in split[q][b]) for b in range(2)], axis=1
+                )
     for r in range(DEC_ROWS):
-        ys = ((0,), (1, 2)) if r % 2 == 0 else ((0, 1), (2,))
         for q in range(2):
             top = (r * 2 + q) * maps
             for y in range(3):
                 left = ((r + y) * 4 + q) * maps
-                wide_ref[top : top + maps, left : left + 3 * maps] = ws[:, y * 3 * maps : (y + 1) * 3 * maps]
-            xs = ((0,), (1, 2)) if q == 0 else ((0, 1), (2,))
+                wide_ref[top : top + maps, left : left + 3 * maps] = ws[y]
             for a in range(2):
-                for b in range(2):
-                    value = sum(k[y][x] for y in ys[a] for x in xs[b])
-                    left = skip_cols + ((r + 1) // 2 + a) * 6 * maps + (q + b) * 2 * maps
-                    wide_ref[top : top + maps, left : left + 2 * maps] = value
+                left = skip_cols + ((r + 1) // 2 + a) * 6 * maps + q * 2 * maps
+                wide_ref[top : top + maps, left : left + 4 * maps] = wu[r % 2, q, a]
     dec_ref[...] = wide_ref[...].astype(BF)
     n = out_ref.shape[1]
     repeat = jnp.where(iota((maps, n), 1) % maps == iota((maps, n), 0), 1.0, 0.0).astype(BF)
@@ -205,50 +231,70 @@
     ).astype(BF)
 
 
-def template_kernel(t_ref, table_ref, a_ref, b_ref, first_ref):
-    count, rows, length = t_ref.shape
-    for k in range(count):
-        y = dot(t_ref[k], table_ref[...]).astype(BF).astype(F32)
-        a = y[:, :length]
-        b = y[:, length:]
-        lane = iota(a.shape, 1)
-        a_ref[k] = a
-        b_ref[k] = jnp.where(lane == 0, 0.0, b)
-        first_ref[k] = jnp.where(lane == 0, b, a)[:, :128]
-
-
-def corr_kernel(count, *refs):
-    x_refs = refs[:count]
-    ta_ref, tb_ref, tf_ref, table_ref, inverse_ref, assign_ref = refs[count : count + 6]
-    outs = refs[count + 6 : -3]
-    sa_ref, p_ref, share_ref = refs[-3:]
-    rows, length = x_refs[0].shape
-    tmpl = ta_ref.shape[0]
-    here = lax.axis_index("tmpl")
-    for k in range(count):
-        sa_ref[(here - k) % count] = dot(x_refs[k][...], table_ref[...]).astype(BF).astype(F32)
-    picks = [assign_ref[r] % tmpl for r in range(tmpl)]
+def products(spectra, ta_ref, tb_ref, tf_ref, put):
+    tmpl, rows, length = ta_ref.shape
+    count = len(spectra)
     for lane in range(0, length, 128):
-        real = [[None] * count for _ in range(tmpl)]
-        imag = [[None] * count for _ in range(tmpl)]
+        real = {}
+        imag = {}
         for c in range(0, rows, 8):
-            at = [ta_ref[picks[r], c : c + 8, lane : lane + 128] for r in range(tmpl)]
-            bt = [tb_ref[picks[r], c : c + 8, lane : lane + 128] for r in range(tmpl)]
-            af = at if lane else [tf_ref[picks[r], c : c + 8, :] for r in range(tmpl)]
+            at = [ta_ref[r, c : c + 8, lane : lane + 128] for r in range(tmpl)]
+            bt = [tb_ref[r, c : c + 8, lane : lane + 128] for r in range(tmpl)]
+            af = at if lane else [tf_ref[r, c : c + 8, :] for r in range(tmpl)]
             for i in range(count):
-                ax = sa_ref[i, c : c + 8, lane : lane + 128]
-                bx = sa_ref[i, c : c + 8, length + lane : length + lane + 128]
+                ax = spectra[i][c : c + 8, lane : lane + 128]
+                bx = spectra[i][c : c + 8, length + lane : length + lane + 128]
                 for r in range(tmpl):
                     re = ax * at[r] + bx * bt[r]
                     im = bx * af[r] - ax * bt[r]
-                    real[r][i] = re if c == 0 else real[r][i] + re
-                    imag[r][i] = im if c == 0 else imag[r][i] + im
+                    real[r, i] = re if c == 0 else real[r, i] + re
+                    imag[r, i] = im if c == 0 else imag[r, i] + im
         for r in range(tmpl):
             for i in range(count):
-                row = r * count + i
-                p_ref[row : row + 1, lane : lane + 128] = jnp.sum(real[r][i], axis=0, keepdims=True)
-                p_ref[row : row + 1, length + lane : length + lane + 128] = jnp.sum(imag[r][i], axis=0, keepdims=True)
-    p = p_ref[...]
+                put(r, i, lane, jnp.sum(real[r, i], axis=0, keepdims=True))
+                put(r, i, length + lane, jnp.sum(imag[r, i], axis=0, keepdims=True))
+
+
+def own_kernel(x_ref, t_ref, table_ref, assign_ref, a_ref, b_ref, first_ref, p_ref, order_ref, s_ref, sem):
+    fetch = pltpu.make_async_copy(assign_ref, order_ref, sem)
+    fetch.start()
+    tmpl, rows, length = t_ref.shape
+    s_ref[...] = dot(x_ref[...], table_ref[...])
+    fetch.wait()
+    for r in range(tmpl):
+        y = dot(t_ref[order_ref[r] % tmpl], table_ref[...])
+        a = y[:, :length]
+        b = y[:, length:]
+        lane = iota((rows, 128), 1)
+        a_ref[r] = a
+        b_ref[r] = b
+        b_ref[r, :, :128] = jnp.where(lane == 0, 0.0, b[:, :128])
+        first_ref[r] = jnp.where(lane == 0, b[:, :128], a[:, :128])
+
+    def put(r, i, lane, row):
+        p_ref[r : r + 1, lane : lane + 128] = row
+
+    products([s_ref], a_ref, b_ref, first_ref, put)
+
+
+def corr_kernel(others, *refs):
+    x_refs = refs[: others + 1]
+    ta_ref, tb_ref, tf_ref, own_ref, table_ref, inverse_ref = refs[others + 1 : others + 7]
+    copy_ref, keep_ref, send_ref, s_ref, p_ref, share_ref, sem = refs[others + 7 :]
+    store = pltpu.make_async_copy(x_refs[0], copy_ref, sem)
+    store.start()
+    count = others + 1
+    tmpl, rows, length = ta_ref.shape
+    here = lax.axis_index("tmpl")
+    p_ref[here] = own_ref[...]
+    if others:
+        s_ref[...] = dot(jnp.concatenate([x_ref[...] for x_ref in x_refs[1:]], axis=0), table_ref[...])
+
+    def put(r, i, lane, row):
+        p_ref[(here + others - i) % count, r : r + 1, lane : lane + 128] = row
+
+    products([s_ref.at[i * rows : (i + 1) * rows] for i in range(others)], ta_ref, tb_ref, tf_ref, put)
+    p = jnp.concatenate([p_ref[i, r : r + 1, :] for r in range(tmpl) for i in range(count)], axis=0)
     high = p.astype(BF)
     low = (p - high.astype(F32)).astype(BF)
     pairs = tmpl * count
@@ -275,23 +321,40 @@
         share_ref[0, c] = near[:, c * width : (c + 1) * width]
         share_ref[1, c] = far[:, c * width : (c + 1) * width]
     chan = lax.axis_index("chan")
+    mine = chan // 2 * 2 + parity
+    for k in range(chans):
+        to = mine ^ k
+        kind = (to + parity) % 2
+        keep_ref[k] = share_ref[kind, to // 2 * 2 + chan % 2]
+        send_ref[k] = share_ref[kind, to // 2 * 2 + 1 - chan % 2].astype(BF)
+    store.wait()
+
+
+def fold_kernel(keep_ref, got_ref, own_ref, *outs):
+    own_ref[...] = keep_ref[0] + got_ref[0].astype(F32)
     for k, out in enumerate(outs):
-        to = (chan * 2 + parity + k) % (2 * chans)
-        out[...] = share_ref[(to + parity) % 2, to // 2].astype(BF)
-
-
-def call(kernel, outs, scratch=(), smem=(), inputs=0, name=None):
-    return pl.pallas_call(
+        out[...] = (keep_ref[k + 1] + got_ref[k + 1].astype(F32)).astype(BF)
+
+
+VMEM = pltpu.MemorySpace.VMEM
+HBM = pltpu.MemorySpace.HBM
+SMEM = pltpu.MemorySpace.SMEM
+
+
+def call(kernel, outs, scratch=(), hbm=(), smem=(), hbm_out=(), inputs=0, name=None):
+    def run(*args):
+        return inner(*[pltpu.with_memory_space_constraint(x, HBM) if i in hbm else x for i, x in enumerate(args)])
+
+    inner = pl.pallas_call(
         kernel,
         out_shape=tuple(jax.ShapeDtypeStruct(s, d) for s, d in outs),
-        in_specs=[
-            pl.BlockSpec(memory_space=pltpu.SMEM if i in smem else pltpu.VMEM) for i in range(inputs)
-        ],
-        out_specs=tuple(pl.BlockSpec(memory_space=pltpu.VMEM) for _ in outs),
+        in_specs=[pl.BlockSpec(memory_space=HBM if i in hbm else SMEM if i in smem else VMEM) for i in range(inputs)],
+        out_specs=tuple(pl.BlockSpec(memory_space=HBM if i in hbm_out else VMEM) for i in range(len(outs))),
         scratch_shapes=scratch,
         name=name,
         compiler_params=pltpu.CompilerParams(vmem_limit_bytes=48 * 1024 * 1024),
     )
+    return run
 
 
 def rotated(x, axes, by):
@@ -306,13 +369,28 @@
     chans = lax.axis_size("chan")
     blocks = lax.axis_size("tmpl")
     tmpl = templates.shape[0]
-    odd = lax.axis_index("chan") % 2 == 1
-    alive = dead_mask.astype(BF)[:, None]
-    head = raw[:EDGE] * alive[:EDGE]
-    tail = raw[-EDGE:] * alive[-EDGE:]
-    r1 = lax.ppermute(jnp.where(odd, head, tail), "chan", [(i, i ^ 1) for i in range(chans) if i ^ 1 < chans])
+    small = [
+        raw,
+        dead_mask[None],
+        w_enc.transpose(1, 2, 3, 0),
+        w_mid.transpose(2, 3, 1, 0),
+        w_dec.transpose(2, 3, 0, 1),
+        b_enc[None],
+        b_mid[None],
+        b_dec[None],
+        w_out[None],
+    ]
+    *loaded, first, second = call(
+        load_kernel,
+        [(x.shape, x.dtype) for x in small] + [((EDGE, length), BF)] * 2,
+        [pltpu.SemaphoreType.DMA((len(small),))],
+        hbm=range(len(small)),
+        inputs=len(small),
+        name="load",
+    )(*small)
+    r1 = lax.ppermute(first, "chan", [(i, i ^ 1) for i in range(chans) if i ^ 1 < chans])
     links = [(i, i + 1) for i in range(1, chans - 1, 2)]
-    r2 = lax.ppermute(jnp.where(odd, tail, head), "chan", links + [(b, a) for a, b in links])
+    r2 = lax.ppermute(second, "chan", links + [(b, a) for a, b in links])
 
     dec_cols = (DEC_ROWS + 2) * 4 * maps + (DEC_ROWS // 2 + 2) * 6 * maps
     weights = call(
@@ -327,18 +405,9 @@
             ((2 * maps, half), F32),
         ],
         [pltpu.VMEM((DEC_ROWS * 2 * maps, dec_cols), F32)],
-        inputs=8,
+        inputs=7,
         name="prep",
-    )(
-        w_enc.reshape(maps, 9),
-        w_mid.transpose(0, 2, 3, 1).reshape(2 * maps, 9 * maps),
-        w_dec[:, 2 * maps :].transpose(0, 2, 3, 1).reshape(maps, 9 * maps),
-        w_dec[:, : 2 * maps].transpose(0, 2, 3, 1).reshape(maps, 18 * maps),
-        b_enc[None],
-        b_mid[None],
-        b_dec[None],
-        w_out[None],
-    )
+    )(*loaded[2:9])
     mid_groups = -(-(rows // 2 + 2) // MID_ROWS)
     (denoised,) = call(
         unet_kernel,
@@ -354,35 +423,42 @@
         smem=(11,),
         inputs=12,
         name="unet",
-    )(raw, dead_mask[None], r1, r2, *weights, b_out)
+    )(*loaded[:2], r1, r2, *weights, b_out)
 
     forward = jnp.asarray(forward_table(length))
     inverse = jnp.asarray(inverse_table(length))
-    spectra_t = call(
-        template_kernel,
-        [((tmpl, rows, length), F32), ((tmpl, rows, length), F32), ((tmpl, rows, 128), F32)],
-        inputs=2,
-        name="tspectra",
-    )(templates, forward)
-    gathered = [denoised] + [rotated(denoised, "tmpl", k) for k in range(1, blocks)]
+    gathered = [rotated(denoised, "tmpl", k) for k in range(1, blocks)]
+    spectra = call(
+        own_kernel,
+        [((tmpl, rows, length), F32), ((tmpl, rows, length), F32), ((tmpl, rows, 128), F32), ((tmpl, 2 * length), F32)],
+        [pltpu.SMEM((tmpl,), jnp.int32), pltpu.VMEM((rows, 2 * length), F32), pltpu.SemaphoreType.DMA],
+        hbm=(3,),
+        inputs=4,
+        name="own",
+    )(denoised, templates, forward, assign)
     width = length // chans
     pairs = tmpl * blocks
-    sent = call(
-        functools.partial(corr_kernel, blocks),
-        [((pairs, width), BF)] * (2 * chans),
+    copied, keep, send = call(
+        functools.partial(corr_kernel, blocks - 1),
+        [((rows, length), BF), ((chans, pairs, width), F32), ((chans, pairs, width), BF)],
         [
-            pltpu.VMEM((blocks, rows, 2 * length), F32),
-            pltpu.VMEM((pairs, 2 * length), F32),
+            pltpu.VMEM(((blocks - 1) * rows, 2 * length), F32),
+            pltpu.VMEM((blocks, tmpl, 2 * length), F32),
             pltpu.VMEM((2, chans, pairs, width), F32),
+            pltpu.SemaphoreType.DMA,
         ],
-        smem=(blocks + 5,),
+        hbm_out=(0,),
         inputs=blocks + 6,
         name="corr",
-    )(*gathered, *spectra_t, forward, inverse, assign)
-    total = sent[0].astype(F32)
-    for k in range(1, 2 * chans):
-        total = total + rotated(sent[k], ("chan", "tm"), k).astype(F32)
-    return denoised, total.reshape(tmpl, blocks, 1, width)
+    )(denoised, *gathered, *spectra, forward, inverse)
+    got = lax.ppermute(send, "chan", [(i, i ^ 1) for i in range(chans)])
+    total, *parts = call(
+        fold_kernel, [((pairs, width), F32)] + [((pairs, width), BF)] * (chans - 1), inputs=2, name="fold"
+    )(keep, got)
+    for k, part in enumerate(parts, 1):
+        step = k // 2 * 4 + k % 2
+        total = total + lax.ppermute(part, ("chan", "tm"), [(i, i ^ step) for i in range(2 * chans)]).astype(F32)
+    return copied, total.reshape(tmpl, blocks, 1, width)
 
 
 def solution(mesh):

time: 46.7 us -> 34.5 us (0.74)
  local copies, waits for them, and re-layouts: 8.34 us -> 0.02 us
  starting transfers between devices: 15.7 us -> 12.2 us
  other arithmetic: 2.14 us -> 0.6 us
  waiting for transfers between devices: 8.32 us -> 9.51 us
    ppermute x2 -> x6, waiting for transfers between devices: 0.01 us -> 5.35 us  [the longest x3 4.5 us: body(): lax.ppermute(part, ('chan', 'tm'), [(i, i ^ step) for i in range(2 * chan...]
    ppermute x10 -> x3, starting transfers between devices: 10.7 us -> 5.68 us  [rotated(): return lax.ppermute(x, axes, [(i, (i + by) % count) for i in range(count)])]
    unnamed x22 -> x6, local copies, waits for them, and re-layouts: 4.77 us -> 0.02 us
    ppermute x10 -> x3, waiting for transfers between devices: 8.31 us -> 4.17 us  [rotated(): return lax.ppermute(x, axes, [(i, (i + by) % count) for i in range(count)])]
    reshape x5 -> x0, local copies, waits for them, and re-layouts: 1.82 us -> none  [the longest x1 0.83 us: body(): w_mid.transpose(0, 2, 3, 1).reshape(2 * maps, 9 * maps)]
    transpose x4 -> x0, local copies, waits for them, and re-layouts: 1.67 us -> none  [the longest x2 0.87 us: body(): w_dec[:, 2 * maps:].transpose(0, 2, 3, 1).reshape(maps, 9 * maps)]
    ppermute x2 -> x6, starting transfers between devices: 5.07 us -> 6.48 us  [the longest x3 4.23 us: body(): lax.ppermute(part, ('chan', 'tm'), [(i, i ^ step) for i in range(2 * chan...]
    select_n x1 -> x0, other arithmetic: 0.79 us -> none  [body(): jnp.where(odd, tail, head)]
  transfers between devices with their start and end apart: 12 -> 9, of which waited for: 5 -> 4; matrix products, arithmetic and copies ran while one was open for 8% -> 0% of each run, Pallas kernels for 4% -> 8%
where the time goes in v1:
time: 34.5 us; the launch traced here: 34.3 us
  starting transfers between devices  12.2 us (35%)
  Pallas kernels  10.6 us (31%)
  waiting for transfers between devices  9.51 us (28%)
  between operations  1.38 us (4%)
  other arithmetic  0.6 us (2%)
    pallas_call x6, Pallas kernels, run(): inner(*[pltpu.with_memory_space_constraint(x, HBM) if i in hbm else x for...  10.6 us
    ppermute x3, starting transfers between devices, rotated(): return lax.ppermute(x, axes, [(i, (i + by) % count) for i in range(count)])  5.68 us
    ppermute x3, waiting for transfers between devices, body(): lax.ppermute(part, ('chan', 'tm'), [(i, i ^ step) for i in range(2 * chan...  4.5 us
    ppermute x3, starting transfers between devices, body(): lax.ppermute(part, ('chan', 'tm'), [(i, i ^ step) for i in range(2 * chan...  4.23 us
    ppermute x3, waiting for transfers between devices, rotated(): return lax.ppermute(x, axes, [(i, (i + by) % count) for i in range(count)])  4.17 us
    ppermute x1, starting transfers between devices, body(): got = lax.ppermute(send, 'chan', [(i, i ^ 1) for i in range(chans)])  1.04 us
    ppermute x1, waiting for transfers between devices, body(): got = lax.ppermute(send, 'chan', [(i, i ^ 1) for i in range(chans)])  0.84 us
  transfers between devices with their start and end apart: 9, of which 4 were waited for; matrix products, arithmetic and copies ran while one was open for 0% of the time, Pallas kernels for 8%

profile of v1, /device:TPU:0, one launch (start us, length us, event | category | flops | bytes accessed | tf_op | source)
XLA Modules:
  0.0 34.3 jit_solution(9243167238560139123)
XLA Ops:
  0.6 0.0 copy-start
  0.6 1.1 %load.1 = (bf16[64,512]{1,0:T(8,128)(2,1)S(1)}, s32[1,64]{1,0:T(1,128)S(1)}, bf16[1,3,3,16]{3,2,1,0:T(4,128)(2,1)S(1)}, bf16[3,3,16,32]{3,2,1,0:T(8,128)(2,1)S(1...) custom-call(bf16[64,512]{1,0:T(8,128)(2,1)} %refs_0_.1, ...), custom_call_target="tpu_custom_call" | custom-call | tf_op jit(solution)/shard_map/load/pallas_call | solution.py:346
  1.8 0.6 %collective-permute-start = (bf16[8,512]{1,0:T(8,128)(2,1)S(1)}, bf16[8,512]{1,0:T(8,128)(2,1)S(1)}, u32[]{:S(2)}, u32[]{:S(2)}) collective-permute-start(bf16[8,512]{1,0:T(8,128)(2,1)S(1)} %get-tuple-element.33), channel_id=1, source_target_pairs={{0,2},{2,0},{4,6},{6,4},{1,3},{3,1},{5,7},{7,5},{8,10},{10,8},{12,... | collective-permute-start | bytes 24584 | tf_op jit(solution)/shard_map/ppermute | solution.py:391
  2.3 0.6 %collective-permute-start.1 = (bf16[8,512]{1,0:T(8,128)(2,1)S(1)}, bf16[8,512]{1,0:T(8,128)(2,1)S(1)}, u32[]{:S(2)}, u32[]{:S(2)}) collective-permute-start(bf16[8,512]{1,0:T(8,128)(2,1)S(1)} %get-tuple-element.34), channel_id=1, source_target_pairs={{2,4},{4,2},{3,5},{5,3},{10,12},{12,10},{11,13},{13,11},{18,20},{2... | collective-permute-start | bytes 24584 | tf_op jit(solution)/shard_map/ppermute | solution.py:393
  3.6 1.0 %prep.1 = (bf16[512,96]{1,0:T(8,128)(2,1)S(1)}, bf16[224,432]{1,0:T(8,128)(2,1)S(1)}, bf16[256,1216]{1,0:T(8,128)(2,1)S(1)}, bf16[16,256]{1,0:T(8,128)(2,1)S(1)}...) custom-call(bf16[1,3,3,16]{3,2,1,0:T(4,128)(2,1)S(1)} %get-tuple-element.35.we_ref, ...), custom_call_target="tpu_custom_call" | custom-call | tf_op jit(solution)/shard_map/prep/pallas_call | solution.py:346
  4.6 0.0 collective-permute-done.1.r2_ref
  4.7 0.0 copy-start.2
  4.7 0.0 copy-start.1
  4.7 5.5 %unet.1.x_ref.refs_0_ = bf16[64,512]{1,0:T(8,128)(2,1)S(1)} custom-call(bf16[64,512]{1,0:T(8,128)(2,1)S(1)} %get-tuple-element.31.raw_ref, s32[1,64]{1,0:T(1,128)S(1)} %get-tuple-element.32.mask_ref, bf16[8,512]{1,0:T(8,128)(2,1)S(1)} %collective-permute-done.r1_ref, bf16[8,512]{1,0:T(8,128)(2,1)S(1)} %collective-permute-done.1.r2_ref, ...), custom_call_target="tpu_custom_call" | custom-call | tf_op jit(solution)/shard_map/unet/pallas_call | solution.py:346
  10.2 4.7 %collective-permute-start.4 = (bf16[64,512]{1,0:T(8,128)(2,1)S(1)}, bf16[64,512]{1,0:T(8,128)(2,1)S(1)}, u32[]{:S(2)}, u32[]{:S(2)}) collective-permute-start(bf16[64,512]{1,0:T(8,128)(2,1)S(1)} %unet.1.x_ref.refs_0_), channel_id=1, source_target_pairs={{0,24},{8,0},{16,8},{24,16},{1,25},{9,1},{17,9},{25,17},{2,26},{10... | collective-permute-start | bytes 196616 | tf_op jit(solution)/shard_map/ppermute | solution.py:362
  14.9 0.0 collective-permute-start.3
  14.9 1.0 %collective-permute-start.2 = (bf16[64,512]{1,0:T(8,128)(2,1)S(1)}, bf16[64,512]{1,0:T(8,128)(2,1)S(1)}, u32[]{:S(2)}, u32[]{:S(2)}) collective-permute-start(bf16[64,512]{1,0:T(8,128)(2,1)S(1)} %unet.1.x_ref.refs_0_), channel_id=1, source_target_pairs={{0,8},{8,16},{16,24},{24,0},{1,9},{9,17},{17,25},{25,1},{2,10},{10... | collective-permute-start | bytes 196616 | tf_op jit(solution)/shard_map/ppermute | solution.py:362
  15.9 1.6 %own.1 = (f32[4,64,512]{2,1,0:T(8,128)S(1)}, f32[4,64,512]{2,1,0:T(8,128)S(1)}, f32[4,64,128]{2,1,0:T(8,128)S(1)}, f32[4,1024]{1,0:T(4,128)S(1)}) custom-call(bf16[64,512]{1,0:T(8,128)(2,1)S(1)} %unet.1.x_ref.refs_0_, bf16[4,64,512]{2,1,0:T(8,128)(2,1)S(1)} %copy-done.2, bf16[512,1024]{1,0:T(8,128)(2,1)S(1)} %copy-done, s32[4]{0:T(128)} %assign_ref.1), custom_call_target="tpu_custom_call" | custom-call | tf_op jit(solution)/shard_map/own/pallas_call | solution.py:346
  17.5 0.0 collective-permute-done.4.refs_3_
  17.6 4.2 %collective-permute-done.3.refs_2_ = bf16[64,512]{1,0:T(8,128)(2,1)S(1)} collective-permute-done((bf16[64,512]{1,0:T(8,128)(2,1)S(1)}, bf16[64,512]{1,0:T(8,128)(2,1)S(1)}, u32[]{:S(2)}, u32[]{:S(2)}) %collective-permute-start.3) | collective-permute-done | bytes 65568 | tf_op jit(solution)/shard_map/ppermute | solution.py:362
  21.7 0.0 collective-permute-done.2.refs_1_
  21.7 1.3 %corr.1 = (bf16[64,512]{1,0:T(8,128)(2,1)}, f32[4,16,128]{2,1,0:T(8,128)S(1)}, bf16[4,16,128]{2,1,0:T(8,128)(2,1)S(1)}) custom-call(bf16[64,512]{1,0:T(8,128)(2,1)S(1)} %unet.1.x_ref.refs_0_, bf16[64,512]{1,0:T(8,128)(2,1)S(1)} %collective-permute-done.2.refs_1_, bf16[64,512]{1,0:T(8,128)(2,1)S(1)} %collective-permute-done.3.refs_2_, ...), custom_call_target="tpu_custom_call" | custom-call | tf_op jit(solution)/shard_map/corr/pallas_call | solution.py:346
  23.1 1.0 %collective-permute-start.5 = (bf16[4,16,128]{2,1,0:T(8,128)(2,1)S(1)}, bf16[4,16,128]{2,1,0:T(8,128)(2,1)S(1)}, u32[]{:S(2)}, u32[]{:S(2)}) collective-permute-start(bf16[4,16,128]{2,1,0:T(8,128)(2,1)S(1)} %get-tuple-element.55), channel_id=1, source_target_pairs={{0,2},{2,0},{4,6},{6,4},{1,3},{3,1},{5,7},{7,5},{8,10},{10,8},{12,... | collective-permute-start | bytes 49160 | tf_op jit(solution)/shard_map/ppermute | solution.py:454
  24.1 0.8 %collective-permute-done.5.got_ref = bf16[4,16,128]{2,1,0:T(8,128)(2,1)S(1)} collective-permute-done((bf16[4,16,128]{2,1,0:T(8,128)(2,1)S(1)}, bf16[4,16,128]{2,1,0:T(8,128)(2,1)S(1)}, u32[]{:S(2)}, u32[]{:S(2)}) %collective-permute-start.5) | collective-permute-done | bytes 16416 | tf_op jit(solution)/shard_map/ppermute | solution.py:454
  25.0 1.5 %collective-permute-start.6 = (bf16[16,128]{1,0:T(8,128)(2,1)S(1)}, bf16[16,128]{1,0:T(8,128)(2,1)S(1)}, u32[]{:S(2)}, u32[]{:S(2)}) collective-permute-start(bf16[16,128]{1,0:T(8,128)(2,1)S(1)} %get-tuple-element.57), channel_id=1, source_target_pairs={{0,1},{1,0},{2,3},{3,2},{4,5},{5,4},{6,7},{7,6},{8,9},{9,8},{10,11... | collective-permute-start | bytes 12296 | tf_op jit(solution)/shard_map/ppermute | solution.py:460
  26.5 2.7 %collective-permute-start.7 = (bf16[16,128]{1,0:T(8,128)(2,1)S(1)}, bf16[16,128]{1,0:T(8,128)(2,1)S(1)}, u32[]{:S(2)}, u32[]{:S(2)}) collective-permute-start(bf16[16,128]{1,0:T(8,128)(2,1)S(1)} %get-tuple-element.58), channel_id=1, source_target_pairs={{0,4},{1,5},{2,6},{3,7},{4,0},{5,1},{6,2},{7,3},{8,12},{9,13},{10,... | collective-permute-start | bytes 12296 | tf_op jit(solution)/shard_map/ppermute | solution.py:460
  29.2 1.6 %collective-permute-done.7 = bf16[16,128]{1,0:T(8,128)(2,1)S(1)} collective-permute-done((bf16[16,128]{1,0:T(8,128)(2,1)S(1)}, bf16[16,128]{1,0:T(8,128)(2,1)S(1)}, u32[]{:S(2)}, u32[]{:S(2)}) %collective-permute-start.7) | collective-permute-done | bytes 4128 | tf_op jit(solution)/shard_map/ppermute | solution.py:460
  30.8 2.9 %collective-permute-done.8 = bf16[16,128]{1,0:T(8,128)(2,1)S(1)} collective-permute-done((bf16[16,128]{1,0:T(8,128)(2,1)S(1)}, bf16[16,128]{1,0:T(8,128)(2,1)S(1)}, u32[]{:S(2)}, u32[]{:S(2)}) %collective-permute-start.8) | collective-permute-done | bytes 4128 | tf_op jit(solution)/shard_map/ppermute | solution.py:460
  33.7 0.6 %convert_add_fusion = f32[16,128]{1,0:T(8,128)} fusion(bf16[16,128]{1,0:T(8,128)(2,1)S(1)} %collective-permute-done.8, bf16[16,128]{1,0:T(8,128)(2,1)S(1)} %collective-permute-done.7, f32[16,128]{1,0:T(8,128)S(1)} %get-tuple-element.56, bf16[16,128]{1,0:T(8,128)(2,1)S(1)} %collective-permute-done.6), kind=kLoop, calls=%fused_computation | loop fusion | flops 12288 | bytes 28672 | tf_op jit(solution)/shard_map/add | solution.py:460
  (7 shorter events, 0.0 us)
Async XLA Ops:
  0.6 15.3 %copy-start = (bf16[512,1024]{1,0:T(8,128)(2,1)S(1)}, bf16[512,1024]{1,0:T(8,128)(2,1)}, u32[]{:S(2)}) copy-start(bf16[512,1024]{1,0:T(8,128)(2,1)} %constant.4.clone.table_ref.refs_8_) | copy-start | bytes 3145732
  1.8 2.9 %collective-permute-start = (bf16[8,512]{1,0:T(8,128)(2,1)S(1)}, bf16[8,512]{1,0:T(8,128)(2,1)S(1)}, u32[]{:S(2)}, u32[]{:S(2)}) collective-permute-start(bf16[8,512]{1,0:T(8,128)(2,1)S(1)} %get-tuple-element.33), channel_id=1, source_target_pairs={{0,2},{2,0},{4,6},{6,4},{1,3},{3,1},{5,7},{7,5},{8,10},{10,8},{12,... | collective-permute-start | bytes 24584 | tf_op jit(solution)/shard_map/ppermute | solution.py:391
  2.3 2.3 %collective-permute-start.1 = (bf16[8,512]{1,0:T(8,128)(2,1)S(1)}, bf16[8,512]{1,0:T(8,128)(2,1)S(1)}, u32[]{:S(2)}, u32[]{:S(2)}) collective-permute-start(bf16[8,512]{1,0:T(8,128)(2,1)S(1)} %get-tuple-element.34), channel_id=1, source_target_pairs={{2,4},{4,2},{3,5},{5,3},{10,12},{12,10},{11,13},{13,11},{18,20},{2... | collective-permute-start | bytes 24584 | tf_op jit(solution)/shard_map/ppermute | solution.py:393
  4.7 11.3 %copy-start.2 = (bf16[4,64,512]{2,1,0:T(8,128)(2,1)S(1)}, bf16[4,64,512]{2,1,0:T(8,128)(2,1)}, u32[]{:S(2)}) copy-start(bf16[4,64,512]{2,1,0:T(8,128)(2,1)} %t_ref.1) | copy-start | bytes 786436
  4.7 17.1 %copy-start.1 = (bf16[1024,512]{1,0:T(8,128)(2,1)S(1)}, bf16[1024,512]{1,0:T(8,128)(2,1)}, u32[]{:S(2)}) copy-start(bf16[1024,512]{1,0:T(8,128)(2,1)} %constant.5.clone.refs_9_) | copy-start | bytes 3145732
  10.2 7.3 %collective-permute-start.4 = (bf16[64,512]{1,0:T(8,128)(2,1)S(1)}, bf16[64,512]{1,0:T(8,128)(2,1)S(1)}, u32[]{:S(2)}, u32[]{:S(2)}) collective-permute-start(bf16[64,512]{1,0:T(8,128)(2,1)S(1)} %unet.1.x_ref.refs_0_), channel_id=1, source_target_pairs={{0,24},{8,0},{16,8},{24,16},{1,25},{9,1},{17,9},{25,17},{2,26},{10... | collective-permute-start | bytes 196616 | tf_op jit(solution)/shard_map/ppermute | solution.py:362
  14.9 6.8 %collective-permute-start.3 = (bf16[64,512]{1,0:T(8,128)(2,1)S(1)}, bf16[64,512]{1,0:T(8,128)(2,1)S(1)}, u32[]{:S(2)}, u32[]{:S(2)}) collective-permute-start(bf16[64,512]{1,0:T(8,128)(2,1)S(1)} %unet.1.x_ref.refs_0_), channel_id=1, source_target_pairs={{0,16},{8,24},{16,0},{24,8},{1,17},{9,25},{17,1},{25,9},{2,18},{10... | collective-permute-start | bytes 196616 | tf_op jit(solution)/shard_map/ppermute | solution.py:362
  14.9 6.8 %collective-permute-start.2 = (bf16[64,512]{1,0:T(8,128)(2,1)S(1)}, bf16[64,512]{1,0:T(8,128)(2,1)S(1)}, u32[]{:S(2)}, u32[]{:S(2)}) collective-permute-start(bf16[64,512]{1,0:T(8,128)(2,1)S(1)} %unet.1.x_ref.refs_0_), channel_id=1, source_target_pairs={{0,8},{8,16},{16,24},{24,0},{1,9},{9,17},{17,25},{25,1},{2,10},{10... | collective-permute-start | bytes 196616 | tf_op jit(solution)/shard_map/ppermute | solution.py:362
  23.1 1.9 %collective-permute-start.5 = (bf16[4,16,128]{2,1,0:T(8,128)(2,1)S(1)}, bf16[4,16,128]{2,1,0:T(8,128)(2,1)S(1)}, u32[]{:S(2)}, u32[]{:S(2)}) collective-permute-start(bf16[4,16,128]{2,1,0:T(8,128)(2,1)S(1)} %get-tuple-element.55), channel_id=1, source_target_pairs={{0,2},{2,0},{4,6},{6,4},{1,3},{3,1},{5,7},{7,5},{8,10},{10,8},{12,... | collective-permute-start | bytes 49160 | tf_op jit(solution)/shard_map/ppermute | solution.py:454
  25.0 4.2 %collective-permute-start.6 = (bf16[16,128]{1,0:T(8,128)(2,1)S(1)}, bf16[16,128]{1,0:T(8,128)(2,1)S(1)}, u32[]{:S(2)}, u32[]{:S(2)}) collective-permute-start(bf16[16,128]{1,0:T(8,128)(2,1)S(1)} %get-tuple-element.57), channel_id=1, source_target_pairs={{0,1},{1,0},{2,3},{3,2},{4,5},{5,4},{6,7},{7,6},{8,9},{9,8},{10,11... | collective-permute-start | bytes 12296 | tf_op jit(solution)/shard_map/ppermute | solution.py:460
  26.5 4.3 %collective-permute-start.7 = (bf16[16,128]{1,0:T(8,128)(2,1)S(1)}, bf16[16,128]{1,0:T(8,128)(2,1)S(1)}, u32[]{:S(2)}, u32[]{:S(2)}) collective-permute-start(bf16[16,128]{1,0:T(8,128)(2,1)S(1)} %get-tuple-element.58), channel_id=1, source_target_pairs={{0,4},{1,5},{2,6},{3,7},{4,0},{5,1},{6,2},{7,3},{8,12},{9,13},{10,... | collective-permute-start | bytes 12296 | tf_op jit(solution)/shard_map/ppermute | solution.py:460
  29.2 4.5 %collective-permute-start.8 = (bf16[16,128]{1,0:T(8,128)(2,1)S(1)}, bf16[16,128]{1,0:T(8,128)(2,1)S(1)}, u32[]{:S(2)}, u32[]{:S(2)}) collective-permute-start(bf16[16,128]{1,0:T(8,128)(2,1)S(1)} %get-tuple-element.59), channel_id=1, source_target_pairs={{0,5},{1,4},{2,7},{3,6},{4,1},{5,0},{6,3},{7,2},{8,13},{9,12},{10,... | collective-permute-start | bytes 12296 | tf_op jit(solution)/shard_map/ppermute | solution.py:460

commit v2 on v1

v2 whole, which is shorter than its diff:
```python
import functools
import math

import jax
import jax.numpy as jnp
import numpy as np
from jax import lax
from jax.experimental import pallas as pl
from jax.experimental.pallas import tpu as pltpu
from jax.sharding import PartitionSpec as P

BF = jnp.bfloat16
F32 = jnp.float32
EDGE = 8
ENC_ROWS = 8
MID_ROWS = 3
DEC_ROWS = 4
OUT_ROWS = 8
PAD = 16
OFF = -1e30


def frequency_order(patch_len):
    return np.concatenate([np.arange(0, patch_len, 2), np.arange(1, patch_len, 2)])


def forward_table(patch_len):
    s = np.arange(patch_len)[:, None]
    f = frequency_order(patch_len)[None, :]
    phase = ((s * f) % (2 * patch_len)).astype(np.float64) * (math.pi / patch_len)
    table = np.concatenate([np.cos(phase), np.sin(phase)], axis=1)
    table[:, patch_len] = 1.0 - 2.0 * (np.arange(patch_len) % 2)
    return table.astype(jnp.bfloat16)


def split_order(patch_len):
    return np.concatenate([np.arange(0, patch_len, 2), np.arange(1, patch_len, 2)])


def dot(a, b):
    return jnp.dot(a, b, preferred_element_type=F32)


def dot_nt(a, b):
    return lax.dot_general(a, b, (((1,), (1,)), ((), ())), preferred_element_type=F32)


def iota(shape, dim):
    return lax.broadcasted_iota(jnp.int32, shape, dim)


def column(row, count):
    m = row.shape[1]
    pick = iota((count, m), 0) % m == iota((count, m), 1)
    return jnp.sum(jnp.where(pick, row, 0.0), axis=1, keepdims=True)


def load_kernel(*refs):
    count = (len(refs) - 3) // 2
    sources = refs[:count]
    copies = refs[count : 2 * count]
    first_ref, second_ref, sems = refs[2 * count :]
    moves = [pltpu.make_async_copy(src, dst, sems.at[i]) for i, (src, dst) in enumerate(zip(sources, copies))]
    for move in moves:
        move.start()
    moves[0].wait()
    moves[1].wait()
    raw_ref, mask_ref = copies[:2]
    rows = raw_ref.shape[0]
    alive = column(mask_ref[...].astype(F32), rows)
    head = raw_ref[:EDGE].astype(F32) * alive[:EDGE]
    tail = raw_ref[rows - EDGE :].astype(F32) * alive[rows - EDGE :]
    odd = lax.axis_index("chan") % 2 == 1
    first_ref[...] = jnp.where(odd, head, tail).astype(BF)
    second_ref[...] = jnp.where(odd, tail, head).astype(BF)
    for move in moves[2:]:
        move.wait()


def thirds(x):
    high = x.astype(BF).astype(F32)
    middle = (x - high).astype(BF).astype(F32)
    return high, middle, x - high - middle


def prep_kernel(
    we_ref, wm_ref, wd_ref, be_ref, bm_ref, bd_ref, wo_ref, enc_ref, mid_ref, dec_ref, out_ref, bdec_ref, wide_ref
):
    maps = we_ref.shape[3]
    rows, cols = enc_ref.shape
    window = ENC_ROWS + EDGE
    spread = jnp.where(iota((rows, maps), 0) % maps == iota((rows, maps), 1), 1.0, 0.0).astype(BF)
    we = jnp.concatenate([we_ref[0, y].astype(F32) for y in range(3)], axis=0).astype(BF)
    taps = dot_nt(spread, we)
    row_id = iota((rows, cols), 0)
    col_id = iota((rows, cols), 1)
    q = row_id // maps % 4
    dy = col_id % window - row_id // (4 * maps) - (EDGE // 2 - 1)
    dx = col_id // window - q
    tap = jnp.where((dy >= 0) & (dy < 3) & (dx >= 0) & (dx < 3), dy * 3 + dx, -1)
    acc = jnp.zeros((rows, cols), F32)
    for t in range(9):
        acc = jnp.where(tap == t, taps[:, t : t + 1], acc)
    at = col_id - 6 * window
    for t, part in enumerate(thirds(column(be_ref[...], rows))):
        acc = jnp.where(at == t, part, acc)
    acc = jnp.where(((at == 3) & (q == 0)) | ((at == 4) & (q == 3)), OFF, acc)
    enc_ref[...] = acc.astype(BF)
    rows, cols = mid_ref.shape
    wide_ref[:rows, :cols] = jnp.zeros((rows, cols), F32)
    wm = wm_ref[...].astype(F32).reshape(9 * maps, 2 * maps).T
    for r in range(MID_ROWS):
        wide_ref[r * 2 * maps : (r + 1) * 2 * maps, r * 3 * maps : r * 3 * maps + 9 * maps] = wm
    acc = wide_ref[:rows, :cols]
    at = iota((rows, cols), 1) - (cols - PAD)
    for t, part in enumerate(thirds(column(bm_ref[...], rows))):
        acc = jnp.where(at == t, part, acc)
    mid_ref[...] = acc.astype(BF)
    wide_ref[...] = jnp.zeros(wide_ref.shape, F32)
    skip_cols = (DEC_ROWS + 2) * 4 * maps
    k = [[wd_ref[y, x].astype(F32) for x in range(3)] for y in range(3)]
    ws = [jnp.concatenate([k[y][x][:, 2 * maps :] for x in range(3)], axis=1) for y in range(3)]
    split = ((0,), (1, 2)), ((0, 1), (2,))
    wu = {}
    for r in range(2):
        for q in range(2):
            for a in range(2):
                wu[r, q, a] = jnp.concatenate(
                    [sum(k[y][x][:, : 2 * maps] for y in split[r][a] for x in split[q][b]) for b in range(2)], axis=1
                )
    for r in range(DEC_ROWS):
        for q in range(2):
            top = (r * 2 + q) * maps
            for y in range(3):
                left = ((r + y) * 4 + q) * maps
                wide_ref[top : top + maps, left : left + 3 * maps] = ws[y]
            for a in range(2):
                left = skip_cols + ((r + 1) // 2 + a) * 6 * maps + q * 2 * maps
                wide_ref[top : top + maps, left : left + 4 * maps] = wu[r % 2, q, a]
    dec_ref[...] = wide_ref[...].astype(BF)
    n = out_ref.shape[1]
    repeat = jnp.where(iota((maps, n), 1) % maps == iota((maps, n), 0), 1.0, 0.0).astype(BF)
    weights = dot(wo_ref[...], repeat)
    r_id = iota(out_ref.shape, 0)
    c_id = iota(out_ref.shape, 1)
    same = (c_id // (2 * maps) == r_id % OUT_ROWS) & (c_id // maps % 2 == r_id // OUT_ROWS)
    out_ref[...] = jnp.where(same, weights, 0.0).astype(BF)
    bdec_ref[...] = jnp.broadcast_to(column(bd_ref[...], 2 * maps), bdec_ref.shape)


def shifted(x, by):
    width = x.shape[1]
    lane = iota(x.shape, 1)
    edge = 0 if by < 0 else width - 1
    return jnp.where(lane == edge, 0.0, pltpu.roll(x, (-by) % width, 1))


def constants(half):
    row = iota((PAD, half), 0)
    lane = iota((PAD, half), 1)
    one = (row < 3) | ((row == 3) & (lane == 0)) | ((row == 4) & (lane == half - 1))
    return jnp.where(one, 1.0, 0.0).astype(BF)


def sixfold(even, uneven):
    return [shifted(even, -1), shifted(uneven, -1), even, uneven, shifted(even, 1), shifted(uneven, 1)]


def relu(y, keep=None):
    if keep is not None:
        y = y * keep
    return jnp.maximum(y.astype(BF), jnp.zeros((), BF))


def encode(weights, pieces, fixed, keeps, e4_ref, p3_ref):
    half = fixed.shape[1]
    window = jnp.concatenate([jnp.concatenate(pieces, axis=0).astype(BF), fixed], axis=0)
    y = dot(weights, window)
    span = y.shape[0] // ENC_ROWS
    maps = span // 4
    both = []
    for r in range(ENC_ROWS):
        piece = relu(y[r * span : (r + 1) * span], keeps[r])
        e4_ref[r * span : (r + 1) * span, :] = piece
        both.append(piece[maps : 3 * maps].astype(F32))
    for r in range(0, ENC_ROWS, 2):
        total = both[r] + both[r + 1]
        pooled = ((total[:maps] + total[maps:]) * 0.25).astype(BF).astype(F32)
        at = r // 2 * 3 * maps
        p3_ref[at : at + 3 * maps, :] = jnp.concatenate(
            [shifted(pooled, -1), pooled, shifted(pooled, 1)], axis=0
        ).astype(BF)


def inner_kernel(raw_ref, mask_ref, enc_ref, x_ref, perm_ref, e4_ref, p3_ref):
    rows, length = raw_ref.shape
    half = length // 2
    s = iota((length, half), 0)
    t = iota((length, half), 1)
    perm_ref[:, :half] = jnp.where(s == 2 * t, 1.0, 0.0).astype(BF)
    perm_ref[:, half:] = jnp.where(s == 2 * t + 1, 1.0, 0.0).astype(BF)
    alive = column(mask_ref[...].astype(F32), rows)
    x = dot((raw_ref[...].astype(F32) * alive).astype(BF), perm_ref[...])
    x_ref[...] = x
    six = sixfold(x[:, :half], x[:, half:])
    fixed = constants(half)
    span = enc_ref.shape[0] // ENC_ROWS
    pooled = span // 4 * 3 * ENC_ROWS // 2
    for g in range(rows // ENC_ROWS - 1):
        top = g * ENC_ROWS
        encode(
            enc_ref[...],
            [piece[top : top + ENC_ROWS + EDGE] for piece in six],
            fixed,
            [None] * ENC_ROWS,
            e4_ref.at[top * span : (top + ENC_ROWS) * span],
            p3_ref.at[g * pooled : (g + 1) * pooled],
        )


def rows_from(parts, low, high, span):
    found = []
    for first, stop, ref in parts:
        a, b = max(low, first), min(high, stop)
        if a < b:
            found.append(ref[(a - first) * span : (b - first) * span, :])
    return found


def unet_kernel(
    x_ref, mask_ref, perm_ref, r1_ref, r2_ref, e4_ref, p3_ref, enc_ref, mid_ref, dec_ref, wout_ref, bdec_ref, bout_ref,
    out_ref, e_top_ref, e_bottom_ref, p_top_ref, p_bottom_ref, m3_ref,
):
    rows, length = x_ref.shape
    half = length // 2
    span = enc_ref.shape[0] // ENC_ROWS
    maps = span // 4
    here = lax.axis_index("chan")
    last = lax.axis_size("chan") - 1
    odd = here % 2 == 1
    keep_top = jnp.where(here == 0, 0.0, 1.0)
    keep_bottom = jnp.where(here == last, 0.0, 1.0)
    alive = column(mask_ref[...].astype(F32), rows)
    r1 = r1_ref[...].astype(F32)
    r2 = r2_ref[...].astype(F32)
    edges = jnp.concatenate([jnp.where(odd, r1, r2), jnp.where(odd, r2, r1)], axis=0).astype(BF)
    edges = dot(edges, perm_ref[...])
    fixed = constants(half)
    margin = EDGE // 2
    for x, keeps, e_ref, p_ref in (
        (
            jnp.concatenate([edges[:EDGE], x_ref[:ENC_ROWS]], axis=0),
            [keep_top] * margin + [None] * (ENC_ROWS - margin),
            e_top_ref,
            p_top_ref,
        ),
        (
            jnp.concatenate([x_ref[rows - ENC_ROWS :], edges[EDGE:]], axis=0),
            [None] * (ENC_ROWS - margin) + [keep_bottom] * margin,
            e_bottom_ref,
            p_bottom_ref,
        ),
    ):
        encode(enc_ref[...], sixfold(x[:, :half], x[:, half:]), fixed, keeps, e_ref, p_ref)
    p_bottom_ref[ENC_ROWS // 2 * 3 * maps :, :] = jnp.zeros(
        (p_bottom_ref.shape[0] - ENC_ROWS // 2 * 3 * maps, half), BF
    )
    e4 = [(0, ENC_ROWS, e_top_ref), (ENC_ROWS, rows, e4_ref), (rows, rows + EDGE, e_bottom_ref)]
    few = ENC_ROWS // 2
    p3 = [(0, few, p_top_ref), (few, rows // 2, p3_ref), (rows // 2, rows // 2 + few + MID_ROWS, p_bottom_ref)]
    total = rows // 2 + 2
    span_m = 6 * maps
    for start in range(0, total, MID_ROWS):
        window = rows_from(p3, start, start + MID_ROWS + 2, 3 * maps)
        y = dot(mid_ref[...], jnp.concatenate(window + [fixed], axis=0))
        for r in range(min(MID_ROWS, total - start)):
            row = start + r
            keep = keep_top if row == 0 else keep_bottom if row == total - 1 else None
            piece = relu(y[r * 2 * maps : (r + 1) * 2 * maps], keep).astype(F32)
            m3_ref[row * span_m : (row + 1) * span_m, :] = jnp.concatenate(
                [shifted(piece, -1), piece, shifted(piece, 1)], axis=0
            ).astype(BF)
    m3 = [(0, total, m3_ref)]
    bias = jnp.concatenate([bdec_ref[...]] * DEC_ROWS, axis=0)
    for top in range(0, rows, OUT_ROWS):
        decoded = []
        for start in range(top, top + OUT_ROWS, DEC_ROWS):
            low = start + margin - 1
            window = rows_from(e4, low, low + DEC_ROWS + 2, span) + rows_from(
                m3, start // 2, start // 2 + DEC_ROWS // 2 + 2, span_m
            )
            decoded.append(relu(dot(dec_ref[...], jnp.concatenate(window, axis=0)) + bias))
        branch = dot(wout_ref[...], jnp.concatenate(decoded, axis=0))
        for q in range(2):
            own = x_ref[top : top + OUT_ROWS, q * half : (q + 1) * half]
            value = own + branch[q * OUT_ROWS : (q + 1) * OUT_ROWS] + bout_ref[0]
            out_ref[top : top + OUT_ROWS, q * half : (q + 1) * half] = (alive[top : top + OUT_ROWS] * value).astype(BF)


def products(spectra, ta_ref, tb_ref, tf_ref, put):
    tmpl, rows, length = ta_ref.shape
    count = len(spectra)
    for lane in range(0, length, 128):
        real = {}
        imag = {}
        for c in range(0, rows, 8):
            at = [ta_ref[r, c : c + 8, lane : lane + 128] for r in range(tmpl)]
            bt = [tb_ref[r, c : c + 8, lane : lane + 128] for r in range(tmpl)]
            af = at if lane else [tf_ref[r, c : c + 8, :] for r in range(tmpl)]
            for i in range(count):
                ax = spectra[i][c : c + 8, lane : lane + 128]
                bx = spectra[i][c : c + 8, length + lane : length + lane + 128]
                for r in range(tmpl):
                    re = ax * at[r] + bx * bt[r]
                    im = bx * af[r] - ax * bt[r]
                    real[r, i] = re if c == 0 else real[r, i] + re
                    imag[r, i] = im if c == 0 else imag[r, i] + im
        for r in range(tmpl):
            for i in range(count):
                put(r, i, lane, jnp.sum(real[r, i], axis=0, keepdims=True))
                put(r, i, length + lane, jnp.sum(imag[r, i], axis=0, keepdims=True))


def own_kernel(
    x_ref, t_ref, table_ref, split_ref, perm_ref, assign_ref,
    a_ref, b_ref, first_ref, p_ref, copy_ref, order_ref, s_ref, natural_ref, sems,
):
    fetch = pltpu.make_async_copy(assign_ref, order_ref, sems.at[0])
    fetch.start()
    natural_ref[...] = dot_nt(x_ref[...], perm_ref[...]).astype(BF)
    store = pltpu.make_async_copy(natural_ref, copy_ref, sems.at[1])
    store.start()
    tmpl, rows, length = t_ref.shape
    s_ref[...] = dot(x_ref[...], split_ref[...])
    fetch.wait()
    for r in range(tmpl):
        y = dot(t_ref[order_ref[r] % tmpl], table_ref[...])
        a = y[:, :length]
        b = y[:, length:]
        lane = iota((rows, 128), 1)
        a_ref[r] = a
        b_ref[r] = b
        b_ref[r, :, :128] = jnp.where(lane == 0, 0.0, b[:, :128])
        first_ref[r] = jnp.where(lane == 0, b[:, :128], a[:, :128])

    def put(r, i, lane, row):
        p_ref[r : r + 1, lane : lane + 128] = row

    products([s_ref], a_ref, b_ref, first_ref, put)
    store.wait()


def corr_kernel(others, *refs):
    x_refs = refs[:others]
    ta_ref, tb_ref, tf_ref, own_ref, table_ref, split_ref = refs[others : others + 6]
    keep_ref, send_ref, s_ref, p_ref, share_ref = refs[others + 6 :]
    count = others + 1
    tmpl, rows, length = ta_ref.shape
    here = lax.axis_index("tmpl")
    p_ref[here] = own_ref[...]
    if others:
        s_ref[...] = dot(jnp.concatenate([x_ref[...] for x_ref in x_refs], axis=0), split_ref[...])

    def put(r, i, lane, row):
        p_ref[(here + others - i) % count, r : r + 1, lane : lane + 128] = row

    products([s_ref.at[i * rows : (i + 1) * rows] for i in range(others)], ta_ref, tb_ref, tf_ref, put)
    p = jnp.concatenate([p_ref[i, r : r + 1, :] for r in range(tmpl) for i in range(count)], axis=0)
    lane = iota(p.shape, 1)
    p = jnp.where((lane == 0) | (lane == length), p * 0.5, p)
    high = p.astype(BF)
    low = (p - high.astype(F32)).astype(BF)
    pairs = tmpl * count
    both = jnp.concatenate([high, low], axis=0)
    half = length // 2

    def part(first):
        y = sum(dot_nt(both[:, at : at + half], table_ref[:, at : at + half]) for at in (first, length + first))
        return (y[:pairs] + y[pairs:]) * (1.0 / length)

    even = part(0)
    uneven = part(half)
    near = even + uneven
    far = even - uneven
    block = iota(far.shape, 0) % count
    later = jnp.where(block == count - 1, 0.0, pltpu.roll(far, pairs - 1, 0))
    parity = lax.axis_index("tm")
    far = jnp.where(parity == 1, far, later)
    width = share_ref.shape[3]
    chans = share_ref.shape[1]
    for c in range(chans):
        share_ref[0, c] = near[:, c * width : (c + 1) * width]
        share_ref[1, c] = far[:, c * width : (c + 1) * width]
    chan = lax.axis_index("chan")
    mine = chan // 2 * 2 + parity
    for k in range(chans):
        to = mine ^ k
        kind = (to + parity) % 2
        keep_ref[k] = share_ref[kind, to // 2 * 2 + chan % 2]
        send_ref[k] = share_ref[kind, to // 2 * 2 + 1 - chan % 2].astype(BF)


def fold_kernel(keep_ref, got_ref, own_ref, *outs):
    own_ref[...] = keep_ref[0] + got_ref[0].astype(F32)
    for k, out in enumerate(outs):
        out[...] = (keep_ref[k + 1] + got_ref[k + 1].astype(F32)).astype(BF)


VMEM = pltpu.MemorySpace.VMEM
HBM = pltpu.MemorySpace.HBM
SMEM = pltpu.MemorySpace.SMEM


def call(kernel, outs, scratch=(), hbm=(), smem=(), hbm_out=(), inputs=0, name=None):
    def run(*args):
        return inner(*[pltpu.with_memory_space_constraint(x, HBM) if i in hbm else x for i, x in enumerate(args)])

    inner = pl.pallas_call(
        kernel,
        out_shape=tuple(jax.ShapeDtypeStruct(s, d) for s, d in outs),
        in_specs=[pl.BlockSpec(memory_space=HBM if i in hbm else SMEM if i in smem else VMEM) for i in range(inputs)],
        out_specs=tuple(pl.BlockSpec(memory_space=HBM if i in hbm_out else VMEM) for i in range(len(outs))),
        scratch_shapes=scratch,
        name=name,
        compiler_params=pltpu.CompilerParams(vmem_limit_bytes=48 * 1024 * 1024),
    )
    return run


def rotated(x, axes, by):
    count = lax.axis_size(axes)
    return lax.ppermute(x, axes, [(i, (i + by) % count) for i in range(count)])


def body(raw, dead_mask, templates, assign, w_enc, b_enc, w_mid, b_mid, w_dec, b_dec, w_out, b_out):
    rows, length = raw.shape
    half = length // 2
    maps = w_enc.shape[0]
    chans = lax.axis_size("chan")
    blocks = lax.axis_size("tmpl")
    tmpl = templates.shape[0]
    small = [
        raw,
        dead_mask[None],
        w_enc.transpose(1, 2, 3, 0),
        w_mid.transpose(2, 3, 1, 0),
        w_dec.transpose(2, 3, 0, 1),
        b_enc[None],
        b_mid[None],
        b_dec[None],
        w_out[None],
    ]
    *loaded, first, second = call(
        load_kernel,
        [(x.shape, x.dtype) for x in small] + [((EDGE, length), BF)] * 2,
        [pltpu.SemaphoreType.DMA((len(small),))],
        hbm=range(len(small)),
        inputs=len(small),
        name="load",
    )(*small)
    r1 = lax.ppermute(first, "chan", [(i, i ^ 1) for i in range(chans) if i ^ 1 < chans])
    links = [(i, i + 1) for i in range(1, chans - 1, 2)]
    r2 = lax.ppermute(second, "chan", links + [(b, a) for a, b in links])

    dec_cols = (DEC_ROWS + 2) * 4 * maps + (DEC_ROWS // 2 + 2) * 6 * maps
    enc_w, mid_w, dec_w, out_w, dec_b = call(
        prep_kernel,
        [
            ((ENC_ROWS * 4 * maps, 6 * (ENC_ROWS + EDGE) + PAD), BF),
            ((MID_ROWS * 2 * maps, (MID_ROWS + 2) * 3 * maps + PAD), BF),
            ((DEC_ROWS * 2 * maps, dec_cols), BF),
            ((2 * OUT_ROWS, OUT_ROWS * 2 * maps), BF),
            ((2 * maps, half), F32),
        ],
        [pltpu.VMEM((DEC_ROWS * 2 * maps, dec_cols), F32)],
        inputs=7,
        name="prep",
    )(*loaded[2:9])
    x, perm, e4, p3 = call(
        inner_kernel,
        [
            ((rows, length), F32),
            ((length, length), BF),
            (((rows - ENC_ROWS) * 4 * maps, half), BF),
            (((rows - ENC_ROWS) // 2 * 3 * maps, half), BF),
        ],
        inputs=3,
        name="inner",
    )(*loaded[:2], enc_w)
    (denoised,) = call(
        unet_kernel,
        [((rows, length), BF)],
        [
            pltpu.VMEM((ENC_ROWS * 4 * maps, half), BF),
            pltpu.VMEM((ENC_ROWS * 4 * maps, half), BF),
            pltpu.VMEM((ENC_ROWS // 2 * 3 * maps, half), BF),
            pltpu.VMEM(((ENC_ROWS // 2 + MID_ROWS) * 3 * maps, half), BF),
            pltpu.VMEM(((rows // 2 + 2) * 6 * maps, half), BF),
        ],
        smem=(12,),
        inputs=13,
        name="unet",
    )(x, loaded[1], perm, r1, r2, e4, p3, enc_w, mid_w, dec_w, out_w, dec_b, b_out)

    forward = jnp.asarray(forward_table(length))
    split = jnp.asarray(forward_table(length)[split_order(length)])
    gathered = [rotated(denoised, "tmpl", k) for k in range(1, blocks)]
    *spectra, natural = call(
        own_kernel,
        [
            ((tmpl, rows, length), F32),
            ((tmpl, rows, length), F32),
            ((tmpl, rows, 128), F32),
            ((tmpl, 2 * length), F32),
            ((rows, length), BF),
        ],
        [
            pltpu.SMEM((tmpl,), jnp.int32),
            pltpu.VMEM((rows, 2 * length), F32),
            pltpu.VMEM((rows, length), BF),
            pltpu.SemaphoreType.DMA((2,)),
        ],
        hbm=(5,),
        hbm_out=(4,),
        inputs=6,
        name="own",
    )(denoised, templates, forward, split, perm, assign)
    width = length // chans
    pairs = tmpl * blocks
    keep, send = call(
        functools.partial(corr_kernel, blocks - 1),
        [((chans, pairs, width), F32), ((chans, pairs, width), BF)],
        [
            pltpu.VMEM(((blocks - 1) * rows, 2 * length), F32),
            pltpu.VMEM((blocks, tmpl, 2 * length), F32),
            pltpu.VMEM((2, chans, pairs, width), F32),
        ],
        inputs=blocks + 5,
        name="corr",
    )(*gathered, *spectra, forward, split)
    got = lax.ppermute(send, "chan", [(i, i ^ 1) for i in range(chans)])
    total, *parts = call(
        fold_kernel, [((pairs, width), F32)] + [((pairs, width), BF)] * (chans - 1), inputs=2, name="fold"
    )(keep, got)
    for k, part in enumerate(parts, 1):
        step = k // 2 * 4 + k % 2
        total = total + lax.ppermute(part, ("chan", "tm"), [(i, i ^ step) for i in range(2 * chans)]).astype(F32)
    return natural, total.reshape(tmpl, blocks, 1, width)


def solution(mesh):
    return jax.shard_map(
        body,
        mesh=mesh,
        in_specs=(
            P("chan", ("tmpl", "tm")),
            P("chan"),
            P("tmpl", "chan", None),
            P("tmpl"),
            P(),
            P(),
            P(),
            P(),
            P(),
            P(),
            P(),
            P(),
        ),
        out_specs=(P("chan", ("tmpl", "tm")), P("tmpl", None, "tm", "chan")),
        check_vma=False,
    )
```

time: 34.5 us -> 31 us (0.90)
  waiting for transfers between devices: 9.51 us -> 7.38 us
  Pallas kernels: 10.6 us -> 9.08 us
    ppermute x3, waiting for transfers between devices: 4.17 us -> 2.12 us  [rotated(): return lax.ppermute(x, axes, [(i, (i + by) % count) for i in range(count)])]
    pallas_call x6 -> x7, Pallas kernels: 10.6 us -> 9.08 us  [run(): inner(*[pltpu.with_memory_space_constraint(x, HBM) if i in hbm else x for...]
    ppermute x3, starting transfers between devices: 5.68 us -> 6.52 us  [rotated(): return lax.ppermute(x, axes, [(i, (i + by) % count) for i in range(count)])]
    ppermute x3, starting transfers between devices: 4.23 us -> 3.49 us  [body(): lax.ppermute(part, ('chan', 'tm'), [(i, i ^ step) for i in range(2 * chan...]
  transfers between devices with their start and end apart: 9 -> 9, of which waited for: 4 -> 5; matrix products, arithmetic and copies ran while one was open for 0% -> 0% of each run, Pallas kernels for 8% -> 12%
where the time goes in v2:
time: 31 us; the launch traced here: 30.8 us
  starting transfers between devices  12.4 us (40%)
  Pallas kernels  9.08 us (29%)
  waiting for transfers between devices  7.38 us (24%)
  between operations  1.38 us (4%)
  other arithmetic  0.6 us (2%)
    pallas_call x7, Pallas kernels, run(): inner(*[pltpu.with_memory_space_constraint(x, HBM) if i in hbm else x for...  9.08 us
    ppermute x3, starting transfers between devices, rotated(): return lax.ppermute(x, axes, [(i, (i + by) % count) for i in range(count)])  6.52 us
    ppermute x3, waiting for transfers between devices, body(): lax.ppermute(part, ('chan', 'tm'), [(i, i ^ step) for i in range(2 * chan...  4.41 us
    ppermute x3, starting transfers between devices, body(): lax.ppermute(part, ('chan', 'tm'), [(i, i ^ step) for i in range(2 * chan...  3.49 us
    ppermute x3, waiting for transfers between devices, rotated(): return lax.ppermute(x, axes, [(i, (i + by) % count) for i in range(count)])  2.12 us
    ppermute x1, starting transfers between devices, body(): got = lax.ppermute(send, 'chan', [(i, i ^ 1) for i in range(chans)])  1.15 us
    ppermute x1, waiting for transfers between devices, body(): got = lax.ppermute(send, 'chan', [(i, i ^ 1) for i in range(chans)])  0.84 us
    ppermute x1, starting transfers between devices, body(): r2 = lax.ppermute(second, 'chan', links + [(b, a) for a, b in links])  0.65 us
  transfers between devices with their start and end apart: 9, of which 5 were waited for; matrix products, arithmetic and copies ran while one was open for 0% of the time, Pallas kernels for 12%

profile of v2, /device:TPU:0, one launch (start us, length us, event | category | flops | bytes accessed | tf_op | source)
XLA Modules:
  0.0 30.8 jit_solution(8816758001215939701)
XLA Ops:
  0.6 1.0 %load.1 = (bf16[64,512]{1,0:T(8,128)(2,1)S(1)}, s32[1,64]{1,0:T(1,128)S(1)}, bf16[1,3,3,16]{3,2,1,0:T(4,128)(2,1)S(1)}, bf16[3,3,16,32]{3,2,1,0:T(8,128)(2,1)S(1...) custom-call(bf16[64,512]{1,0:T(8,128)(2,1)} %refs_0_.1, ...), custom_call_target="tpu_custom_call" | custom-call | tf_op jit(solution)/shard_map/load/pallas_call | solution.py:416
  1.7 0.6 %collective-permute-start = (bf16[8,512]{1,0:T(8,128)(2,1)S(1)}, bf16[8,512]{1,0:T(8,128)(2,1)S(1)}, u32[]{:S(2)}, u32[]{:S(2)}) collective-permute-start(bf16[8,512]{1,0:T(8,128)(2,1)S(1)} %get-tuple-element.45), channel_id=1, source_target_pairs={{0,2},{2,0},{4,6},{6,4},{1,3},{3,1},{5,7},{7,5},{8,10},{10,8},{12,... | collective-permute-start | bytes 24584 | tf_op jit(solution)/shard_map/ppermute | solution.py:461
  2.2 0.6 %collective-permute-start.1 = (bf16[8,512]{1,0:T(8,128)(2,1)S(1)}, bf16[8,512]{1,0:T(8,128)(2,1)S(1)}, u32[]{:S(2)}, u32[]{:S(2)}) collective-permute-start(bf16[8,512]{1,0:T(8,128)(2,1)S(1)} %get-tuple-element.46), channel_id=1, source_target_pairs={{2,4},{4,2},{3,5},{5,3},{10,12},{12,10},{11,13},{13,11},{18,20},{2... | collective-permute-start | bytes 24584 | tf_op jit(solution)/shard_map/ppermute | solution.py:463
  3.5 1.0 %prep.1 = (bf16[512,112]{1,0:T(8,128)(2,1)S(1)}, bf16[96,256]{1,0:T(8,128)(2,1)S(1)}, bf16[128,768]{1,0:T(8,128)(2,1)S(1)}, bf16[16,256]{1,0:T(8,128)(2,1)S(1)}, f32[32,256]{1,0:T(8,128)S(1)}) custom-call(bf16[1,3,3,16]{3,2,1,0:T(4,128)(2,1)S(1)} %get-tuple-element.35.we_ref, bf16[3,3,16,32]{3,2,1,0:T(8,128)(2,1)S(1)} %get-tuple-element.36.wm_ref, ...), custom_call_target="tpu_custom_call" | custom-call | tf_op jit(solution)/shard_map/prep/pallas_call | solution.py:416
  4.5 1.0 %inner.1 = (f32[64,512]{1,0:T(8,128)S(1)}, bf16[512,512]{1,0:T(8,128)(2,1)S(1)}, bf16[3584,256]{1,0:T(8,128)(2,1)S(1)}, bf16[1344,256]{1,0:T(8,128)(2,1)S(1)}) custom-call(bf16[64,512]{1,0:T(8,128)(2,1)S(1)} %get-tuple-element.33.raw_ref, s32[1,64]{1,0:T(1,128)S(1)} %get-tuple-element.34.mask_ref, bf16[512,112]{1,0:T(8,128)(2,1)S(1)} %get-tuple-element.42.enc_ref), custom_call_target="tpu_custom_call" | custom-call | tf_op jit(solution)/shard_map/inner/pallas_call | solution.py:416
  5.6 0.0 copy-start
  5.6 0.0 copy-start.1
  5.6 0.0 copy-start.2
  5.7 3.0 %unet.1.x_ref = bf16[64,512]{1,0:T(8,128)(2,1)S(1)} custom-call(f32[64,512]{1,0:T(8,128)S(1)} %get-tuple-element.43.x_ref, s32[1,64]{1,0:T(1,128)S(1)} %get-tuple-element.34.mask_ref, bf16[512,512]{1,0:T(8,128)(2,1)S(1)} %get-tuple-element.44.perm_ref, bf16[8,512]{1,0:T(8,128)(2,1)S(1)} %collective-permute-done.r1_ref, ...), custom_call_target="tpu_custom_call" | custom-call | tf_op jit(solution)/shard_map/unet/pallas_call | solution.py:416
  8.6 2.6 %collective-permute-start.2 = (bf16[64,512]{1,0:T(8,128)(2,1)S(1)}, bf16[64,512]{1,0:T(8,128)(2,1)S(1)}, u32[]{:S(2)}, u32[]{:S(2)}) collective-permute-start(bf16[64,512]{1,0:T(8,128)(2,1)S(1)} %unet.1.x_ref), channel_id=1, source_target_pairs={{0,8},{8,16},{16,24},{24,0},{1,9},{9,17},{17,25},{25,1},{2,10},{10... | collective-permute-start | bytes 196616 | tf_op jit(solution)/shard_map/ppermute | solution.py:432
  11.2 2.6 %collective-permute-start.3 = (bf16[64,512]{1,0:T(8,128)(2,1)S(1)}, bf16[64,512]{1,0:T(8,128)(2,1)S(1)}, u32[]{:S(2)}, u32[]{:S(2)}) collective-permute-start(bf16[64,512]{1,0:T(8,128)(2,1)S(1)} %unet.1.x_ref), channel_id=1, source_target_pairs={{0,16},{8,24},{16,0},{24,8},{1,17},{9,25},{17,1},{25,9},{2,18},{10... | collective-permute-start | bytes 196616 | tf_op jit(solution)/shard_map/ppermute | solution.py:432
  13.8 1.3 %collective-permute-start.4 = (bf16[64,512]{1,0:T(8,128)(2,1)S(1)}, bf16[64,512]{1,0:T(8,128)(2,1)S(1)}, u32[]{:S(2)}, u32[]{:S(2)}) collective-permute-start(bf16[64,512]{1,0:T(8,128)(2,1)S(1)} %unet.1.x_ref), channel_id=1, source_target_pairs={{0,24},{8,0},{16,8},{24,16},{1,25},{9,1},{17,9},{25,17},{2,26},{10... | collective-permute-start | bytes 196616 | tf_op jit(solution)/shard_map/ppermute | solution.py:432
  15.2 1.6 %own.1 = (f32[4,64,512]{2,1,0:T(8,128)S(1)}, f32[4,64,512]{2,1,0:T(8,128)S(1)}, f32[4,64,128]{2,1,0:T(8,128)S(1)}, f32[4,1024]{1,0:T(4,128)S(1)}, bf16[64,512]{1,0:T(8,128)(2,1)}) custom-call(bf16[64,512]{1,0:T(8,128)(2,1)S(1)} %unet.1.x_ref, bf16[4,64,512]{2,1,0:T(8,128)(2,1)S(1)} %copy-done.2, bf16[512,1024]{1,0:T(8,128)(2,1)S(1)} %copy-done, ...), custom_call_target="tpu_custom_call" | custom-call | tf_op jit(solution)/shard_map/own/pallas_call | solution.py:416
  16.8 2.1 %collective-permute-done.4.refs_2_ = bf16[64,512]{1,0:T(8,128)(2,1)S(1)} collective-permute-done((bf16[64,512]{1,0:T(8,128)(2,1)S(1)}, bf16[64,512]{1,0:T(8,128)(2,1)S(1)}, u32[]{:S(2)}, u32[]{:S(2)}) %collective-permute-start.4) | collective-permute-done | bytes 65568 | tf_op jit(solution)/shard_map/ppermute | solution.py:432
  19.0 1.4 %corr.1 = (f32[4,16,128]{2,1,0:T(8,128)S(1)}, bf16[4,16,128]{2,1,0:T(8,128)(2,1)S(1)}) custom-call(bf16[64,512]{1,0:T(8,128)(2,1)S(1)} %collective-permute-done.2.refs_0_, bf16[64,512]{1,0:T(8,128)(2,1)S(1)} %collective-permute-done.3.refs_1_, bf16[64,512]{1,0:T(8,128)(2,1)S(1)} %collective-permute-done.4.refs_2_, ...), custom_call_target="tpu_custom_call" | custom-call | tf_op jit(solution)/shard_map/corr/pallas_call | solution.py:416
  20.3 1.1 %collective-permute-start.5 = (bf16[4,16,128]{2,1,0:T(8,128)(2,1)S(1)}, bf16[4,16,128]{2,1,0:T(8,128)(2,1)S(1)}, u32[]{:S(2)}, u32[]{:S(2)}) collective-permute-start(bf16[4,16,128]{2,1,0:T(8,128)(2,1)S(1)} %get-tuple-element.59), channel_id=1, source_target_pairs={{0,2},{2,0},{4,6},{6,4},{1,3},{3,1},{5,7},{7,5},{8,10},{10,8},{12,... | collective-permute-start | bytes 49160 | tf_op jit(solution)/shard_map/ppermute | solution.py:541
  21.5 0.8 %collective-permute-done.5.got_ref = bf16[4,16,128]{2,1,0:T(8,128)(2,1)S(1)} collective-permute-done((bf16[4,16,128]{2,1,0:T(8,128)(2,1)S(1)}, bf16[4,16,128]{2,1,0:T(8,128)(2,1)S(1)}, u32[]{:S(2)}, u32[]{:S(2)}) %collective-permute-start.5) | collective-permute-done | bytes 16416 | tf_op jit(solution)/shard_map/ppermute | solution.py:541
  22.3 1.5 %collective-permute-start.6 = (bf16[16,128]{1,0:T(8,128)(2,1)S(1)}, bf16[16,128]{1,0:T(8,128)(2,1)S(1)}, u32[]{:S(2)}, u32[]{:S(2)}) collective-permute-start(bf16[16,128]{1,0:T(8,128)(2,1)S(1)} %get-tuple-element.61), channel_id=1, source_target_pairs={{0,1},{1,0},{2,3},{3,2},{4,5},{5,4},{6,7},{7,6},{8,9},{9,8},{10,11... | collective-permute-start | bytes 12296 | tf_op jit(solution)/shard_map/ppermute | solution.py:547
  23.8 1.9 %collective-permute-start.7 = (bf16[16,128]{1,0:T(8,128)(2,1)S(1)}, bf16[16,128]{1,0:T(8,128)(2,1)S(1)}, u32[]{:S(2)}, u32[]{:S(2)}) collective-permute-start(bf16[16,128]{1,0:T(8,128)(2,1)S(1)} %get-tuple-element.62), channel_id=1, source_target_pairs={{0,4},{1,5},{2,6},{3,7},{4,0},{5,1},{6,2},{7,3},{8,12},{9,13},{10,... | collective-permute-start | bytes 12296 | tf_op jit(solution)/shard_map/ppermute | solution.py:547
  25.7 0.1 collective-permute-start.8
  25.8 0.1 collective-permute-done.6
  25.9 1.5 %collective-permute-done.7 = bf16[16,128]{1,0:T(8,128)(2,1)S(1)} collective-permute-done((bf16[16,128]{1,0:T(8,128)(2,1)S(1)}, bf16[16,128]{1,0:T(8,128)(2,1)S(1)}, u32[]{:S(2)}, u32[]{:S(2)}) %collective-permute-start.7) | collective-permute-done | bytes 4128 | tf_op jit(solution)/shard_map/ppermute | solution.py:547
  27.4 2.8 %collective-permute-done.8 = bf16[16,128]{1,0:T(8,128)(2,1)S(1)} collective-permute-done((bf16[16,128]{1,0:T(8,128)(2,1)S(1)}, bf16[16,128]{1,0:T(8,128)(2,1)S(1)}, u32[]{:S(2)}, u32[]{:S(2)}) %collective-permute-start.8) | collective-permute-done | bytes 4128 | tf_op jit(solution)/shard_map/ppermute | solution.py:547
  30.2 0.6 %convert_add_fusion = f32[16,128]{1,0:T(8,128)} fusion(bf16[16,128]{1,0:T(8,128)(2,1)S(1)} %collective-permute-done.8, bf16[16,128]{1,0:T(8,128)(2,1)S(1)} %collective-permute-done.7, f32[16,128]{1,0:T(8,128)S(1)} %get-tuple-element.60, bf16[16,128]{1,0:T(8,128)(2,1)S(1)} %collective-permute-done.6), kind=kLoop, calls=%fused_computation | loop fusion | flops 12288 | bytes 28672 | tf_op jit(solution)/shard_map/add | solution.py:547
  (8 shorter events, 0.0 us)
Async XLA Ops:
  1.7 3.9 %collective-permute-start = (bf16[8,512]{1,0:T(8,128)(2,1)S(1)}, bf16[8,512]{1,0:T(8,128)(2,1)S(1)}, u32[]{:S(2)}, u32[]{:S(2)}) collective-permute-start(bf16[8,512]{1,0:T(8,128)(2,1)S(1)} %get-tuple-element.45), channel_id=1, source_target_pairs={{0,2},{2,0},{4,6},{6,4},{1,3},{3,1},{5,7},{7,5},{8,10},{10,8},{12,... | collective-permute-start | bytes 24584 | tf_op jit(solution)/shard_map/ppermute | solution.py:461
  2.2 3.4 %collective-permute-start.1 = (bf16[8,512]{1,0:T(8,128)(2,1)S(1)}, bf16[8,512]{1,0:T(8,128)(2,1)S(1)}, u32[]{:S(2)}, u32[]{:S(2)}) collective-permute-start(bf16[8,512]{1,0:T(8,128)(2,1)S(1)} %get-tuple-element.46), channel_id=1, source_target_pairs={{2,4},{4,2},{3,5},{5,3},{10,12},{12,10},{11,13},{13,11},{18,20},{2... | collective-permute-start | bytes 24584 | tf_op jit(solution)/shard_map/ppermute | solution.py:463
  5.6 9.6 %copy-start = (bf16[512,1024]{1,0:T(8,128)(2,1)S(1)}, bf16[512,1024]{1,0:T(8,128)(2,1)}, u32[]{:S(2)}) copy-start(bf16[512,1024]{1,0:T(8,128)(2,1)} %constant.4.clone.table_ref.refs_7_) | copy-start | bytes 3145732
  5.6 9.6 %copy-start.1 = (bf16[512,1024]{1,0:T(8,128)(2,1)S(1)}, bf16[512,1024]{1,0:T(8,128)(2,1)}, u32[]{:S(2)}) copy-start(bf16[512,1024]{1,0:T(8,128)(2,1)} %constant.5.clone.split_ref.refs_8_) | copy-start | bytes 3145732
  5.6 9.5 %copy-start.2 = (bf16[4,64,512]{2,1,0:T(8,128)(2,1)S(1)}, bf16[4,64,512]{2,1,0:T(8,128)(2,1)}, u32[]{:S(2)}) copy-start(bf16[4,64,512]{2,1,0:T(8,128)(2,1)} %t_ref.1) | copy-start | bytes 786436
  8.6 8.2 %collective-permute-start.2 = (bf16[64,512]{1,0:T(8,128)(2,1)S(1)}, bf16[64,512]{1,0:T(8,128)(2,1)S(1)}, u32[]{:S(2)}, u32[]{:S(2)}) collective-permute-start(bf16[64,512]{1,0:T(8,128)(2,1)S(1)} %unet.1.x_ref), channel_id=1, source_target_pairs={{0,8},{8,16},{16,24},{24,0},{1,9},{9,17},{17,25},{25,1},{2,10},{10... | collective-permute-start | bytes 196616 | tf_op jit(solution)/shard_map/ppermute | solution.py:432
  11.2 5.6 %collective-permute-start.3 = (bf16[64,512]{1,0:T(8,128)(2,1)S(1)}, bf16[64,512]{1,0:T(8,128)(2,1)S(1)}, u32[]{:S(2)}, u32[]{:S(2)}) collective-permute-start(bf16[64,512]{1,0:T(8,128)(2,1)S(1)} %unet.1.x_ref), channel_id=1, source_target_pairs={{0,16},{8,24},{16,0},{24,8},{1,17},{9,25},{17,1},{25,9},{2,18},{10... | collective-permute-start | bytes 196616 | tf_op jit(solution)/shard_map/ppermute | solution.py:432
  13.8 5.1 %collective-permute-start.4 = (bf16[64,512]{1,0:T(8,128)(2,1)S(1)}, bf16[64,512]{1,0:T(8,128)(2,1)S(1)}, u32[]{:S(2)}, u32[]{:S(2)}) collective-permute-start(bf16[64,512]{1,0:T(8,128)(2,1)S(1)} %unet.1.x_ref), channel_id=1, source_target_pairs={{0,24},{8,0},{16,8},{24,16},{1,25},{9,1},{17,9},{25,17},{2,26},{10... | collective-permute-start | bytes 196616 | tf_op jit(solution)/shard_map/ppermute | solution.py:432
  20.3 2.0 %collective-permute-start.5 = (bf16[4,16,128]{2,1,0:T(8,128)(2,1)S(1)}, bf16[4,16,128]{2,1,0:T(8,128)(2,1)S(1)}, u32[]{:S(2)}, u32[]{:S(2)}) collective-permute-start(bf16[4,16,128]{2,1,0:T(8,128)(2,1)S(1)} %get-tuple-element.59), channel_id=1, source_target_pairs={{0,2},{2,0},{4,6},{6,4},{1,3},{3,1},{5,7},{7,5},{8,10},{10,8},{12,... | collective-permute-start | bytes 49160 | tf_op jit(solution)/shard_map/ppermute | solution.py:541
  22.3 3.6 %collective-permute-start.6 = (bf16[16,128]{1,0:T(8,128)(2,1)S(1)}, bf16[16,128]{1,0:T(8,128)(2,1)S(1)}, u32[]{:S(2)}, u32[]{:S(2)}) collective-permute-start(bf16[16,128]{1,0:T(8,128)(2,1)S(1)} %get-tuple-element.61), channel_id=1, source_target_pairs={{0,1},{1,0},{2,3},{3,2},{4,5},{5,4},{6,7},{7,6},{8,9},{9,8},{10,11... | collective-permute-start | bytes 12296 | tf_op jit(solution)/shard_map/ppermute | solution.py:547
  23.8 3.6 %collective-permute-start.7 = (bf16[16,128]{1,0:T(8,128)(2,1)S(1)}, bf16[16,128]{1,0:T(8,128)(2,1)S(1)}, u32[]{:S(2)}, u32[]{:S(2)}) collective-permute-start(bf16[16,128]{1,0:T(8,128)(2,1)S(1)} %get-tuple-element.62), channel_id=1, source_target_pairs={{0,4},{1,5},{2,6},{3,7},{4,0},{5,1},{6,2},{7,3},{8,12},{9,13},{10,... | collective-permute-start | bytes 12296 | tf_op jit(solution)/shard_map/ppermute | solution.py:547
  25.7 4.5 %collective-permute-start.8 = (bf16[16,128]{1,0:T(8,128)(2,1)S(1)}, bf16[16,128]{1,0:T(8,128)(2,1)S(1)}, u32[]{:S(2)}, u32[]{:S(2)}) collective-permute-start(bf16[16,128]{1,0:T(8,128)(2,1)S(1)} %get-tuple-element.63), channel_id=1, source_target_pairs={{0,5},{1,4},{2,7},{3,6},{4,1},{5,0},{6,3},{7,2},{8,13},{9,12},{10,... | collective-permute-start | bytes 12296 | tf_op jit(solution)/shard_map/ppermute | solution.py:547

commit v3 on v2

--- a/solution.py
+++ b/solution.py
@@ -8,6 +8,7 @@
 from jax.experimental import pallas as pl
 from jax.experimental.pallas import tpu as pltpu
 from jax.sharding import PartitionSpec as P
+
 
 BF = jnp.bfloat16
 F32 = jnp.float32
@@ -87,25 +88,28 @@
     we_ref, wm_ref, wd_ref, be_ref, bm_ref, bd_ref, wo_ref, enc_ref, mid_ref, dec_ref, out_ref, bdec_ref, wide_ref
 ):
     maps = we_ref.shape[3]
-    rows, cols = enc_ref.shape
+    span = 4 * maps
+    width = -(-enc_ref.shape[1] // 128) * 128
     window = ENC_ROWS + EDGE
-    spread = jnp.where(iota((rows, maps), 0) % maps == iota((rows, maps), 1), 1.0, 0.0).astype(BF)
+    spread = jnp.where(iota((span, maps), 0) % maps == iota((span, maps), 1), 1.0, 0.0).astype(BF)
     we = jnp.concatenate([we_ref[0, y].astype(F32) for y in range(3)], axis=0).astype(BF)
     taps = dot_nt(spread, we)
-    row_id = iota((rows, cols), 0)
-    col_id = iota((rows, cols), 1)
-    q = row_id // maps % 4
-    dy = col_id % window - row_id // (4 * maps) - (EDGE // 2 - 1)
+    q = iota((span, width), 0) // maps
+    col_id = iota((span, width), 1)
+    dy = col_id % window - (EDGE // 2 - 1)
     dx = col_id // window - q
     tap = jnp.where((dy >= 0) & (dy < 3) & (dx >= 0) & (dx < 3), dy * 3 + dx, -1)
-    acc = jnp.zeros((rows, cols), F32)
+    band = jnp.zeros((span, width), F32)
     for t in range(9):
-        acc = jnp.where(tap == t, taps[:, t : t + 1], acc)
+        band = jnp.where(tap == t, taps[:, t : t + 1], band)
     at = col_id - 6 * window
-    for t, part in enumerate(thirds(column(be_ref[...], rows))):
-        acc = jnp.where(at == t, part, acc)
-    acc = jnp.where(((at == 3) & (q == 0)) | ((at == 4) & (q == 3)), OFF, acc)
-    enc_ref[...] = acc.astype(BF)
+    fixed = jnp.zeros((span, width), F32)
+    for t, part in enumerate(thirds(column(be_ref[...], span))):
+        fixed = jnp.where(at == t, part, fixed)
+    fixed = jnp.where(((at == 3) & (q == 0)) | ((at == 4) & (q == 3)), OFF, fixed)
+    for r in range(ENC_ROWS):
+        row = (pltpu.roll(band, r, 1) if r else band) + fixed
+        enc_ref[r * span : (r + 1) * span, :] = row[:, : enc_ref.shape[1]].astype(BF)
     rows, cols = mid_ref.shape
     wide_ref[:rows, :cols] = jnp.zeros((rows, cols), F32)
     wm = wm_ref[...].astype(F32).reshape(9 * maps, 2 * maps).T
@@ -173,7 +177,6 @@
 
 
 def encode(weights, pieces, fixed, keeps, e4_ref, p3_ref):
-    half = fixed.shape[1]
     window = jnp.concatenate([jnp.concatenate(pieces, axis=0).astype(BF), fixed], axis=0)
     y = dot(weights, window)
     span = y.shape[0] // ENC_ROWS
@@ -192,7 +195,34 @@
         ).astype(BF)
 
 
-def inner_kernel(raw_ref, mask_ref, enc_ref, x_ref, perm_ref, e4_ref, p3_ref):
+def rows_from(parts, low, high, span):
+    found = []
+    for first, stop, ref in parts:
+        a, b = max(low, first), min(high, stop)
+        if a < b:
+            found.append(ref[(a - first) * span : (b - first) * span, :])
+    return found
+
+
+def narrow(weights, parts, fixed, start, keeps, m3_ref, at):
+    maps2 = weights.shape[0] // MID_ROWS
+    window = rows_from(parts, start, start + MID_ROWS + 2, maps2 // 2 * 3)
+    y = dot(weights, jnp.concatenate(window + [fixed], axis=0))
+    for r, keep in enumerate(keeps):
+        piece = relu(y[r * maps2 : (r + 1) * maps2], keep).astype(F32)
+        m3_ref[(at + r) * 3 * maps2 : (at + r + 1) * 3 * maps2, :] = jnp.concatenate(
+            [shifted(piece, -1), piece, shifted(piece, 1)], axis=0
+        ).astype(BF)
+
+
+def early_middle(rows):
+    few = ENC_ROWS // 2
+    first = -(-few // MID_ROWS)
+    stop = (rows // 2 - MID_ROWS - 2) // MID_ROWS + 1
+    return first, stop
+
+
+def inner_kernel(raw_ref, mask_ref, enc_ref, mid_ref, x_ref, perm_ref, e4_ref, p3_ref, m3_ref):
     rows, length = raw_ref.shape
     half = length // 2
     s = iota((length, half), 0)
@@ -216,20 +246,15 @@
             e4_ref.at[top * span : (top + ENC_ROWS) * span],
             p3_ref.at[g * pooled : (g + 1) * pooled],
         )
-
-
-def rows_from(parts, low, high, span):
-    found = []
-    for first, stop, ref in parts:
-        a, b = max(low, first), min(high, stop)
-        if a < b:
-            found.append(ref[(a - first) * span : (b - first) * span, :])
-    return found
-
-
-def unet_kernel(
-    x_ref, mask_ref, perm_ref, r1_ref, r2_ref, e4_ref, p3_ref, enc_ref, mid_ref, dec_ref, wout_ref, bdec_ref, bout_ref,
-    out_ref, e_top_ref, e_bottom_ref, p_top_ref, p_bottom_ref, m3_ref,
+    first, stop = early_middle(rows)
+    parts = [(ENC_ROWS // 2, rows // 2, p3_ref)]
+    for g in range(first, stop):
+        narrow(mid_ref[...], parts, fixed, g * MID_ROWS, [None] * MID_ROWS, m3_ref, (g - first) * MID_ROWS)
+
+
+def edge_kernel(
+    x_ref, perm_ref, r1_ref, r2_ref, p3_ref, enc_ref, mid_ref,
+    e_top_ref, e_bottom_ref, m_top_ref, m_bottom_ref, p_top_ref, p_bottom_ref,
 ):
     rows, length = x_ref.shape
     half = length // 2
@@ -240,7 +265,6 @@
     odd = here % 2 == 1
     keep_top = jnp.where(here == 0, 0.0, 1.0)
     keep_bottom = jnp.where(here == last, 0.0, 1.0)
-    alive = column(mask_ref[...].astype(F32), rows)
     r1 = r1_ref[...].astype(F32)
     r2 = r2_ref[...].astype(F32)
     edges = jnp.concatenate([jnp.where(odd, r1, r2), jnp.where(odd, r2, r1)], axis=0).astype(BF)
@@ -265,36 +289,96 @@
     p_bottom_ref[ENC_ROWS // 2 * 3 * maps :, :] = jnp.zeros(
         (p_bottom_ref.shape[0] - ENC_ROWS // 2 * 3 * maps, half), BF
     )
-    e4 = [(0, ENC_ROWS, e_top_ref), (ENC_ROWS, rows, e4_ref), (rows, rows + EDGE, e_bottom_ref)]
     few = ENC_ROWS // 2
     p3 = [(0, few, p_top_ref), (few, rows // 2, p3_ref), (rows // 2, rows // 2 + few + MID_ROWS, p_bottom_ref)]
     total = rows // 2 + 2
-    span_m = 6 * maps
-    for start in range(0, total, MID_ROWS):
-        window = rows_from(p3, start, start + MID_ROWS + 2, 3 * maps)
-        y = dot(mid_ref[...], jnp.concatenate(window + [fixed], axis=0))
-        for r in range(min(MID_ROWS, total - start)):
-            row = start + r
-            keep = keep_top if row == 0 else keep_bottom if row == total - 1 else None
-            piece = relu(y[r * 2 * maps : (r + 1) * 2 * maps], keep).astype(F32)
-            m3_ref[row * span_m : (row + 1) * span_m, :] = jnp.concatenate(
-                [shifted(piece, -1), piece, shifted(piece, 1)], axis=0
-            ).astype(BF)
-    m3 = [(0, total, m3_ref)]
+    first, stop = early_middle(rows)
+    keeps = [keep_top] + [None] * (total - 2) + [keep_bottom]
+    for g in range(-(-total // MID_ROWS)):
+        start = g * MID_ROWS
+        if g < first:
+            narrow(mid_ref[...], p3, fixed, start, keeps[start : start + MID_ROWS], m_top_ref, start)
+        elif g >= stop:
+            narrow(
+                mid_ref[...], p3, fixed, start, keeps[start : start + MID_ROWS], m_bottom_ref, start - stop * MID_ROWS
+            )
+
+
+def decode_kernel(
+    x_ref, mask_ref, e_top_ref, e4_ref, e_bottom_ref, m_top_ref, m_ref, m_bottom_ref, dec_ref, wout_ref, bdec_ref, bout_ref,
+    out_ref,
+):
+    rows, length = x_ref.shape
+    half = length // 2
+    span = bdec_ref.shape[0] * 2
+    span_m = bdec_ref.shape[0] * 3
+    total = rows // 2 + 2
+    first, stop = early_middle(rows)
+    e4 = [(0, ENC_ROWS, e_top_ref), (ENC_ROWS, rows, e4_ref), (rows, rows + EDGE, e_bottom_ref)]
+    m3 = [
+        (0, first * MID_ROWS, m_top_ref),
+        (first * MID_ROWS, stop * MID_ROWS, m_ref),
+        (stop * MID_ROWS, total, m_bottom_ref),
+    ]
+    alive = column(mask_ref[...].astype(F32), rows)
     bias = jnp.concatenate([bdec_ref[...]] * DEC_ROWS, axis=0)
-    for top in range(0, rows, OUT_ROWS):
-        decoded = []
-        for start in range(top, top + OUT_ROWS, DEC_ROWS):
-            low = start + margin - 1
-            window = rows_from(e4, low, low + DEC_ROWS + 2, span) + rows_from(
-                m3, start // 2, start // 2 + DEC_ROWS // 2 + 2, span_m
-            )
-            decoded.append(relu(dot(dec_ref[...], jnp.concatenate(window, axis=0)) + bias))
-        branch = dot(wout_ref[...], jnp.concatenate(decoded, axis=0))
-        for q in range(2):
-            own = x_ref[top : top + OUT_ROWS, q * half : (q + 1) * half]
-            value = own + branch[q * OUT_ROWS : (q + 1) * OUT_ROWS] + bout_ref[0]
-            out_ref[top : top + OUT_ROWS, q * half : (q + 1) * half] = (alive[top : top + OUT_ROWS] * value).astype(BF)
+    depth = half
+    steps = dec_ref.shape[1] // depth
+    units = OUT_ROWS // DEC_ROWS
+    tiles = DEC_ROWS * bdec_ref.shape[0] * units // depth
+
+    def finish(*accs):
+        sums = [accs[:units], accs[units : 2 * units]]
+        outs = accs[2 * units :]
+        turn = [0] * units
+        waiting = None
+
+        def push(tile, unit):
+            slot = turn[unit] % 2
+            turn[unit] += 1
+            pltpu.matmul_push_rhs(tile, slot, unit)
+            return slot
+
+        def project(item):
+            top, decoded = item
+            unit = top // OUT_ROWS % units
+            for k in range(tiles):
+                slot = push(decoded[k * depth : (k + 1) * depth], unit)
+                pltpu.matmul_acc_lhs(outs[unit], wout_ref[:, k * depth : (k + 1) * depth], load_staged_rhs=slot)
+            branch = pltpu.matmul_pop(outs[unit])
+            for q in range(2):
+                own = x_ref[top : top + OUT_ROWS, q * half : (q + 1) * half]
+                value = own + branch[q * OUT_ROWS : (q + 1) * OUT_ROWS] + bout_ref[0]
+                out_ref[top : top + OUT_ROWS, q * half : (q + 1) * half] = (
+                    alive[top : top + OUT_ROWS] * value
+                ).astype(BF)
+
+        for top in range(0, rows, OUT_ROWS):
+            windows = []
+            for start in range(top, top + OUT_ROWS, DEC_ROWS):
+                low = start + EDGE // 2 - 1
+                windows.append(
+                    jnp.concatenate(
+                        rows_from(e4, low, low + DEC_ROWS + 2, span)
+                        + rows_from(m3, start // 2, start // 2 + DEC_ROWS // 2 + 2, span_m),
+                        axis=0,
+                    )
+                )
+            now = sums[top // OUT_ROWS % 2]
+            for k in range(steps):
+                slots = [push(w[k * depth : (k + 1) * depth], unit) for unit, w in enumerate(windows)]
+                for acc, slot in zip(now, slots):
+                    pltpu.matmul_acc_lhs(acc, dec_ref[:, k * depth : (k + 1) * depth], load_staged_rhs=slot)
+            if waiting:
+                project(waiting)
+            waiting = top, jnp.concatenate([relu(pltpu.matmul_pop(acc) + bias) for acc in now], axis=0)
+        project(waiting)
+
+    pl.run_scoped(
+        finish,
+        *(pltpu.ACC(unit)((dec_ref.shape[0], half), F32) for _ in range(2) for unit in range(units)),
+        *(pltpu.ACC(unit)((wout_ref.shape[0], half), F32) for unit in range(units)),
+    )
 
 
 def products(spectra, ta_ref, tb_ref, tf_ref, put):
@@ -350,21 +434,29 @@
     store.wait()
 
 
-def corr_kernel(others, *refs):
-    x_refs = refs[:others]
-    ta_ref, tb_ref, tf_ref, own_ref, table_ref, split_ref = refs[others : others + 6]
-    keep_ref, send_ref, s_ref, p_ref, share_ref = refs[others + 6 :]
-    count = others + 1
-    tmpl, rows, length = ta_ref.shape
+def other_kernel(x_ref, ta_ref, tb_ref, tf_ref, split_ref, p_ref, s_ref):
+    s_ref[...] = dot(x_ref[...], split_ref[...])
+
+    def put(r, i, lane, row):
+        p_ref[r : r + 1, lane : lane + 128] = row
+
+    products([s_ref], ta_ref, tb_ref, tf_ref, put)
+
+
+def corr_kernel(count, *refs):
+    part_refs = refs[: count - 1]
+    x_ref, ta_ref, tb_ref, tf_ref, table_ref, split_ref = refs[count - 1 : count + 5]
+    keep_ref, send_ref, s_ref, p_ref, share_ref = refs[count + 5 :]
+    tmpl, _, length = ta_ref.shape
     here = lax.axis_index("tmpl")
-    p_ref[here] = own_ref[...]
-    if others:
-        s_ref[...] = dot(jnp.concatenate([x_ref[...] for x_ref in x_refs], axis=0), split_ref[...])
+    for i, part_ref in enumerate(part_refs):
+        p_ref[(here - i) % count] = part_ref[...]
+    s_ref[...] = dot(x_ref[...], split_ref[...])
 
     def put(r, i, lane, row):
-        p_ref[(here + others - i) % count, r : r + 1, lane : lane + 128] = row
-
-    products([s_ref.at[i * rows : (i + 1) * rows] for i in range(others)], ta_ref, tb_ref, tf_ref, put)
+        p_ref[(here + 1) % count, r : r + 1, lane : lane + 128] = row
+
+    products([s_ref], ta_ref, tb_ref, tf_ref, put)
     p = jnp.concatenate([p_ref[i, r : r + 1, :] for r in range(tmpl) for i in range(count)], axis=0)
     lane = iota(p.shape, 1)
     p = jnp.where((lane == 0) | (lane == length), p * 0.5, p)
@@ -411,7 +503,7 @@
 SMEM = pltpu.MemorySpace.SMEM
 
 
-def call(kernel, outs, scratch=(), hbm=(), smem=(), hbm_out=(), inputs=0, name=None):
+def call(kernel, outs, scratch=(), hbm=(), smem=(), hbm_out=(), inputs=0):
     def run(*args):
         return inner(*[pltpu.with_memory_space_constraint(x, HBM) if i in hbm else x for i, x in enumerate(args)])
 
@@ -421,7 +513,6 @@
         in_specs=[pl.BlockSpec(memory_space=HBM if i in hbm else SMEM if i in smem else VMEM) for i in range(inputs)],
         out_specs=tuple(pl.BlockSpec(memory_space=HBM if i in hbm_out else VMEM) for i in range(len(outs))),
         scratch_shapes=scratch,
-        name=name,
         compiler_params=pltpu.CompilerParams(vmem_limit_bytes=48 * 1024 * 1024),
     )
     return run
@@ -450,17 +541,16 @@
         b_dec[None],
         w_out[None],
     ]
-    *loaded, first, second = call(
+    *loaded, send1, send2 = call(
         load_kernel,
         [(x.shape, x.dtype) for x in small] + [((EDGE, length), BF)] * 2,
         [pltpu.SemaphoreType.DMA((len(small),))],
         hbm=range(len(small)),
         inputs=len(small),
-        name="load",
     )(*small)
-    r1 = lax.ppermute(first, "chan", [(i, i ^ 1) for i in range(chans) if i ^ 1 < chans])
+    r1 = lax.ppermute(send1, "chan", [(i, i ^ 1) for i in range(chans) if i ^ 1 < chans])
     links = [(i, i + 1) for i in range(1, chans - 1, 2)]
-    r2 = lax.ppermute(second, "chan", links + [(b, a) for a, b in links])
+    r2 = lax.ppermute(send2, "chan", links + [(b, a) for a, b in links])
 
     dec_cols = (DEC_ROWS + 2) * 4 * maps + (DEC_ROWS // 2 + 2) * 6 * maps
     enc_w, mid_w, dec_w, out_w, dec_b = call(
@@ -474,37 +564,42 @@
         ],
         [pltpu.VMEM((DEC_ROWS * 2 * maps, dec_cols), F32)],
         inputs=7,
-        name="prep",
     )(*loaded[2:9])
-    x, perm, e4, p3 = call(
+    first, stop = early_middle(rows)
+    x, perm, e4, p3, m3 = call(
         inner_kernel,
         [
             ((rows, length), F32),
             ((length, length), BF),
             (((rows - ENC_ROWS) * 4 * maps, half), BF),
             (((rows - ENC_ROWS) // 2 * 3 * maps, half), BF),
+            (((stop - first) * MID_ROWS * 6 * maps, half), BF),
         ],
-        inputs=3,
-        name="inner",
-    )(*loaded[:2], enc_w)
-    (denoised,) = call(
-        unet_kernel,
-        [((rows, length), BF)],
+        inputs=4,
+    )(*loaded[:2], enc_w, mid_w)
+    e_top, e_bottom, m_top, m_bottom = call(
+        edge_kernel,
         [
-            pltpu.VMEM((ENC_ROWS * 4 * maps, half), BF),
-            pltpu.VMEM((ENC_ROWS * 4 * maps, half), BF),
+            ((ENC_ROWS * 4 * maps, half), BF),
+            ((ENC_ROWS * 4 * maps, half), BF),
+            ((first * MID_ROWS * 6 * maps, half), BF),
+            (((rows // 2 + 2 - stop * MID_ROWS) * 6 * maps, half), BF),
+        ],
+        [
             pltpu.VMEM((ENC_ROWS // 2 * 3 * maps, half), BF),
             pltpu.VMEM(((ENC_ROWS // 2 + MID_ROWS) * 3 * maps, half), BF),
-            pltpu.VMEM(((rows // 2 + 2) * 6 * maps, half), BF),
         ],
-        smem=(12,),
-        inputs=13,
-        name="unet",
-    )(x, loaded[1], perm, r1, r2, e4, p3, enc_w, mid_w, dec_w, out_w, dec_b, b_out)
+        inputs=7,
+    )(x, perm, r1, r2, p3, enc_w, mid_w)
+    (denoised,) = call(
+        decode_kernel, [((rows, length), BF)], smem=(11,), inputs=12
+    )(x, loaded[1], e_top, e4, e_bottom, m_top, m3, m_bottom, dec_w, out_w, dec_b, b_out)
 
     forward = jnp.asarray(forward_table(length))
     split = jnp.asarray(forward_table(length)[split_order(length)])
-    gathered = [rotated(denoised, "tmpl", k) for k in range(1, blocks)]
+    gathered = []
+    for k in range(1, blocks):
+        gathered.append(rotated(denoised, "tmpl", k))
     *spectra, natural = call(
         own_kernel,
         [
@@ -523,28 +618,33 @@
         hbm=(5,),
         hbm_out=(4,),
         inputs=6,
-        name="own",
     )(denoised, templates, forward, split, perm, assign)
     width = length // chans
     pairs = tmpl * blocks
+    sums = [spectra.pop()]
+    for x in gathered[:-1]:
+        (more,) = call(
+            other_kernel, [((tmpl, 2 * length), F32)], [pltpu.VMEM((rows, 2 * length), F32)], inputs=5
+        )(x, *spectra, split)
+        sums.append(more)
     keep, send = call(
-        functools.partial(corr_kernel, blocks - 1),
+        functools.partial(corr_kernel, blocks),
         [((chans, pairs, width), F32), ((chans, pairs, width), BF)],
         [
-            pltpu.VMEM(((blocks - 1) * rows, 2 * length), F32),
+            pltpu.VMEM((rows, 2 * length), F32),
             pltpu.VMEM((blocks, tmpl, 2 * length), F32),
             pltpu.VMEM((2, chans, pairs, width), F32),
         ],
         inputs=blocks + 5,
-        name="corr",
-    )(*gathered, *spectra, forward, split)
+    )(*sums, gathered[-1], *spectra, forward, split)
     got = lax.ppermute(send, "chan", [(i, i ^ 1) for i in range(chans)])
     total, *parts = call(
-        fold_kernel, [((pairs, width), F32)] + [((pairs, width), BF)] * (chans - 1), inputs=2, name="fold"
+        fold_kernel, [((pairs, width), F32)] + [((pairs, width), BF)] * (chans - 1), inputs=2
     )(keep, got)
     for k, part in enumerate(parts, 1):
         step = k // 2 * 4 + k % 2
-        total = total + lax.ppermute(part, ("chan", "tm"), [(i, i ^ step) for i in range(2 * chans)]).astype(F32)
+        got = lax.ppermute(part, ("chan", "tm"), [(i, i ^ step) for i in range(2 * chans)])
+        total = total + got.astype(F32)
     return natural, total.reshape(tmpl, blocks, 1, width)
 
 

time: 31 us -> 30.5 us (0.984)
  waiting for transfers between devices: 7.38 us -> 5.66 us
  starting transfers between devices: 12.4 us -> 13.8 us
    ppermute x3, waiting for transfers between devices: 2.12 us -> 0.45 us  [rotated(): return lax.ppermute(x, axes, [(i, (i + by) % count) for i in range(count)])]
    ppermute x3, starting transfers between devices: 6.52 us -> 7.43 us  [rotated(): return lax.ppermute(x, axes, [(i, (i + by) % count) for i in range(count)])]
    ppermute x1, starting transfers between devices: 1.15 us -> 1.68 us  [body(): got = lax.ppermute(send, 'chan', [(i, i ^ 1) for i in range(chans)])]
    pallas_call x7 -> x10, Pallas kernels: 9.08 us -> 8.85 us  [run(): inner(*[pltpu.with_memory_space_constraint(x, HBM) if i in hbm else x for...]
  transfers between devices with their start and end apart: 9 -> 9, of which waited for: 5 -> 5; matrix products, arithmetic and copies ran while one was open for 0% -> 0% of each run, Pallas kernels for 12% -> 15%
where the time goes in v3:
time: 30.5 us; the launch traced here: 30.3 us
  starting transfers between devices  13.8 us (45%)
  Pallas kernels  8.85 us (29%)
  waiting for transfers between devices  5.66 us (19%)
  between operations  1.41 us (5%)
  other arithmetic  0.6 us (2%)
    pallas_call x10, Pallas kernels, run(): inner(*[pltpu.with_memory_space_constraint(x, HBM) if i in hbm else x for...  8.85 us
    ppermute x3, starting transfers between devices, rotated(): return lax.ppermute(x, axes, [(i, (i + by) % count) for i in range(count)])  7.43 us
    ppermute x3, waiting for transfers between devices, body(): lax.ppermute(part, ('chan', 'tm'), [(i, i ^ step) for i in range(2 * chan...  4.37 us
    ppermute x3, starting transfers between devices, body(): lax.ppermute(part, ('chan', 'tm'), [(i, i ^ step) for i in range(2 * chan...  3.49 us
    ppermute x1, starting transfers between devices, body(): got = lax.ppermute(send, 'chan', [(i, i ^ 1) for i in range(chans)])  1.68 us
    ppermute x1, waiting for transfers between devices, body(): got = lax.ppermute(send, 'chan', [(i, i ^ 1) for i in range(chans)])  0.84 us
    ppermute x1, starting transfers between devices, body(): r2 = lax.ppermute(send2, 'chan', links + [(b, a) for a, b in links])  0.65 us
  transfers between devices with their start and end apart: 9, of which 5 were waited for; matrix products, arithmetic and copies ran while one was open for 0% of the time, Pallas kernels for 15%

profile of v3, /device:TPU:0, one launch (start us, length us, event | category | flops | bytes accessed | tf_op | source)
XLA Modules:
  0.0 30.3 jit_solution(14736207275154208959)
XLA Ops:
  0.6 1.0 %shard_map.149 = (bf16[64,512]{1,0:T(8,128)(2,1)S(1)}, s32[1,64]{1,0:T(1,128)S(1)}, bf16[1,3,3,16]{3,2,1,0:T(4,128)(2,1)S(1)}, bf16[3,3,16,32]{3,2,1,0:T(8,128)(...) custom-call(bf16[64,512]{1,0:T(8,128)(2,1)} %refs_0_.1, ...), custom_call_target="tpu_custom_call" | custom-call | tf_op jit(solution)/shard_map/pallas_call | solution.py:508
  1.7 0.6 %collective-permute-start = (bf16[8,512]{1,0:T(8,128)(2,1)S(1)}, bf16[8,512]{1,0:T(8,128)(2,1)S(1)}, u32[]{:S(2)}, u32[]{:S(2)}) collective-permute-start(bf16[8,512]{1,0:T(8,128)(2,1)S(1)} %get-tuple-element.51), channel_id=1, source_target_pairs={{0,2},{2,0},{4,6},{6,4},{1,3},{3,1},{5,7},{7,5},{8,10},{10,8},{12,... | collective-permute-start | bytes 24584 | tf_op jit(solution)/shard_map/ppermute | solution.py:551
  2.2 0.6 %collective-permute-start.1 = (bf16[8,512]{1,0:T(8,128)(2,1)S(1)}, bf16[8,512]{1,0:T(8,128)(2,1)S(1)}, u32[]{:S(2)}, u32[]{:S(2)}) collective-permute-start(bf16[8,512]{1,0:T(8,128)(2,1)S(1)} %get-tuple-element.52), channel_id=1, source_target_pairs={{2,4},{4,2},{3,5},{5,3},{10,12},{12,10},{11,13},{13,11},{18,20},{2... | collective-permute-start | bytes 24584 | tf_op jit(solution)/shard_map/ppermute | solution.py:553
  3.5 0.7 %shard_map.150 = (bf16[512,112]{1,0:T(8,128)(2,1)S(1)}, bf16[96,256]{1,0:T(8,128)(2,1)S(1)}, bf16[128,768]{1,0:T(8,128)(2,1)S(1)}, bf16[16,256]{1,0:T(8,128)(2,1)S(1)}, f32[32,256]{1,0:T(8,128)S(1)}) custom-call(bf16[1,3,3,16]{3,2,1,0:T(4,128)(2,1)S(1)} %get-tuple-element.40.we_ref, bf16[3,3,16,32]{3,2,1,0:T(8,128)(2,1)S(1)} %get-tuple-element.41.wm_ref, ...), custom_call_target="tpu_custom_call" | custom-call | tf_op jit(solution)/shard_map/pallas_call | solution.py:508
  4.2 1.3 %shard_map.151 = (f32[64,512]{1,0:T(8,128)S(1)}, bf16[512,512]{1,0:T(8,128)(2,1)S(1)}, bf16[3584,256]{1,0:T(8,128)(2,1)S(1)}, bf16[1344,256]{1,0:T(8,128)(2,1)S(1)}, bf16[2304,256]{1,0:T(8,128)(2,1)S(1)}) custom-call(bf16[64,512]{1,0:T(8,128)(2,1)S(1)} %get-tuple-element.38.raw_ref, s32[1,64]{1,0:T(1,128)S(1)} %get-tuple-element.39.mask_ref, ...), custom_call_target="tpu_custom_call" | custom-call | tf_op jit(solution)/shard_map/pallas_call | solution.py:508
  5.6 0.9 %shard_map.152 = (bf16[512,256]{1,0:T(8,128)(2,1)S(1)}, bf16[512,256]{1,0:T(8,128)(2,1)S(1)}, bf16[576,256]{1,0:T(8,128)(2,1)S(1)}, bf16[384,256]{1,0:T(8,128)(2,1)S(1)}) custom-call(f32[64,512]{1,0:T(8,128)S(1)} %get-tuple-element.49.x_ref, bf16[512,512]{1,0:T(8,128)(2,1)S(1)} %get-tuple-element.50.perm_ref, ...), custom_call_target="tpu_custom_call" | custom-call | tf_op jit(solution)/shard_map/pallas_call | solution.py:508
  6.5 1.5 %shard_map.153.x_ref = bf16[64,512]{1,0:T(8,128)(2,1)S(1)} custom-call(f32[64,512]{1,0:T(8,128)S(1)} %get-tuple-element.49.x_ref, s32[1,64]{1,0:T(1,128)S(1)} %get-tuple-element.39.mask_ref, bf16[512,256]{1,0:T(8,128)(2,1)S(1)} %get-tuple-element.54.e_top_ref, bf16[3584,256]{1,0:T(8,128)(2,1)S(1)} %get-tuple-element.55.e4_ref, ...), custom_call_target="tpu_custom_call" | custom-call | tf_op jit(solution)/shard_map/pallas_call | solution.py:508
  8.0 3.6 %collective-permute-start.3 = (bf16[64,512]{1,0:T(8,128)(2,1)S(1)}, bf16[64,512]{1,0:T(8,128)(2,1)S(1)}, u32[]{:S(2)}, u32[]{:S(2)}) collective-permute-start(bf16[64,512]{1,0:T(8,128)(2,1)S(1)} %shard_map.153.x_ref), channel_id=1, source_target_pairs={{0,16},{8,24},{16,0},{24,8},{1,17},{9,25},{17,1},{25,9},{2,18},{10... | collective-permute-start | bytes 196616 | tf_op jit(solution)/shard_map/ppermute | solution.py:523
  11.6 1.6 %collective-permute-start.2 = (bf16[64,512]{1,0:T(8,128)(2,1)S(1)}, bf16[64,512]{1,0:T(8,128)(2,1)S(1)}, u32[]{:S(2)}, u32[]{:S(2)}) collective-permute-start(bf16[64,512]{1,0:T(8,128)(2,1)S(1)} %shard_map.153.x_ref), channel_id=1, source_target_pairs={{0,8},{8,16},{16,24},{24,0},{1,9},{9,17},{17,25},{25,1},{2,10},{10... | collective-permute-start | bytes 196616 | tf_op jit(solution)/shard_map/ppermute | solution.py:523
  13.2 2.2 %collective-permute-start.4 = (bf16[64,512]{1,0:T(8,128)(2,1)S(1)}, bf16[64,512]{1,0:T(8,128)(2,1)S(1)}, u32[]{:S(2)}, u32[]{:S(2)}) collective-permute-start(bf16[64,512]{1,0:T(8,128)(2,1)S(1)} %shard_map.153.x_ref), channel_id=1, source_target_pairs={{0,24},{8,0},{16,8},{24,16},{1,25},{9,1},{17,9},{25,17},{2,26},{10... | collective-permute-start | bytes 196616 | tf_op jit(solution)/shard_map/ppermute | solution.py:523
  15.5 1.6 %shard_map.154 = (f32[4,64,512]{2,1,0:T(8,128)S(1)}, f32[4,64,512]{2,1,0:T(8,128)S(1)}, f32[4,64,128]{2,1,0:T(8,128)S(1)}, f32[4,1024]{1,0:T(4,128)S(1)}, bf16[64,512]{1,0:T(8,128)(2,1)}) custom-call(bf16[64,512]{1,0:T(8,128)(2,1)S(1)} %shard_map.153.x_ref, bf16[4,64,512]{2,1,0:T(8,128)(2,1)S(1)} %copy-done.2, bf16[512,1024]{1,0:T(8,128)(2,1)S(1)} %copy-done.1, ...), custom_call_target="tpu_custom_call" | custom-call | tf_op jit(solution)/shard_map/pallas_call | solution.py:508
  17.1 0.5 %shard_map.156.refs_2_ = f32[4,1024]{1,0:T(4,128)S(1)} custom-call(bf16[64,512]{1,0:T(8,128)(2,1)S(1)} %collective-permute-done.3.x_ref, f32[4,64,512]{2,1,0:T(8,128)S(1)} %get-tuple-element.65.ta_ref.refs_4_, f32[4,64,512]{2,1,0:T(8,128)S(1)} %get-tuple-element.66.tb_ref.refs_5_, f32[4,64,128]{2,1,0:T(8,128)S(1)} %get-tuple-element.67.tf_ref.refs_6_, ...), custom_call_target="tpu_custom_call" | custom-call | tf_op jit(solution)/shard_map/pallas_call | solution.py:508
  17.6 0.4 %collective-permute-done.2.x_ref = bf16[64,512]{1,0:T(8,128)(2,1)S(1)} collective-permute-done((bf16[64,512]{1,0:T(8,128)(2,1)S(1)}, bf16[64,512]{1,0:T(8,128)(2,1)S(1)}, u32[]{:S(2)}, u32[]{:S(2)}) %collective-permute-start.2) | collective-permute-done | bytes 65568 | tf_op jit(solution)/shard_map/ppermute | solution.py:523
  18.0 0.4 %shard_map.155.refs_1_ = f32[4,1024]{1,0:T(4,128)S(1)} custom-call(bf16[64,512]{1,0:T(8,128)(2,1)S(1)} %collective-permute-done.2.x_ref, f32[4,64,512]{2,1,0:T(8,128)S(1)} %get-tuple-element.65.ta_ref.refs_4_, f32[4,64,512]{2,1,0:T(8,128)S(1)} %get-tuple-element.66.tb_ref.refs_5_, f32[4,64,128]{2,1,0:T(8,128)S(1)} %get-tuple-element.67.tf_ref.refs_6_, ...), custom_call_target="tpu_custom_call" | custom-call | tf_op jit(solution)/shard_map/pallas_call | solution.py:508
  18.5 0.9 %shard_map.157 = (f32[4,16,128]{2,1,0:T(8,128)S(1)}, bf16[4,16,128]{2,1,0:T(8,128)(2,1)S(1)}) custom-call(f32[4,1024]{1,0:T(4,128)S(1)} %get-tuple-element.64.refs_0_, f32[4,1024]{1,0:T(4,128)S(1)} %shard_map.155.refs_1_, f32[4,1024]{1,0:T(4,128)S(1)} %shard_map.156.refs_2_, bf16[64,512]{1,0:T(8,128)(2,1)S(1)} %collective-permute-done.4.refs_3_, ...), custom_call_target="tpu_custom_call" | custom-call | tf_op jit(solution)/shard_map/pallas_call | solution.py:508
  19.4 1.7 %collective-permute-start.5 = (bf16[4,16,128]{2,1,0:T(8,128)(2,1)S(1)}, bf16[4,16,128]{2,1,0:T(8,128)(2,1)S(1)}, u32[]{:S(2)}, u32[]{:S(2)}) collective-permute-start(bf16[4,16,128]{2,1,0:T(8,128)(2,1)S(1)} %get-tuple-element.69), channel_id=1, source_target_pairs={{0,2},{2,0},{4,6},{6,4},{1,3},{3,1},{5,7},{7,5},{8,10},{10,8},{12,... | collective-permute-start | bytes 49160 | tf_op jit(solution)/shard_map/ppermute | solution.py:640
  21.0 0.8 %collective-permute-done.5.got_ref = bf16[4,16,128]{2,1,0:T(8,128)(2,1)S(1)} collective-permute-done((bf16[4,16,128]{2,1,0:T(8,128)(2,1)S(1)}, bf16[4,16,128]{2,1,0:T(8,128)(2,1)S(1)}, u32[]{:S(2)}, u32[]{:S(2)}) %collective-permute-start.5) | collective-permute-done | bytes 16416 | tf_op jit(solution)/shard_map/ppermute | solution.py:640
  21.9 1.5 %collective-permute-start.6 = (bf16[16,128]{1,0:T(8,128)(2,1)S(1)}, bf16[16,128]{1,0:T(8,128)(2,1)S(1)}, u32[]{:S(2)}, u32[]{:S(2)}) collective-permute-start(bf16[16,128]{1,0:T(8,128)(2,1)S(1)} %get-tuple-element.71), channel_id=1, source_target_pairs={{0,1},{1,0},{2,3},{3,2},{4,5},{5,4},{6,7},{7,6},{8,9},{9,8},{10,11... | collective-permute-start | bytes 12296 | tf_op jit(solution)/shard_map/ppermute | solution.py:646
  23.4 1.9 %collective-permute-start.7 = (bf16[16,128]{1,0:T(8,128)(2,1)S(1)}, bf16[16,128]{1,0:T(8,128)(2,1)S(1)}, u32[]{:S(2)}, u32[]{:S(2)}) collective-permute-start(bf16[16,128]{1,0:T(8,128)(2,1)S(1)} %get-tuple-element.72), channel_id=1, source_target_pairs={{0,4},{1,5},{2,6},{3,7},{4,0},{5,1},{6,2},{7,3},{8,12},{9,13},{10,... | collective-permute-start | bytes 12296 | tf_op jit(solution)/shard_map/ppermute | solution.py:646
  25.2 0.1 collective-permute-start.8
  25.4 0.1 collective-permute-done.6
  25.5 1.5 %collective-permute-done.7 = bf16[16,128]{1,0:T(8,128)(2,1)S(1)} collective-permute-done((bf16[16,128]{1,0:T(8,128)(2,1)S(1)}, bf16[16,128]{1,0:T(8,128)(2,1)S(1)}, u32[]{:S(2)}, u32[]{:S(2)}) %collective-permute-start.7) | collective-permute-done | bytes 4128 | tf_op jit(solution)/shard_map/ppermute | solution.py:646
  27.0 2.8 %collective-permute-done.8 = bf16[16,128]{1,0:T(8,128)(2,1)S(1)} collective-permute-done((bf16[16,128]{1,0:T(8,128)(2,1)S(1)}, bf16[16,128]{1,0:T(8,128)(2,1)S(1)}, u32[]{:S(2)}, u32[]{:S(2)}) %collective-permute-start.8) | collective-permute-done | bytes 4128 | tf_op jit(solution)/shard_map/ppermute | solution.py:646
  29.7 0.6 %convert_add_fusion = f32[16,128]{1,0:T(8,128)} fusion(bf16[16,128]{1,0:T(8,128)(2,1)S(1)} %collective-permute-done.8, bf16[16,128]{1,0:T(8,128)(2,1)S(1)} %collective-permute-done.7, f32[16,128]{1,0:T(8,128)S(1)} %get-tuple-element.70, bf16[16,128]{1,0:T(8,128)(2,1)S(1)} %collective-permute-done.6), kind=kLoop, calls=%fused_computation | loop fusion | flops 12288 | bytes 28672 | tf_op jit(solution)/shard_map/add | solution.py:647
  (11 shorter events, 0.0 us)
Async XLA Ops:
  1.7 3.9 %collective-permute-start = (bf16[8,512]{1,0:T(8,128)(2,1)S(1)}, bf16[8,512]{1,0:T(8,128)(2,1)S(1)}, u32[]{:S(2)}, u32[]{:S(2)}) collective-permute-start(bf16[8,512]{1,0:T(8,128)(2,1)S(1)} %get-tuple-element.51), channel_id=1, source_target_pairs={{0,2},{2,0},{4,6},{6,4},{1,3},{3,1},{5,7},{7,5},{8,10},{10,8},{12,... | collective-permute-start | bytes 24584 | tf_op jit(solution)/shard_map/ppermute | solution.py:551
  2.2 3.3 %collective-permute-start.1 = (bf16[8,512]{1,0:T(8,128)(2,1)S(1)}, bf16[8,512]{1,0:T(8,128)(2,1)S(1)}, u32[]{:S(2)}, u32[]{:S(2)}) collective-permute-start(bf16[8,512]{1,0:T(8,128)(2,1)S(1)} %get-tuple-element.52), channel_id=1, source_target_pairs={{2,4},{4,2},{3,5},{5,3},{10,12},{12,10},{11,13},{13,11},{18,20},{2... | collective-permute-start | bytes 24584 | tf_op jit(solution)/shard_map/ppermute | solution.py:553
  6.5 9.0 %copy-start = (bf16[512,1024]{1,0:T(8,128)(2,1)S(1)}, bf16[512,1024]{1,0:T(8,128)(2,1)}, u32[]{:S(2)}) copy-start(bf16[512,1024]{1,0:T(8,128)(2,1)} %constant.5.clone.split_ref.refs_8_) | copy-start | bytes 3145732
  6.5 8.9 %copy-start.1 = (bf16[512,1024]{1,0:T(8,128)(2,1)S(1)}, bf16[512,1024]{1,0:T(8,128)(2,1)}, u32[]{:S(2)}) copy-start(bf16[512,1024]{1,0:T(8,128)(2,1)} %constant.4.clone.table_ref.refs_7_) | copy-start | bytes 3145732
  6.5 8.9 %copy-start.2 = (bf16[4,64,512]{2,1,0:T(8,128)(2,1)S(1)}, bf16[4,64,512]{2,1,0:T(8,128)(2,1)}, u32[]{:S(2)}) copy-start(bf16[4,64,512]{2,1,0:T(8,128)(2,1)} %t_ref.1) | copy-start | bytes 786436
  8.0 9.1 %collective-permute-start.3 = (bf16[64,512]{1,0:T(8,128)(2,1)S(1)}, bf16[64,512]{1,0:T(8,128)(2,1)S(1)}, u32[]{:S(2)}, u32[]{:S(2)}) collective-permute-start(bf16[64,512]{1,0:T(8,128)(2,1)S(1)} %shard_map.153.x_ref), channel_id=1, source_target_pairs={{0,16},{8,24},{16,0},{24,8},{1,17},{9,25},{17,1},{25,9},{2,18},{10... | collective-permute-start | bytes 196616 | tf_op jit(solution)/shard_map/ppermute | solution.py:523
  11.6 6.4 %collective-permute-start.2 = (bf16[64,512]{1,0:T(8,128)(2,1)S(1)}, bf16[64,512]{1,0:T(8,128)(2,1)S(1)}, u32[]{:S(2)}, u32[]{:S(2)}) collective-permute-start(bf16[64,512]{1,0:T(8,128)(2,1)S(1)} %shard_map.153.x_ref), channel_id=1, source_target_pairs={{0,8},{8,16},{16,24},{24,0},{1,9},{9,17},{17,25},{25,1},{2,10},{10... | collective-permute-start | bytes 196616 | tf_op jit(solution)/shard_map/ppermute | solution.py:523
  13.2 5.3 %collective-permute-start.4 = (bf16[64,512]{1,0:T(8,128)(2,1)S(1)}, bf16[64,512]{1,0:T(8,128)(2,1)S(1)}, u32[]{:S(2)}, u32[]{:S(2)}) collective-permute-start(bf16[64,512]{1,0:T(8,128)(2,1)S(1)} %shard_map.153.x_ref), channel_id=1, source_target_pairs={{0,24},{8,0},{16,8},{24,16},{1,25},{9,1},{17,9},{25,17},{2,26},{10... | collective-permute-start | bytes 196616 | tf_op jit(solution)/shard_map/ppermute | solution.py:523
  19.4 2.5 %collective-permute-start.5 = (bf16[4,16,128]{2,1,0:T(8,128)(2,1)S(1)}, bf16[4,16,128]{2,1,0:T(8,128)(2,1)S(1)}, u32[]{:S(2)}, u32[]{:S(2)}) collective-permute-start(bf16[4,16,128]{2,1,0:T(8,128)(2,1)S(1)} %get-tuple-element.69), channel_id=1, source_target_pairs={{0,2},{2,0},{4,6},{6,4},{1,3},{3,1},{5,7},{7,5},{8,10},{10,8},{12,... | collective-permute-start | bytes 49160 | tf_op jit(solution)/shard_map/ppermute | solution.py:640
  21.9 3.6 %collective-permute-start.6 = (bf16[16,128]{1,0:T(8,128)(2,1)S(1)}, bf16[16,128]{1,0:T(8,128)(2,1)S(1)}, u32[]{:S(2)}, u32[]{:S(2)}) collective-permute-start(bf16[16,128]{1,0:T(8,128)(2,1)S(1)} %get-tuple-element.71), channel_id=1, source_target_pairs={{0,1},{1,0},{2,3},{3,2},{4,5},{5,4},{6,7},{7,6},{8,9},{9,8},{10,11... | collective-permute-start | bytes 12296 | tf_op jit(solution)/shard_map/ppermute | solution.py:646
  23.4 3.6 %collective-permute-start.7 = (bf16[16,128]{1,0:T(8,128)(2,1)S(1)}, bf16[16,128]{1,0:T(8,128)(2,1)S(1)}, u32[]{:S(2)}, u32[]{:S(2)}) collective-permute-start(bf16[16,128]{1,0:T(8,128)(2,1)S(1)} %get-tuple-element.72), channel_id=1, source_target_pairs={{0,4},{1,5},{2,6},{3,7},{4,0},{5,1},{6,2},{7,3},{8,12},{9,13},{10,... | collective-permute-start | bytes 12296 | tf_op jit(solution)/shard_map/ppermute | solution.py:646
  25.2 4.5 %collective-permute-start.8 = (bf16[16,128]{1,0:T(8,128)(2,1)S(1)}, bf16[16,128]{1,0:T(8,128)(2,1)S(1)}, u32[]{:S(2)}, u32[]{:S(2)}) collective-permute-start(bf16[16,128]{1,0:T(8,128)(2,1)S(1)} %get-tuple-element.73), channel_id=1, source_target_pairs={{0,5},{1,4},{2,7},{3,6},{4,1},{5,0},{6,3},{7,2},{8,13},{9,12},{10,... | collective-permute-start | bytes 12296 | tf_op jit(solution)/shard_map/ppermute | solution.py:646

commit v4 on v3

--- a/solution.py
+++ b/solution.py
@@ -18,7 +18,6 @@
 DEC_ROWS = 4
 OUT_ROWS = 8
 PAD = 16
-OFF = -1e30
 
 
 def frequency_order(patch_len):
@@ -57,13 +56,19 @@
 
 
 def load_kernel(*refs):
-    count = (len(refs) - 3) // 2
+    count = (len(refs) - 4) // 2
     sources = refs[:count]
     copies = refs[count : 2 * count]
-    first_ref, second_ref, sems = refs[2 * count :]
+    first_ref, second_ref, perm_ref, sems = refs[2 * count :]
     moves = [pltpu.make_async_copy(src, dst, sems.at[i]) for i, (src, dst) in enumerate(zip(sources, copies))]
     for move in moves:
         move.start()
+    length = perm_ref.shape[0]
+    half = length // 2
+    s = iota((length, half), 0)
+    t = iota((length, half), 1)
+    perm_ref[:, :half] = jnp.where(s == 2 * t, 1.0, 0.0).astype(BF)
+    perm_ref[:, half:] = jnp.where(s == 2 * t + 1, 1.0, 0.0).astype(BF)
     moves[0].wait()
     moves[1].wait()
     raw_ref, mask_ref = copies[:2]
@@ -88,7 +93,7 @@
     we_ref, wm_ref, wd_ref, be_ref, bm_ref, bd_ref, wo_ref, enc_ref, mid_ref, dec_ref, out_ref, bdec_ref, wide_ref
 ):
     maps = we_ref.shape[3]
-    span = 4 * maps
+    span = 2 * maps
     width = -(-enc_ref.shape[1] // 128) * 128
     window = ENC_ROWS + EDGE
     spread = jnp.where(iota((span, maps), 0) % maps == iota((span, maps), 1), 1.0, 0.0).astype(BF)
@@ -102,11 +107,10 @@
     band = jnp.zeros((span, width), F32)
     for t in range(9):
         band = jnp.where(tap == t, taps[:, t : t + 1], band)
-    at = col_id - 6 * window
+    at = col_id - 4 * window
     fixed = jnp.zeros((span, width), F32)
     for t, part in enumerate(thirds(column(be_ref[...], span))):
         fixed = jnp.where(at == t, part, fixed)
-    fixed = jnp.where(((at == 3) & (q == 0)) | ((at == 4) & (q == 3)), OFF, fixed)
     for r in range(ENC_ROWS):
         row = (pltpu.roll(band, r, 1) if r else band) + fixed
         enc_ref[r * span : (r + 1) * span, :] = row[:, : enc_ref.shape[1]].astype(BF)
@@ -154,20 +158,21 @@
 
 def shifted(x, by):
     width = x.shape[1]
-    lane = iota(x.shape, 1)
-    edge = 0 if by < 0 else width - 1
-    return jnp.where(lane == edge, 0.0, pltpu.roll(x, (-by) % width, 1))
+    moved = pltpu.roll(x, (-by) % width, 1)
+    cut = width // 2
+    parts = [moved[:, :cut], moved[:, cut:]]
+    at = 0 if by < 0 else 1
+    edge = iota(parts[at].shape, 1) == (0 if by < 0 else width - cut - 1)
+    parts[at] = jnp.where(edge, jnp.zeros((), x.dtype), parts[at])
+    return jnp.concatenate(parts, axis=1)
 
 
 def constants(half):
-    row = iota((PAD, half), 0)
-    lane = iota((PAD, half), 1)
-    one = (row < 3) | ((row == 3) & (lane == 0)) | ((row == 4) & (lane == half - 1))
-    return jnp.where(one, 1.0, 0.0).astype(BF)
-
-
-def sixfold(even, uneven):
-    return [shifted(even, -1), shifted(uneven, -1), even, uneven, shifted(even, 1), shifted(uneven, 1)]
+    return jnp.where(iota((PAD, half), 0) < 3, 1.0, 0.0).astype(BF)
+
+
+def fourfold(even, uneven):
+    return [shifted(uneven, -1), even, uneven, shifted(even, 1)]
 
 
 def relu(y, keep=None):
@@ -180,19 +185,19 @@
     window = jnp.concatenate([jnp.concatenate(pieces, axis=0).astype(BF), fixed], axis=0)
     y = dot(weights, window)
     span = y.shape[0] // ENC_ROWS
-    maps = span // 4
+    maps = span // 2
     both = []
     for r in range(ENC_ROWS):
         piece = relu(y[r * span : (r + 1) * span], keeps[r])
-        e4_ref[r * span : (r + 1) * span, :] = piece
-        both.append(piece[maps : 3 * maps].astype(F32))
+        e4_ref[r * 2 * span : (r + 1) * 2 * span, :] = jnp.concatenate(fourfold(piece[:maps], piece[maps:]), axis=0)
+        both.append(piece.astype(F32))
     for r in range(0, ENC_ROWS, 2):
         total = both[r] + both[r + 1]
-        pooled = ((total[:maps] + total[maps:]) * 0.25).astype(BF).astype(F32)
+        pooled = ((total[:maps] + total[maps:]) * 0.25).astype(BF)
         at = r // 2 * 3 * maps
         p3_ref[at : at + 3 * maps, :] = jnp.concatenate(
             [shifted(pooled, -1), pooled, shifted(pooled, 1)], axis=0
-        ).astype(BF)
+        )
 
 
 def rows_from(parts, low, high, span):
@@ -209,10 +214,10 @@
     window = rows_from(parts, start, start + MID_ROWS + 2, maps2 // 2 * 3)
     y = dot(weights, jnp.concatenate(window + [fixed], axis=0))
     for r, keep in enumerate(keeps):
-        piece = relu(y[r * maps2 : (r + 1) * maps2], keep).astype(F32)
+        piece = relu(y[r * maps2 : (r + 1) * maps2], keep)
         m3_ref[(at + r) * 3 * maps2 : (at + r + 1) * 3 * maps2, :] = jnp.concatenate(
             [shifted(piece, -1), piece, shifted(piece, 1)], axis=0
-        ).astype(BF)
+        )
 
 
 def early_middle(rows):
@@ -222,25 +227,22 @@
     return first, stop
 
 
-def inner_kernel(raw_ref, mask_ref, enc_ref, mid_ref, x_ref, perm_ref, e4_ref, p3_ref, m3_ref):
+def inner_kernel(raw_ref, mask_ref, perm_ref, enc_ref, mid_ref, x_ref, e4_ref, p3_ref, m3_ref):
     rows, length = raw_ref.shape
     half = length // 2
-    s = iota((length, half), 0)
-    t = iota((length, half), 1)
-    perm_ref[:, :half] = jnp.where(s == 2 * t, 1.0, 0.0).astype(BF)
-    perm_ref[:, half:] = jnp.where(s == 2 * t + 1, 1.0, 0.0).astype(BF)
     alive = column(mask_ref[...].astype(F32), rows)
     x = dot((raw_ref[...].astype(F32) * alive).astype(BF), perm_ref[...])
     x_ref[...] = x
-    six = sixfold(x[:, :half], x[:, half:])
+    four = fourfold(x[:, :half], x[:, half:])
     fixed = constants(half)
-    span = enc_ref.shape[0] // ENC_ROWS
-    pooled = span // 4 * 3 * ENC_ROWS // 2
+    maps = enc_ref.shape[0] // ENC_ROWS // 2
+    span = 4 * maps
+    pooled = 3 * maps * ENC_ROWS // 2
     for g in range(rows // ENC_ROWS - 1):
         top = g * ENC_ROWS
         encode(
             enc_ref[...],
-            [piece[top : top + ENC_ROWS + EDGE] for piece in six],
+            [piece[top : top + ENC_ROWS + EDGE] for piece in four],
             fixed,
             [None] * ENC_ROWS,
             e4_ref.at[top * span : (top + ENC_ROWS) * span],
@@ -258,8 +260,7 @@
 ):
     rows, length = x_ref.shape
     half = length // 2
-    span = enc_ref.shape[0] // ENC_ROWS
-    maps = span // 4
+    maps = enc_ref.shape[0] // ENC_ROWS // 2
     here = lax.axis_index("chan")
     last = lax.axis_size("chan") - 1
     odd = here % 2 == 1
@@ -285,7 +286,7 @@
             p_bottom_ref,
         ),
     ):
-        encode(enc_ref[...], sixfold(x[:, :half], x[:, half:]), fixed, keeps, e_ref, p_ref)
+        encode(enc_ref[...], fourfold(x[:, :half], x[:, half:]), fixed, keeps, e_ref, p_ref)
     p_bottom_ref[ENC_ROWS // 2 * 3 * maps :, :] = jnp.zeros(
         (p_bottom_ref.shape[0] - ENC_ROWS // 2 * 3 * maps, half), BF
     )
@@ -434,7 +435,8 @@
     store.wait()
 
 
-def other_kernel(x_ref, ta_ref, tb_ref, tf_ref, split_ref, p_ref, s_ref):
+def other_kernel(x_ref, ta_ref, tb_ref, tf_ref, split_ref, before_ref, p_ref, s_ref):
+    del before_ref
     s_ref[...] = dot(x_ref[...], split_ref[...])
 
     def put(r, i, lane, row):
@@ -541,9 +543,9 @@
         b_dec[None],
         w_out[None],
     ]
-    *loaded, send1, send2 = call(
+    *loaded, send1, send2, perm = call(
         load_kernel,
-        [(x.shape, x.dtype) for x in small] + [((EDGE, length), BF)] * 2,
+        [(x.shape, x.dtype) for x in small] + [((EDGE, length), BF)] * 2 + [((length, length), BF)],
         [pltpu.SemaphoreType.DMA((len(small),))],
         hbm=range(len(small)),
         inputs=len(small),
@@ -556,7 +558,7 @@
     enc_w, mid_w, dec_w, out_w, dec_b = call(
         prep_kernel,
         [
-            ((ENC_ROWS * 4 * maps, 6 * (ENC_ROWS + EDGE) + PAD), BF),
+            ((ENC_ROWS * 2 * maps, 4 * (ENC_ROWS + EDGE) + PAD), BF),
             ((MID_ROWS * 2 * maps, (MID_ROWS + 2) * 3 * maps + PAD), BF),
             ((DEC_ROWS * 2 * maps, dec_cols), BF),
             ((2 * OUT_ROWS, OUT_ROWS * 2 * maps), BF),
@@ -566,17 +568,16 @@
         inputs=7,
     )(*loaded[2:9])
     first, stop = early_middle(rows)
-    x, perm, e4, p3, m3 = call(
+    x, e4, p3, m3 = call(
         inner_kernel,
         [
             ((rows, length), F32),
-            ((length, length), BF),
             (((rows - ENC_ROWS) * 4 * maps, half), BF),
             (((rows - ENC_ROWS) // 2 * 3 * maps, half), BF),
             (((stop - first) * MID_ROWS * 6 * maps, half), BF),
         ],
-        inputs=4,
-    )(*loaded[:2], enc_w, mid_w)
+        inputs=5,
+    )(*loaded[:2], perm, enc_w, mid_w)
     e_top, e_bottom, m_top, m_bottom = call(
         edge_kernel,
         [
@@ -624,8 +625,8 @@
     sums = [spectra.pop()]
     for x in gathered[:-1]:
         (more,) = call(
-            other_kernel, [((tmpl, 2 * length), F32)], [pltpu.VMEM((rows, 2 * length), F32)], inputs=5
-        )(x, *spectra, split)
+            other_kernel, [((tmpl, 2 * length), F32)], [pltpu.VMEM((rows, 2 * length), F32)], inputs=6
+        )(x, *spectra, split, sums[-1])
         sums.append(more)
     keep, send = call(
         functools.partial(corr_kernel, blocks),

time: 30.5 us -> 29.5 us (0.967)
  starting transfers between devices: 13.8 us -> 12.9 us
  Pallas kernels: 8.85 us -> 8.41 us
    ppermute x3, starting transfers between devices: 7.43 us -> 6.54 us  [rotated(): return lax.ppermute(x, axes, [(i, (i + by) % count) for i in range(count)])]
    ppermute x3, waiting for transfers between devices: 0.45 us -> 1.17 us  [rotated(): return lax.ppermute(x, axes, [(i, (i + by) % count) for i in range(count)])]
    pallas_call x10, Pallas kernels: 8.85 us -> 8.41 us  [run(): inner(*[pltpu.with_memory_space_constraint(x, HBM) if i in hbm else x for...]
    ppermute x3, waiting for transfers between devices: 4.37 us -> 3.95 us  [body(): lax.ppermute(part, ('chan', 'tm'), [(i, i ^ step) for i in range(2 * chan...]
  transfers between devices with their start and end apart: 9 -> 9, of which waited for: 5 -> 5; matrix products, arithmetic and copies ran while one was open for 0% -> 0% of each run, Pallas kernels for 15% -> 14%
where the time goes in v4:
time: 29.5 us; the launch traced here: 29.3 us
  starting transfers between devices  12.9 us (44%)
  Pallas kernels  8.41 us (29%)
  waiting for transfers between devices  5.96 us (20%)
  between operations  1.41 us (5%)
  other arithmetic  0.6 us (2%)
    pallas_call x10, Pallas kernels, run(): inner(*[pltpu.with_memory_space_constraint(x, HBM) if i in hbm else x for...  8.41 us
    ppermute x3, starting transfers between devices, rotated(): return lax.ppermute(x, axes, [(i, (i + by) % count) for i in range(count)])  6.54 us
    ppermute x3, waiting for transfers between devices, body(): lax.ppermute(part, ('chan', 'tm'), [(i, i ^ step) for i in range(2 * chan...  3.95 us
    ppermute x3, starting transfers between devices, body(): lax.ppermute(part, ('chan', 'tm'), [(i, i ^ step) for i in range(2 * chan...  3.49 us
    ppermute x1, starting transfers between devices, body(): got = lax.ppermute(send, 'chan', [(i, i ^ 1) for i in range(chans)])  1.64 us
    ppermute x3, waiting for transfers between devices, rotated(): return lax.ppermute(x, axes, [(i, (i + by) % count) for i in range(count)])  1.17 us
    ppermute x1, waiting for transfers between devices, body(): got = lax.ppermute(send, 'chan', [(i, i ^ 1) for i in range(chans)])  0.84 us
    ppermute x1, starting transfers between devices, body(): r2 = lax.ppermute(send2, 'chan', links + [(b, a) for a, b in links])  0.65 us
  transfers between devices with their start and end apart: 9, of which 5 were waited for; matrix products, arithmetic and copies ran while one was open for 0% of the time, Pallas kernels for 14%

profile of v4, /device:TPU:0, one launch (start us, length us, event | category | flops | bytes accessed | tf_op | source)
XLA Modules:
  0.0 29.3 jit_solution(12819616472846787393)
XLA Ops:
  0.6 1.0 %shard_map.149 = (bf16[64,512]{1,0:T(8,128)(2,1)S(1)}, s32[1,64]{1,0:T(1,128)S(1)}, bf16[1,3,3,16]{3,2,1,0:T(4,128)(2,1)S(1)}, bf16[3,3,16,32]{3,2,1,0:T(8,128)(...) custom-call(bf16[64,512]{1,0:T(8,128)(2,1)} %refs_0_.1, ...), custom_call_target="tpu_custom_call" | custom-call | tf_op jit(solution)/shard_map/pallas_call | solution.py:510
  1.7 0.6 %collective-permute-start = (bf16[8,512]{1,0:T(8,128)(2,1)S(1)}, bf16[8,512]{1,0:T(8,128)(2,1)S(1)}, u32[]{:S(2)}, u32[]{:S(2)}) collective-permute-start(bf16[8,512]{1,0:T(8,128)(2,1)S(1)} %get-tuple-element.51), channel_id=1, source_target_pairs={{0,2},{2,0},{4,6},{6,4},{1,3},{3,1},{5,7},{7,5},{8,10},{10,8},{12,... | collective-permute-start | bytes 24584 | tf_op jit(solution)/shard_map/ppermute | solution.py:553
  2.2 0.6 %collective-permute-start.1 = (bf16[8,512]{1,0:T(8,128)(2,1)S(1)}, bf16[8,512]{1,0:T(8,128)(2,1)S(1)}, u32[]{:S(2)}, u32[]{:S(2)}) collective-permute-start(bf16[8,512]{1,0:T(8,128)(2,1)S(1)} %get-tuple-element.52), channel_id=1, source_target_pairs={{2,4},{4,2},{3,5},{5,3},{10,12},{12,10},{11,13},{13,11},{18,20},{2... | collective-permute-start | bytes 24584 | tf_op jit(solution)/shard_map/ppermute | solution.py:555
  3.5 0.5 %shard_map.150 = (bf16[256,80]{1,0:T(8,128)(2,1)S(1)}, bf16[96,256]{1,0:T(8,128)(2,1)S(1)}, bf16[128,768]{1,0:T(8,128)(2,1)S(1)}, bf16[16,256]{1,0:T(8,128)(2,1)S(1)}, f32[32,256]{1,0:T(8,128)S(1)}) custom-call(bf16[1,3,3,16]{3,2,1,0:T(4,128)(2,1)S(1)} %get-tuple-element.41.we_ref, bf16[3,3,16,32]{3,2,1,0:T(8,128)(2,1)S(1)} %get-tuple-element.42.wm_ref, ...), custom_call_target="tpu_custom_call" | custom-call | tf_op jit(solution)/shard_map/pallas_call | solution.py:510
  4.0 1.2 %shard_map.151 = (f32[64,512]{1,0:T(8,128)S(1)}, bf16[3584,256]{1,0:T(8,128)(2,1)S(1)}, bf16[1344,256]{1,0:T(8,128)(2,1)S(1)}, bf16[2304,256]{1,0:T(8,128)(2,1)S(1)}) custom-call(bf16[64,512]{1,0:T(8,128)(2,1)S(1)} %get-tuple-element.38.raw_ref, s32[1,64]{1,0:T(1,128)S(1)} %get-tuple-element.39.mask_ref, bf16[512,512]{1,0:T(8,128)(2,1)S(1)} %get-tuple-element.40.perm_ref, ...), custom_call_target="tpu_custom_call" | custom-call | tf_op jit(solution)/shard_map/pallas_call | solution.py:510
  5.2 0.8 %shard_map.152 = (bf16[512,256]{1,0:T(8,128)(2,1)S(1)}, bf16[512,256]{1,0:T(8,128)(2,1)S(1)}, bf16[576,256]{1,0:T(8,128)(2,1)S(1)}, bf16[384,256]{1,0:T(8,128)(2,1)S(1)}) custom-call(f32[64,512]{1,0:T(8,128)S(1)} %get-tuple-element.50.x_ref, bf16[512,512]{1,0:T(8,128)(2,1)S(1)} %get-tuple-element.40.perm_ref, ...), custom_call_target="tpu_custom_call" | custom-call | tf_op jit(solution)/shard_map/pallas_call | solution.py:510
  6.1 1.5 %shard_map.153.x_ref = bf16[64,512]{1,0:T(8,128)(2,1)S(1)} custom-call(f32[64,512]{1,0:T(8,128)S(1)} %get-tuple-element.50.x_ref, s32[1,64]{1,0:T(1,128)S(1)} %get-tuple-element.39.mask_ref, bf16[512,256]{1,0:T(8,128)(2,1)S(1)} %get-tuple-element.54.e_top_ref, bf16[3584,256]{1,0:T(8,128)(2,1)S(1)} %get-tuple-element.55.e4_ref, ...), custom_call_target="tpu_custom_call" | custom-call | tf_op jit(solution)/shard_map/pallas_call | solution.py:510
  7.6 2.6 %collective-permute-start.2 = (bf16[64,512]{1,0:T(8,128)(2,1)S(1)}, bf16[64,512]{1,0:T(8,128)(2,1)S(1)}, u32[]{:S(2)}, u32[]{:S(2)}) collective-permute-start(bf16[64,512]{1,0:T(8,128)(2,1)S(1)} %shard_map.153.x_ref), channel_id=1, source_target_pairs={{0,8},{8,16},{16,24},{24,0},{1,9},{9,17},{17,25},{25,1},{2,10},{10... | collective-permute-start | bytes 196616 | tf_op jit(solution)/shard_map/ppermute | solution.py:525
  10.2 2.6 %collective-permute-start.3 = (bf16[64,512]{1,0:T(8,128)(2,1)S(1)}, bf16[64,512]{1,0:T(8,128)(2,1)S(1)}, u32[]{:S(2)}, u32[]{:S(2)}) collective-permute-start(bf16[64,512]{1,0:T(8,128)(2,1)S(1)} %shard_map.153.x_ref), channel_id=1, source_target_pairs={{0,16},{8,24},{16,0},{24,8},{1,17},{9,25},{17,1},{25,9},{2,18},{10... | collective-permute-start | bytes 196616 | tf_op jit(solution)/shard_map/ppermute | solution.py:525
  12.8 1.3 %collective-permute-start.4 = (bf16[64,512]{1,0:T(8,128)(2,1)S(1)}, bf16[64,512]{1,0:T(8,128)(2,1)S(1)}, u32[]{:S(2)}, u32[]{:S(2)}) collective-permute-start(bf16[64,512]{1,0:T(8,128)(2,1)S(1)} %shard_map.153.x_ref), channel_id=1, source_target_pairs={{0,24},{8,0},{16,8},{24,16},{1,25},{9,1},{17,9},{25,17},{2,26},{10... | collective-permute-start | bytes 196616 | tf_op jit(solution)/shard_map/ppermute | solution.py:525
  14.1 1.6 %shard_map.154 = (f32[4,64,512]{2,1,0:T(8,128)S(1)}, f32[4,64,512]{2,1,0:T(8,128)S(1)}, f32[4,64,128]{2,1,0:T(8,128)S(1)}, f32[4,1024]{1,0:T(4,128)S(1)}, bf16[64,512]{1,0:T(8,128)(2,1)}) custom-call(bf16[64,512]{1,0:T(8,128)(2,1)S(1)} %shard_map.153.x_ref, bf16[4,64,512]{2,1,0:T(8,128)(2,1)S(1)} %copy-done.2, bf16[512,1024]{1,0:T(8,128)(2,1)S(1)} %copy-done.1, ...), custom_call_target="tpu_custom_call" | custom-call | tf_op jit(solution)/shard_map/pallas_call | solution.py:510
  15.8 0.5 %shard_map.155.before_ref.refs_1_ = f32[4,1024]{1,0:T(4,128)S(1)} custom-call(bf16[64,512]{1,0:T(8,128)(2,1)S(1)} %collective-permute-done.2.x_ref, f32[4,64,512]{2,1,0:T(8,128)S(1)} %get-tuple-element.65.ta_ref.refs_4_, f32[4,64,512]{2,1,0:T(8,128)S(1)} %get-tuple-element.66.tb_ref.refs_5_, f32[4,64,128]{2,1,0:T(8,128)S(1)} %get-tuple-element.67.tf_ref.refs_6_, ...), custom_call_target="tpu_custom_call" | custom-call | tf_op jit(solution)/shard_map/pallas_call | solution.py:510
  16.3 0.5 %shard_map.156.refs_2_ = f32[4,1024]{1,0:T(4,128)S(1)} custom-call(bf16[64,512]{1,0:T(8,128)(2,1)S(1)} %collective-permute-done.3.x_ref, f32[4,64,512]{2,1,0:T(8,128)S(1)} %get-tuple-element.65.ta_ref.refs_4_, f32[4,64,512]{2,1,0:T(8,128)S(1)} %get-tuple-element.66.tb_ref.refs_5_, f32[4,64,128]{2,1,0:T(8,128)S(1)} %get-tuple-element.67.tf_ref.refs_6_, ...), custom_call_target="tpu_custom_call" | custom-call | tf_op jit(solution)/shard_map/pallas_call | solution.py:510
  16.7 1.2 %collective-permute-done.4.refs_3_ = bf16[64,512]{1,0:T(8,128)(2,1)S(1)} collective-permute-done((bf16[64,512]{1,0:T(8,128)(2,1)S(1)}, bf16[64,512]{1,0:T(8,128)(2,1)S(1)}, u32[]{:S(2)}, u32[]{:S(2)}) %collective-permute-start.4) | collective-permute-done | bytes 65568 | tf_op jit(solution)/shard_map/ppermute | solution.py:525
  17.9 0.9 %shard_map.157 = (f32[4,16,128]{2,1,0:T(8,128)S(1)}, bf16[4,16,128]{2,1,0:T(8,128)(2,1)S(1)}) custom-call(f32[4,1024]{1,0:T(4,128)S(1)} %get-tuple-element.64.before_ref.refs_0_, f32[4,1024]{1,0:T(4,128)S(1)} %shard_map.155.before_ref.refs_1_, f32[4,1024]{1,0:T(4,128)S(1)} %shard_map.156.refs_2_, bf16[64,512]{1,0:T(8,128)(2,1)S(1)} %collective-permute-done.4.refs_3_, ...), custom_call_target="tpu_custom_call" | custom-call | tf_op jit(solution)/shard_map/pallas_call | solution.py:510
  18.8 1.6 %collective-permute-start.5 = (bf16[4,16,128]{2,1,0:T(8,128)(2,1)S(1)}, bf16[4,16,128]{2,1,0:T(8,128)(2,1)S(1)}, u32[]{:S(2)}, u32[]{:S(2)}) collective-permute-start(bf16[4,16,128]{2,1,0:T(8,128)(2,1)S(1)} %get-tuple-element.69), channel_id=1, source_target_pairs={{0,2},{2,0},{4,6},{6,4},{1,3},{3,1},{5,7},{7,5},{8,10},{10,8},{12,... | collective-permute-start | bytes 49160 | tf_op jit(solution)/shard_map/ppermute | solution.py:641
  20.4 0.8 %collective-permute-done.5.got_ref = bf16[4,16,128]{2,1,0:T(8,128)(2,1)S(1)} collective-permute-done((bf16[4,16,128]{2,1,0:T(8,128)(2,1)S(1)}, bf16[4,16,128]{2,1,0:T(8,128)(2,1)S(1)}, u32[]{:S(2)}, u32[]{:S(2)}) %collective-permute-start.5) | collective-permute-done | bytes 16416 | tf_op jit(solution)/shard_map/ppermute | solution.py:641
  21.2 1.5 %collective-permute-start.6 = (bf16[16,128]{1,0:T(8,128)(2,1)S(1)}, bf16[16,128]{1,0:T(8,128)(2,1)S(1)}, u32[]{:S(2)}, u32[]{:S(2)}) collective-permute-start(bf16[16,128]{1,0:T(8,128)(2,1)S(1)} %get-tuple-element.71), channel_id=1, source_target_pairs={{0,1},{1,0},{2,3},{3,2},{4,5},{5,4},{6,7},{7,6},{8,9},{9,8},{10,11... | collective-permute-start | bytes 12296 | tf_op jit(solution)/shard_map/ppermute | solution.py:647
  22.7 1.4 %collective-permute-start.7 = (bf16[16,128]{1,0:T(8,128)(2,1)S(1)}, bf16[16,128]{1,0:T(8,128)(2,1)S(1)}, u32[]{:S(2)}, u32[]{:S(2)}) collective-permute-start(bf16[16,128]{1,0:T(8,128)(2,1)S(1)} %get-tuple-element.72), channel_id=1, source_target_pairs={{0,4},{1,5},{2,6},{3,7},{4,0},{5,1},{6,2},{7,3},{8,12},{9,13},{10,... | collective-permute-start | bytes 12296 | tf_op jit(solution)/shard_map/ppermute | solution.py:647
  24.2 0.6 %collective-permute-start.8 = (bf16[16,128]{1,0:T(8,128)(2,1)S(1)}, bf16[16,128]{1,0:T(8,128)(2,1)S(1)}, u32[]{:S(2)}, u32[]{:S(2)}) collective-permute-start(bf16[16,128]{1,0:T(8,128)(2,1)S(1)} %get-tuple-element.73), channel_id=1, source_target_pairs={{0,5},{1,4},{2,7},{3,6},{4,1},{5,0},{6,3},{7,2},{8,13},{9,12},{10,... | collective-permute-start | bytes 12296 | tf_op jit(solution)/shard_map/ppermute | solution.py:647
  24.7 0.1 collective-permute-done.6
  24.8 1.5 %collective-permute-done.7 = bf16[16,128]{1,0:T(8,128)(2,1)S(1)} collective-permute-done((bf16[16,128]{1,0:T(8,128)(2,1)S(1)}, bf16[16,128]{1,0:T(8,128)(2,1)S(1)}, u32[]{:S(2)}, u32[]{:S(2)}) %collective-permute-start.7) | collective-permute-done | bytes 4128 | tf_op jit(solution)/shard_map/ppermute | solution.py:647
  26.3 2.3 %collective-permute-done.8 = bf16[16,128]{1,0:T(8,128)(2,1)S(1)} collective-permute-done((bf16[16,128]{1,0:T(8,128)(2,1)S(1)}, bf16[16,128]{1,0:T(8,128)(2,1)S(1)}, u32[]{:S(2)}, u32[]{:S(2)}) %collective-permute-start.8) | collective-permute-done | bytes 4128 | tf_op jit(solution)/shard_map/ppermute | solution.py:647
  28.7 0.6 %convert_add_fusion = f32[16,128]{1,0:T(8,128)} fusion(bf16[16,128]{1,0:T(8,128)(2,1)S(1)} %collective-permute-done.8, bf16[16,128]{1,0:T(8,128)(2,1)S(1)} %collective-permute-done.7, f32[16,128]{1,0:T(8,128)S(1)} %get-tuple-element.70, bf16[16,128]{1,0:T(8,128)(2,1)S(1)} %collective-permute-done.6), kind=kLoop, calls=%fused_computation | loop fusion | flops 12288 | bytes 28672 | tf_op jit(solution)/shard_map/add | solution.py:648
  (11 shorter events, 0.0 us)
Async XLA Ops:
  1.7 3.5 %collective-permute-start = (bf16[8,512]{1,0:T(8,128)(2,1)S(1)}, bf16[8,512]{1,0:T(8,128)(2,1)S(1)}, u32[]{:S(2)}, u32[]{:S(2)}) collective-permute-start(bf16[8,512]{1,0:T(8,128)(2,1)S(1)} %get-tuple-element.51), channel_id=1, source_target_pairs={{0,2},{2,0},{4,6},{6,4},{1,3},{3,1},{5,7},{7,5},{8,10},{10,8},{12,... | collective-permute-start | bytes 24584 | tf_op jit(solution)/shard_map/ppermute | solution.py:553
  2.2 3.0 %collective-permute-start.1 = (bf16[8,512]{1,0:T(8,128)(2,1)S(1)}, bf16[8,512]{1,0:T(8,128)(2,1)S(1)}, u32[]{:S(2)}, u32[]{:S(2)}) collective-permute-start(bf16[8,512]{1,0:T(8,128)(2,1)S(1)} %get-tuple-element.52), channel_id=1, source_target_pairs={{2,4},{4,2},{3,5},{5,3},{10,12},{12,10},{11,13},{13,11},{18,20},{2... | collective-permute-start | bytes 24584 | tf_op jit(solution)/shard_map/ppermute | solution.py:555
  6.1 8.1 %copy-start = (bf16[512,1024]{1,0:T(8,128)(2,1)S(1)}, bf16[512,1024]{1,0:T(8,128)(2,1)}, u32[]{:S(2)}) copy-start(bf16[512,1024]{1,0:T(8,128)(2,1)} %constant.5.clone.split_ref.refs_8_) | copy-start | bytes 3145732
  6.1 8.0 %copy-start.1 = (bf16[512,1024]{1,0:T(8,128)(2,1)S(1)}, bf16[512,1024]{1,0:T(8,128)(2,1)}, u32[]{:S(2)}) copy-start(bf16[512,1024]{1,0:T(8,128)(2,1)} %constant.4.clone.table_ref.refs_7_) | copy-start | bytes 3145732
  6.1 8.0 %copy-start.2 = (bf16[4,64,512]{2,1,0:T(8,128)(2,1)S(1)}, bf16[4,64,512]{2,1,0:T(8,128)(2,1)}, u32[]{:S(2)}) copy-start(bf16[4,64,512]{2,1,0:T(8,128)(2,1)} %t_ref.1) | copy-start | bytes 786436
  7.6 8.2 %collective-permute-start.2 = (bf16[64,512]{1,0:T(8,128)(2,1)S(1)}, bf16[64,512]{1,0:T(8,128)(2,1)S(1)}, u32[]{:S(2)}, u32[]{:S(2)}) collective-permute-start(bf16[64,512]{1,0:T(8,128)(2,1)S(1)} %shard_map.153.x_ref), channel_id=1, source_target_pairs={{0,8},{8,16},{16,24},{24,0},{1,9},{9,17},{17,25},{25,1},{2,10},{10... | collective-permute-start | bytes 196616 | tf_op jit(solution)/shard_map/ppermute | solution.py:525
  10.2 6.1 %collective-permute-start.3 = (bf16[64,512]{1,0:T(8,128)(2,1)S(1)}, bf16[64,512]{1,0:T(8,128)(2,1)S(1)}, u32[]{:S(2)}, u32[]{:S(2)}) collective-permute-start(bf16[64,512]{1,0:T(8,128)(2,1)S(1)} %shard_map.153.x_ref), channel_id=1, source_target_pairs={{0,16},{8,24},{16,0},{24,8},{1,17},{9,25},{17,1},{25,9},{2,18},{10... | collective-permute-start | bytes 196616 | tf_op jit(solution)/shard_map/ppermute | solution.py:525
  12.8 5.1 %collective-permute-start.4 = (bf16[64,512]{1,0:T(8,128)(2,1)S(1)}, bf16[64,512]{1,0:T(8,128)(2,1)S(1)}, u32[]{:S(2)}, u32[]{:S(2)}) collective-permute-start(bf16[64,512]{1,0:T(8,128)(2,1)S(1)} %shard_map.153.x_ref), channel_id=1, source_target_pairs={{0,24},{8,0},{16,8},{24,16},{1,25},{9,1},{17,9},{25,17},{2,26},{10... | collective-permute-start | bytes 196616 | tf_op jit(solution)/shard_map/ppermute | solution.py:525
  18.8 2.5 %collective-permute-start.5 = (bf16[4,16,128]{2,1,0:T(8,128)(2,1)S(1)}, bf16[4,16,128]{2,1,0:T(8,128)(2,1)S(1)}, u32[]{:S(2)}, u32[]{:S(2)}) collective-permute-start(bf16[4,16,128]{2,1,0:T(8,128)(2,1)S(1)} %get-tuple-element.69), channel_id=1, source_target_pairs={{0,2},{2,0},{4,6},{6,4},{1,3},{3,1},{5,7},{7,5},{8,10},{10,8},{12,... | collective-permute-start | bytes 49160 | tf_op jit(solution)/shard_map/ppermute | solution.py:641
  21.2 3.6 %collective-permute-start.6 = (bf16[16,128]{1,0:T(8,128)(2,1)S(1)}, bf16[16,128]{1,0:T(8,128)(2,1)S(1)}, u32[]{:S(2)}, u32[]{:S(2)}) collective-permute-start(bf16[16,128]{1,0:T(8,128)(2,1)S(1)} %get-tuple-element.71), channel_id=1, source_target_pairs={{0,1},{1,0},{2,3},{3,2},{4,5},{5,4},{6,7},{7,6},{8,9},{9,8},{10,11... | collective-permute-start | bytes 12296 | tf_op jit(solution)/shard_map/ppermute | solution.py:647
  22.7 3.6 %collective-permute-start.7 = (bf16[16,128]{1,0:T(8,128)(2,1)S(1)}, bf16[16,128]{1,0:T(8,128)(2,1)S(1)}, u32[]{:S(2)}, u32[]{:S(2)}) collective-permute-start(bf16[16,128]{1,0:T(8,128)(2,1)S(1)} %get-tuple-element.72), channel_id=1, source_target_pairs={{0,4},{1,5},{2,6},{3,7},{4,0},{5,1},{6,2},{7,3},{8,12},{9,13},{10,... | collective-permute-start | bytes 12296 | tf_op jit(solution)/shard_map/ppermute | solution.py:647
  24.2 4.5 %collective-permute-start.8 = (bf16[16,128]{1,0:T(8,128)(2,1)S(1)}, bf16[16,128]{1,0:T(8,128)(2,1)S(1)}, u32[]{:S(2)}, u32[]{:S(2)}) collective-permute-start(bf16[16,128]{1,0:T(8,128)(2,1)S(1)} %get-tuple-element.73), channel_id=1, source_target_pairs={{0,5},{1,4},{2,7},{3,6},{4,1},{5,0},{6,3},{7,2},{8,13},{9,12},{10,... | collective-permute-start | bytes 12296 | tf_op jit(solution)/shard_map/ppermute | solution.py:647

commit v5 on v4

--- a/solution.py
+++ b/solution.py
@@ -94,7 +94,7 @@
 ):
     maps = we_ref.shape[3]
     span = 2 * maps
-    width = -(-enc_ref.shape[1] // 128) * 128
+    width = enc_ref.shape[1]
     window = ENC_ROWS + EDGE
     spread = jnp.where(iota((span, maps), 0) % maps == iota((span, maps), 1), 1.0, 0.0).astype(BF)
     we = jnp.concatenate([we_ref[0, y].astype(F32) for y in range(3)], axis=0).astype(BF)
@@ -113,7 +113,7 @@
         fixed = jnp.where(at == t, part, fixed)
     for r in range(ENC_ROWS):
         row = (pltpu.roll(band, r, 1) if r else band) + fixed
-        enc_ref[r * span : (r + 1) * span, :] = row[:, : enc_ref.shape[1]].astype(BF)
+        enc_ref[r * span : (r + 1) * span, :] = row.astype(BF)
     rows, cols = mid_ref.shape
     wide_ref[:rows, :cols] = jnp.zeros((rows, cols), F32)
     wm = wm_ref[...].astype(F32).reshape(9 * maps, 2 * maps).T
@@ -183,7 +183,10 @@
 
 def encode(weights, pieces, fixed, keeps, e4_ref, p3_ref):
     window = jnp.concatenate([jnp.concatenate(pieces, axis=0).astype(BF), fixed], axis=0)
-    y = dot(weights, window)
+    keep_encoded(dot(weights[:, : window.shape[0]], window), keeps, e4_ref, p3_ref)
+
+
+def keep_encoded(y, keeps, e4_ref, p3_ref):
     span = y.shape[0] // ENC_ROWS
     maps = span // 2
     both = []
@@ -212,7 +215,11 @@
 def narrow(weights, parts, fixed, start, keeps, m3_ref, at):
     maps2 = weights.shape[0] // MID_ROWS
     window = rows_from(parts, start, start + MID_ROWS + 2, maps2 // 2 * 3)
-    y = dot(weights, jnp.concatenate(window + [fixed], axis=0))
+    keep_middle(dot(weights, jnp.concatenate(window + [fixed], axis=0)), keeps, m3_ref, at)
+
+
+def keep_middle(y, keeps, m3_ref, at):
+    maps2 = y.shape[0] // MID_ROWS
     for r, keep in enumerate(keeps):
         piece = relu(y[r * maps2 : (r + 1) * maps2], keep)
         m3_ref[(at + r) * 3 * maps2 : (at + r + 1) * 3 * maps2, :] = jnp.concatenate(
@@ -254,68 +261,26 @@
         narrow(mid_ref[...], parts, fixed, g * MID_ROWS, [None] * MID_ROWS, m3_ref, (g - first) * MID_ROWS)
 
 
-def edge_kernel(
-    x_ref, perm_ref, r1_ref, r2_ref, p3_ref, enc_ref, mid_ref,
-    e_top_ref, e_bottom_ref, m_top_ref, m_bottom_ref, p_top_ref, p_bottom_ref,
+def rest_kernel(
+    x_ref, mask_ref, perm_ref, r1_ref, r2_ref, e4_ref, p3_ref, m_ref,
+    enc_ref, mid_ref, dec_ref, wout_ref, bdec_ref, bout_ref,
+    out_ref, e_top_ref, e_bottom_ref, p_top_ref, p_bottom_ref, m_top_ref, m_bottom_ref,
 ):
     rows, length = x_ref.shape
     half = length // 2
-    maps = enc_ref.shape[0] // ENC_ROWS // 2
+    maps2 = bdec_ref.shape[0]
+    span = maps2 * 2
+    span_m = maps2 * 3
+    total = rows // 2 + 2
+    first, stop = early_middle(rows)
+    few = ENC_ROWS // 2
     here = lax.axis_index("chan")
     last = lax.axis_size("chan") - 1
     odd = here % 2 == 1
     keep_top = jnp.where(here == 0, 0.0, 1.0)
     keep_bottom = jnp.where(here == last, 0.0, 1.0)
-    r1 = r1_ref[...].astype(F32)
-    r2 = r2_ref[...].astype(F32)
-    edges = jnp.concatenate([jnp.where(odd, r1, r2), jnp.where(odd, r2, r1)], axis=0).astype(BF)
-    edges = dot(edges, perm_ref[...])
-    fixed = constants(half)
-    margin = EDGE // 2
-    for x, keeps, e_ref, p_ref in (
-        (
-            jnp.concatenate([edges[:EDGE], x_ref[:ENC_ROWS]], axis=0),
-            [keep_top] * margin + [None] * (ENC_ROWS - margin),
-            e_top_ref,
-            p_top_ref,
-        ),
-        (
-            jnp.concatenate([x_ref[rows - ENC_ROWS :], edges[EDGE:]], axis=0),
-            [None] * (ENC_ROWS - margin) + [keep_bottom] * margin,
-            e_bottom_ref,
-            p_bottom_ref,
-        ),
-    ):
-        encode(enc_ref[...], fourfold(x[:, :half], x[:, half:]), fixed, keeps, e_ref, p_ref)
-    p_bottom_ref[ENC_ROWS // 2 * 3 * maps :, :] = jnp.zeros(
-        (p_bottom_ref.shape[0] - ENC_ROWS // 2 * 3 * maps, half), BF
-    )
-    few = ENC_ROWS // 2
+    e4 = [(0, ENC_ROWS, e_top_ref), (ENC_ROWS, rows, e4_ref), (rows, rows + EDGE, e_bottom_ref)]
     p3 = [(0, few, p_top_ref), (few, rows // 2, p3_ref), (rows // 2, rows // 2 + few + MID_ROWS, p_bottom_ref)]
-    total = rows // 2 + 2
-    first, stop = early_middle(rows)
-    keeps = [keep_top] + [None] * (total - 2) + [keep_bottom]
-    for g in range(-(-total // MID_ROWS)):
-        start = g * MID_ROWS
-        if g < first:
-            narrow(mid_ref[...], p3, fixed, start, keeps[start : start + MID_ROWS], m_top_ref, start)
-        elif g >= stop:
-            narrow(
-                mid_ref[...], p3, fixed, start, keeps[start : start + MID_ROWS], m_bottom_ref, start - stop * MID_ROWS
-            )
-
-
-def decode_kernel(
-    x_ref, mask_ref, e_top_ref, e4_ref, e_bottom_ref, m_top_ref, m_ref, m_bottom_ref, dec_ref, wout_ref, bdec_ref, bout_ref,
-    out_ref,
-):
-    rows, length = x_ref.shape
-    half = length // 2
-    span = bdec_ref.shape[0] * 2
-    span_m = bdec_ref.shape[0] * 3
-    total = rows // 2 + 2
-    first, stop = early_middle(rows)
-    e4 = [(0, ENC_ROWS, e_top_ref), (ENC_ROWS, rows, e4_ref), (rows, rows + EDGE, e_bottom_ref)]
     m3 = [
         (0, first * MID_ROWS, m_top_ref),
         (first * MID_ROWS, stop * MID_ROWS, m_ref),
@@ -323,16 +288,21 @@
     ]
     alive = column(mask_ref[...].astype(F32), rows)
     bias = jnp.concatenate([bdec_ref[...]] * DEC_ROWS, axis=0)
+    fixed = constants(half)
     depth = half
     steps = dec_ref.shape[1] // depth
     units = OUT_ROWS // DEC_ROWS
-    tiles = DEC_ROWS * bdec_ref.shape[0] * units // depth
+    tiles = DEC_ROWS * maps2 * units // depth
+    p_bottom_ref[few * 3 * maps2 // 2 :, :] = jnp.zeros((p_bottom_ref.shape[0] - few * 3 * maps2 // 2, half), BF)
+
+    sides = range(first), range(stop, -(-total // MID_ROWS))
 
     def finish(*accs):
         sums = [accs[:units], accs[units : 2 * units]]
-        outs = accs[2 * units :]
+        outs = accs[2 * units : 3 * units]
+        edges = accs[3 * units : 4 * units]
+        mids = accs[4 * units : 4 * units + len(sides[0])], accs[4 * units + len(sides[0]) :]
         turn = [0] * units
-        waiting = None
 
         def push(tile, unit):
             slot = turn[unit] % 2
@@ -340,8 +310,8 @@
             pltpu.matmul_push_rhs(tile, slot, unit)
             return slot
 
-        def project(item):
-            top, decoded = item
+        def project(top, now):
+            decoded = jnp.concatenate([relu(pltpu.matmul_pop(acc) + bias) for acc in now], axis=0)
             unit = top // OUT_ROWS % units
             for k in range(tiles):
                 slot = push(decoded[k * depth : (k + 1) * depth], unit)
@@ -354,7 +324,7 @@
                     alive[top : top + OUT_ROWS] * value
                 ).astype(BF)
 
-        for top in range(0, rows, OUT_ROWS):
+        def decode(top, now):
             windows = []
             for start in range(top, top + OUT_ROWS, DEC_ROWS):
                 low = start + EDGE // 2 - 1
@@ -365,20 +335,90 @@
                         axis=0,
                     )
                 )
-            now = sums[top // OUT_ROWS % 2]
             for k in range(steps):
                 slots = [push(w[k * depth : (k + 1) * depth], unit) for unit, w in enumerate(windows)]
                 for acc, slot in zip(now, slots):
                     pltpu.matmul_acc_lhs(acc, dec_ref[:, k * depth : (k + 1) * depth], load_staged_rhs=slot)
+
+        def split():
+            r1 = r1_ref[...].astype(F32)
+            r2 = r2_ref[...].astype(F32)
+            lhs = jnp.concatenate([jnp.where(odd, r1, r2), jnp.where(odd, r2, r1)], axis=0).astype(BF)
+            for k in range(length // depth):
+                for unit in range(2):
+                    slot = push(perm_ref[k * depth : (k + 1) * depth, unit * half : (unit + 1) * half], unit)
+                    pltpu.matmul_acc_lhs(outs[unit], lhs[:, k * depth : (k + 1) * depth], load_staged_rhs=slot)
+
+        def encode_edges():
+            even, uneven = (pltpu.matmul_pop(outs[unit]) for unit in range(2))
+            for unit in range(2):
+                pair = []
+                for q, part in enumerate((even, uneven)):
+                    lanes = slice(q * half, (q + 1) * half)
+                    if unit == 0:
+                        pair.append(jnp.concatenate([part[:EDGE], x_ref[:ENC_ROWS, lanes]], axis=0))
+                    else:
+                        pair.append(jnp.concatenate([x_ref[rows - ENC_ROWS :, lanes], part[EDGE:]], axis=0))
+                window = [jnp.concatenate(fourfold(*pair), axis=0).astype(BF), fixed]
+                blank = depth - sum(w.shape[0] for w in window)
+                window = jnp.concatenate(window + [jnp.zeros((blank, half), BF)], axis=0)
+                slot = push(window, unit)
+                pltpu.matmul_acc_lhs(edges[unit], enc_ref[...], load_staged_rhs=slot)
+
+        def middle_edges():
+            margin = EDGE // 2
+            free = [None] * (ENC_ROWS - margin)
+            keep_encoded(pltpu.matmul_pop(edges[0]), [keep_top] * margin + free, e_top_ref, p_top_ref)
+            keep_encoded(pltpu.matmul_pop(edges[1]), free + [keep_bottom] * margin, e_bottom_ref, p_bottom_ref)
+            for unit, groups in enumerate(sides):
+                for i, g in enumerate(groups):
+                    window = rows_from(p3, g * MID_ROWS, (g + 1) * MID_ROWS + 2, maps2 // 2 * 3)
+                    slot = push(jnp.concatenate(window + [fixed], axis=0), unit)
+                    pltpu.matmul_acc_lhs(mids[unit][i], mid_ref[...], load_staged_rhs=slot)
+
+        def finish_edges():
+            keeps = [keep_top] + [None] * (total - 2) + [keep_bottom]
+            for unit, groups in enumerate(sides):
+                for i, g in enumerate(groups):
+                    y = pltpu.matmul_pop(mids[unit][i])
+                    start = g * MID_ROWS
+                    keep_middle(
+                        y,
+                        keeps[start : start + MID_ROWS],
+                        m_bottom_ref if unit else m_top_ref,
+                        start - (stop * MID_ROWS if unit else 0),
+                    )
+
+        tops = list(range(0, rows, OUT_ROWS))
+        inside = [
+            t
+            for t in tops
+            if t + EDGE // 2 - 1 >= ENC_ROWS
+            and t + OUT_ROWS + EDGE // 2 + 1 <= rows
+            and t // 2 >= first * MID_ROWS
+            and t // 2 + OUT_ROWS // 2 + 2 <= stop * MID_ROWS
+        ]
+        between = [split, encode_edges, middle_edges, finish_edges]
+        waiting = None
+        for turn_of, top in enumerate(inside + [t for t in tops if t not in inside]):
+            now = sums[turn_of % 2]
+            if top not in inside:
+                while between:
+                    between.pop(0)()
+            if between:
+                between.pop(0)()
+            decode(top, now)
             if waiting:
-                project(waiting)
-            waiting = top, jnp.concatenate([relu(pltpu.matmul_pop(acc) + bias) for acc in now], axis=0)
-        project(waiting)
+                project(*waiting)
+            waiting = top, now
+        project(*waiting)
 
     pl.run_scoped(
         finish,
         *(pltpu.ACC(unit)((dec_ref.shape[0], half), F32) for _ in range(2) for unit in range(units)),
         *(pltpu.ACC(unit)((wout_ref.shape[0], half), F32) for unit in range(units)),
+        *(pltpu.ACC(unit)((enc_ref.shape[0], half), F32) for unit in range(units)),
+        *(pltpu.ACC(unit)((mid_ref.shape[0], half), F32) for unit in range(units) for _ in sides[unit]),
     )
 
 
@@ -558,7 +598,7 @@
     enc_w, mid_w, dec_w, out_w, dec_b = call(
         prep_kernel,
         [
-            ((ENC_ROWS * 2 * maps, 4 * (ENC_ROWS + EDGE) + PAD), BF),
+            ((ENC_ROWS * 2 * maps, half), BF),
             ((MID_ROWS * 2 * maps, (MID_ROWS + 2) * 3 * maps + PAD), BF),
             ((DEC_ROWS * 2 * maps, dec_cols), BF),
             ((2 * OUT_ROWS, OUT_ROWS * 2 * maps), BF),
@@ -578,23 +618,20 @@
         ],
         inputs=5,
     )(*loaded[:2], perm, enc_w, mid_w)
-    e_top, e_bottom, m_top, m_bottom = call(
-        edge_kernel,
+    (denoised,) = call(
+        rest_kernel,
+        [((rows, length), BF)],
         [
-            ((ENC_ROWS * 4 * maps, half), BF),
-            ((ENC_ROWS * 4 * maps, half), BF),
-            ((first * MID_ROWS * 6 * maps, half), BF),
-            (((rows // 2 + 2 - stop * MID_ROWS) * 6 * maps, half), BF),
-        ],
-        [
+            pltpu.VMEM((ENC_ROWS * 4 * maps, half), BF),
+            pltpu.VMEM((ENC_ROWS * 4 * maps, half), BF),
             pltpu.VMEM((ENC_ROWS // 2 * 3 * maps, half), BF),
             pltpu.VMEM(((ENC_ROWS // 2 + MID_ROWS) * 3 * maps, half), BF),
+            pltpu.VMEM((first * MID_ROWS * 6 * maps, half), BF),
+            pltpu.VMEM(((rows // 2 + 2 - stop * MID_ROWS) * 6 * maps, half), BF),
         ],
-        inputs=7,
-    )(x, perm, r1, r2, p3, enc_w, mid_w)
-    (denoised,) = call(
-        decode_kernel, [((rows, length), BF)], smem=(11,), inputs=12
-    )(x, loaded[1], e_top, e4, e_bottom, m_top, m3, m_bottom, dec_w, out_w, dec_b, b_out)
+        smem=(13,),
+        inputs=14,
+    )(x, loaded[1], perm, r1, r2, e4, p3, m3, enc_w, mid_w, dec_w, out_w, dec_b, b_out)
 
     forward = jnp.asarray(forward_table(length))
     split = jnp.asarray(forward_table(length)[split_order(length)])

time: 29.5 us -> 29.2 us (0.990)
    pallas_call x10 -> x9, Pallas kernels: 8.41 us -> 8.12 us  [run(): inner(*[pltpu.with_memory_space_constraint(x, HBM) if i in hbm else x for...]
  transfers between devices with their start and end apart: 9 -> 9, of which waited for: 5 -> 5; matrix products, arithmetic and copies ran while one was open for 0% -> 0% of each run, Pallas kernels for 14% -> 15%
where the time goes in v5:
time: 29.2 us; the launch traced here: 29 us
  starting transfers between devices  12.8 us (44%)
  Pallas kernels  8.12 us (28%)
  waiting for transfers between devices  6.03 us (21%)
  between operations  1.4 us (5%)
  other arithmetic  0.6 us (2%)
    pallas_call x9, Pallas kernels, run(): inner(*[pltpu.with_memory_space_constraint(x, HBM) if i in hbm else x for...  8.12 us
    ppermute x3, starting transfers between devices, rotated(): return lax.ppermute(x, axes, [(i, (i + by) % count) for i in range(count)])  6.52 us
    ppermute x3, waiting for transfers between devices, body(): lax.ppermute(part, ('chan', 'tm'), [(i, i ^ step) for i in range(2 * chan...  3.97 us
    ppermute x3, starting transfers between devices, body(): lax.ppermute(part, ('chan', 'tm'), [(i, i ^ step) for i in range(2 * chan...  3.49 us
    ppermute x1, starting transfers between devices, body(): got = lax.ppermute(send, 'chan', [(i, i ^ 1) for i in range(chans)])  1.6 us
    ppermute x3, waiting for transfers between devices, rotated(): return lax.ppermute(x, axes, [(i, (i + by) % count) for i in range(count)])  1.22 us
    ppermute x1, waiting for transfers between devices, body(): got = lax.ppermute(send, 'chan', [(i, i ^ 1) for i in range(chans)])  0.84 us
    ppermute x1, starting transfers between devices, body(): r2 = lax.ppermute(send2, 'chan', links + [(b, a) for a, b in links])  0.65 us
  transfers between devices with their start and end apart: 9, of which 5 were waited for; matrix products, arithmetic and copies ran while one was open for 0% of the time, Pallas kernels for 15%

profile of v5, /device:TPU:0, one launch (start us, length us, event | category | flops | bytes accessed | tf_op | source)
XLA Modules:
  0.0 29.0 jit_solution(17456880156958443349)
XLA Ops:
  0.6 1.0 %shard_map.149 = (bf16[64,512]{1,0:T(8,128)(2,1)S(1)}, s32[1,64]{1,0:T(1,128)S(1)}, bf16[1,3,3,16]{3,2,1,0:T(4,128)(2,1)S(1)}, bf16[3,3,16,32]{3,2,1,0:T(8,128)(...) custom-call(bf16[64,512]{1,0:T(8,128)(2,1)} %refs_0_.1, ...), custom_call_target="tpu_custom_call" | custom-call | tf_op jit(solution)/shard_map/pallas_call | solution.py:550
  1.7 0.6 %collective-permute-start = (bf16[8,512]{1,0:T(8,128)(2,1)S(1)}, bf16[8,512]{1,0:T(8,128)(2,1)S(1)}, u32[]{:S(2)}, u32[]{:S(2)}) collective-permute-start(bf16[8,512]{1,0:T(8,128)(2,1)S(1)} %get-tuple-element.47), channel_id=1, source_target_pairs={{0,2},{2,0},{4,6},{6,4},{1,3},{3,1},{5,7},{7,5},{8,10},{10,8},{12,... | collective-permute-start | bytes 24584 | tf_op jit(solution)/shard_map/ppermute | solution.py:593
  2.2 0.6 %collective-permute-start.1 = (bf16[8,512]{1,0:T(8,128)(2,1)S(1)}, bf16[8,512]{1,0:T(8,128)(2,1)S(1)}, u32[]{:S(2)}, u32[]{:S(2)}) collective-permute-start(bf16[8,512]{1,0:T(8,128)(2,1)S(1)} %get-tuple-element.48), channel_id=1, source_target_pairs={{2,4},{4,2},{3,5},{5,3},{10,12},{12,10},{11,13},{13,11},{18,20},{2... | collective-permute-start | bytes 24584 | tf_op jit(solution)/shard_map/ppermute | solution.py:595
  3.5 0.6 %shard_map.150 = (bf16[256,256]{1,0:T(8,128)(2,1)S(1)}, bf16[96,256]{1,0:T(8,128)(2,1)S(1)}, bf16[128,768]{1,0:T(8,128)(2,1)S(1)}, bf16[16,256]{1,0:T(8,128)(2,1)S(1)}, f32[32,256]{1,0:T(8,128)S(1)}) custom-call(bf16[1,3,3,16]{3,2,1,0:T(4,128)(2,1)S(1)} %get-tuple-element.37.we_ref, bf16[3,3,16,32]{3,2,1,0:T(8,128)(2,1)S(1)} %get-tuple-element.38.wm_ref, ...), custom_call_target="tpu_custom_call" | custom-call | tf_op jit(solution)/shard_map/pallas_call | solution.py:550
  4.1 1.2 %shard_map.151 = (f32[64,512]{1,0:T(8,128)S(1)}, bf16[3584,256]{1,0:T(8,128)(2,1)S(1)}, bf16[1344,256]{1,0:T(8,128)(2,1)S(1)}, bf16[2304,256]{1,0:T(8,128)(2,1)S(1)}) custom-call(bf16[64,512]{1,0:T(8,128)(2,1)S(1)} %get-tuple-element.34.raw_ref, s32[1,64]{1,0:T(1,128)S(1)} %get-tuple-element.35.mask_ref, bf16[512,512]{1,0:T(8,128)(2,1)S(1)} %get-tuple-element.36.perm_ref, ...), custom_call_target="tpu_custom_call" | custom-call | tf_op jit(solution)/shard_map/pallas_call | solution.py:550
  5.3 0.0 copy-start
  5.4 2.0 %shard_map.152.x_ref = bf16[64,512]{1,0:T(8,128)(2,1)S(1)} custom-call(f32[64,512]{1,0:T(8,128)S(1)} %get-tuple-element.46.x_ref, s32[1,64]{1,0:T(1,128)S(1)} %get-tuple-element.35.mask_ref, bf16[512,512]{1,0:T(8,128)(2,1)S(1)} %get-tuple-element.36.perm_ref, bf16[8,512]{1,0:T(8,128)(2,1)S(1)} %collective-permute-done.r1_ref, ...), custom_call_target="tpu_custom_call" | custom-call | tf_op jit(solution)/shard_map/pallas_call | solution.py:550
  7.3 2.6 %collective-permute-start.2 = (bf16[64,512]{1,0:T(8,128)(2,1)S(1)}, bf16[64,512]{1,0:T(8,128)(2,1)S(1)}, u32[]{:S(2)}, u32[]{:S(2)}) collective-permute-start(bf16[64,512]{1,0:T(8,128)(2,1)S(1)} %shard_map.152.x_ref), channel_id=1, source_target_pairs={{0,8},{8,16},{16,24},{24,0},{1,9},{9,17},{17,25},{25,1},{2,10},{10... | collective-permute-start | bytes 196616 | tf_op jit(solution)/shard_map/ppermute | solution.py:565
  9.9 2.6 %collective-permute-start.3 = (bf16[64,512]{1,0:T(8,128)(2,1)S(1)}, bf16[64,512]{1,0:T(8,128)(2,1)S(1)}, u32[]{:S(2)}, u32[]{:S(2)}) collective-permute-start(bf16[64,512]{1,0:T(8,128)(2,1)S(1)} %shard_map.152.x_ref), channel_id=1, source_target_pairs={{0,16},{8,24},{16,0},{24,8},{1,17},{9,25},{17,1},{25,9},{2,18},{10... | collective-permute-start | bytes 196616 | tf_op jit(solution)/shard_map/ppermute | solution.py:565
  12.5 1.3 %collective-permute-start.4 = (bf16[64,512]{1,0:T(8,128)(2,1)S(1)}, bf16[64,512]{1,0:T(8,128)(2,1)S(1)}, u32[]{:S(2)}, u32[]{:S(2)}) collective-permute-start(bf16[64,512]{1,0:T(8,128)(2,1)S(1)} %shard_map.152.x_ref), channel_id=1, source_target_pairs={{0,24},{8,0},{16,8},{24,16},{1,25},{9,1},{17,9},{25,17},{2,26},{10... | collective-permute-start | bytes 196616 | tf_op jit(solution)/shard_map/ppermute | solution.py:565
  13.9 1.6 %shard_map.153 = (f32[4,64,512]{2,1,0:T(8,128)S(1)}, f32[4,64,512]{2,1,0:T(8,128)S(1)}, f32[4,64,128]{2,1,0:T(8,128)S(1)}, f32[4,1024]{1,0:T(4,128)S(1)}, bf16[64,512]{1,0:T(8,128)(2,1)}) custom-call(bf16[64,512]{1,0:T(8,128)(2,1)S(1)} %shard_map.152.x_ref, bf16[4,64,512]{2,1,0:T(8,128)(2,1)S(1)} %copy-done.2, bf16[512,1024]{1,0:T(8,128)(2,1)S(1)} %copy-done.1, ...), custom_call_target="tpu_custom_call" | custom-call | tf_op jit(solution)/shard_map/pallas_call | solution.py:550
  15.5 0.4 %shard_map.154.before_ref.refs_1_ = f32[4,1024]{1,0:T(4,128)S(1)} custom-call(bf16[64,512]{1,0:T(8,128)(2,1)S(1)} %collective-permute-done.2.x_ref, f32[4,64,512]{2,1,0:T(8,128)S(1)} %get-tuple-element.57.ta_ref.refs_4_, f32[4,64,512]{2,1,0:T(8,128)S(1)} %get-tuple-element.58.tb_ref.refs_5_, f32[4,64,128]{2,1,0:T(8,128)S(1)} %get-tuple-element.59.tf_ref.refs_6_, ...), custom_call_target="tpu_custom_call" | custom-call | tf_op jit(solution)/shard_map/pallas_call | solution.py:550
  16.0 0.4 %shard_map.155.refs_2_ = f32[4,1024]{1,0:T(4,128)S(1)} custom-call(bf16[64,512]{1,0:T(8,128)(2,1)S(1)} %collective-permute-done.3.x_ref, f32[4,64,512]{2,1,0:T(8,128)S(1)} %get-tuple-element.57.ta_ref.refs_4_, f32[4,64,512]{2,1,0:T(8,128)S(1)} %get-tuple-element.58.tb_ref.refs_5_, f32[4,64,128]{2,1,0:T(8,128)S(1)} %get-tuple-element.59.tf_ref.refs_6_, ...), custom_call_target="tpu_custom_call" | custom-call | tf_op jit(solution)/shard_map/pallas_call | solution.py:550
  16.4 1.2 %collective-permute-done.4.refs_3_ = bf16[64,512]{1,0:T(8,128)(2,1)S(1)} collective-permute-done((bf16[64,512]{1,0:T(8,128)(2,1)S(1)}, bf16[64,512]{1,0:T(8,128)(2,1)S(1)}, u32[]{:S(2)}, u32[]{:S(2)}) %collective-permute-start.4) | collective-permute-done | bytes 65568 | tf_op jit(solution)/shard_map/ppermute | solution.py:565
  17.7 0.8 %shard_map.156 = (f32[4,16,128]{2,1,0:T(8,128)S(1)}, bf16[4,16,128]{2,1,0:T(8,128)(2,1)S(1)}) custom-call(f32[4,1024]{1,0:T(4,128)S(1)} %get-tuple-element.56.before_ref.refs_0_, f32[4,1024]{1,0:T(4,128)S(1)} %shard_map.154.before_ref.refs_1_, f32[4,1024]{1,0:T(4,128)S(1)} %shard_map.155.refs_2_, bf16[64,512]{1,0:T(8,128)(2,1)S(1)} %collective-permute-done.4.refs_3_, ...), custom_call_target="tpu_custom_call" | custom-call | tf_op jit(solution)/shard_map/pallas_call | solution.py:550
  18.5 1.6 %collective-permute-start.5 = (bf16[4,16,128]{2,1,0:T(8,128)(2,1)S(1)}, bf16[4,16,128]{2,1,0:T(8,128)(2,1)S(1)}, u32[]{:S(2)}, u32[]{:S(2)}) collective-permute-start(bf16[4,16,128]{2,1,0:T(8,128)(2,1)S(1)} %get-tuple-element.61), channel_id=1, source_target_pairs={{0,2},{2,0},{4,6},{6,4},{1,3},{3,1},{5,7},{7,5},{8,10},{10,8},{12,... | collective-permute-start | bytes 49160 | tf_op jit(solution)/shard_map/ppermute | solution.py:678
  20.1 0.8 %collective-permute-done.5.got_ref = bf16[4,16,128]{2,1,0:T(8,128)(2,1)S(1)} collective-permute-done((bf16[4,16,128]{2,1,0:T(8,128)(2,1)S(1)}, bf16[4,16,128]{2,1,0:T(8,128)(2,1)S(1)}, u32[]{:S(2)}, u32[]{:S(2)}) %collective-permute-start.5) | collective-permute-done | bytes 16416 | tf_op jit(solution)/shard_map/ppermute | solution.py:678
  20.9 1.5 %collective-permute-start.6 = (bf16[16,128]{1,0:T(8,128)(2,1)S(1)}, bf16[16,128]{1,0:T(8,128)(2,1)S(1)}, u32[]{:S(2)}, u32[]{:S(2)}) collective-permute-start(bf16[16,128]{1,0:T(8,128)(2,1)S(1)} %get-tuple-element.63), channel_id=1, source_target_pairs={{0,1},{1,0},{2,3},{3,2},{4,5},{5,4},{6,7},{7,6},{8,9},{9,8},{10,11... | collective-permute-start | bytes 12296 | tf_op jit(solution)/shard_map/ppermute | solution.py:684
  22.4 1.5 %collective-permute-start.7 = (bf16[16,128]{1,0:T(8,128)(2,1)S(1)}, bf16[16,128]{1,0:T(8,128)(2,1)S(1)}, u32[]{:S(2)}, u32[]{:S(2)}) collective-permute-start(bf16[16,128]{1,0:T(8,128)(2,1)S(1)} %get-tuple-element.64), channel_id=1, source_target_pairs={{0,4},{1,5},{2,6},{3,7},{4,0},{5,1},{6,2},{7,3},{8,12},{9,13},{10,... | collective-permute-start | bytes 12296 | tf_op jit(solution)/shard_map/ppermute | solution.py:684
  23.9 0.5 %collective-permute-start.8 = (bf16[16,128]{1,0:T(8,128)(2,1)S(1)}, bf16[16,128]{1,0:T(8,128)(2,1)S(1)}, u32[]{:S(2)}, u32[]{:S(2)}) collective-permute-start(bf16[16,128]{1,0:T(8,128)(2,1)S(1)} %get-tuple-element.65), channel_id=1, source_target_pairs={{0,5},{1,4},{2,7},{3,6},{4,1},{5,0},{6,3},{7,2},{8,13},{9,12},{10,... | collective-permute-start | bytes 12296 | tf_op jit(solution)/shard_map/ppermute | solution.py:684
  24.4 0.1 collective-permute-done.6
  24.5 1.5 %collective-permute-done.7 = bf16[16,128]{1,0:T(8,128)(2,1)S(1)} collective-permute-done((bf16[16,128]{1,0:T(8,128)(2,1)S(1)}, bf16[16,128]{1,0:T(8,128)(2,1)S(1)}, u32[]{:S(2)}, u32[]{:S(2)}) %collective-permute-start.7) | collective-permute-done | bytes 4128 | tf_op jit(solution)/shard_map/ppermute | solution.py:684
  26.0 2.4 %collective-permute-done.8 = bf16[16,128]{1,0:T(8,128)(2,1)S(1)} collective-permute-done((bf16[16,128]{1,0:T(8,128)(2,1)S(1)}, bf16[16,128]{1,0:T(8,128)(2,1)S(1)}, u32[]{:S(2)}, u32[]{:S(2)}) %collective-permute-start.8) | collective-permute-done | bytes 4128 | tf_op jit(solution)/shard_map/ppermute | solution.py:684
  28.4 0.6 %convert_add_fusion = f32[16,128]{1,0:T(8,128)} fusion(bf16[16,128]{1,0:T(8,128)(2,1)S(1)} %collective-permute-done.8, bf16[16,128]{1,0:T(8,128)(2,1)S(1)} %collective-permute-done.7, f32[16,128]{1,0:T(8,128)S(1)} %get-tuple-element.62, bf16[16,128]{1,0:T(8,128)(2,1)S(1)} %collective-permute-done.6), kind=kLoop, calls=%fused_computation | loop fusion | flops 12288 | bytes 28672 | tf_op jit(solution)/shard_map/add | solution.py:685
  (10 shorter events, 0.0 us)
Async XLA Ops:
  1.7 3.6 %collective-permute-start = (bf16[8,512]{1,0:T(8,128)(2,1)S(1)}, bf16[8,512]{1,0:T(8,128)(2,1)S(1)}, u32[]{:S(2)}, u32[]{:S(2)}) collective-permute-start(bf16[8,512]{1,0:T(8,128)(2,1)S(1)} %get-tuple-element.47), channel_id=1, source_target_pairs={{0,2},{2,0},{4,6},{6,4},{1,3},{3,1},{5,7},{7,5},{8,10},{10,8},{12,... | collective-permute-start | bytes 24584 | tf_op jit(solution)/shard_map/ppermute | solution.py:593
  2.2 3.1 %collective-permute-start.1 = (bf16[8,512]{1,0:T(8,128)(2,1)S(1)}, bf16[8,512]{1,0:T(8,128)(2,1)S(1)}, u32[]{:S(2)}, u32[]{:S(2)}) collective-permute-start(bf16[8,512]{1,0:T(8,128)(2,1)S(1)} %get-tuple-element.48), channel_id=1, source_target_pairs={{2,4},{4,2},{3,5},{5,3},{10,12},{12,10},{11,13},{13,11},{18,20},{2... | collective-permute-start | bytes 24584 | tf_op jit(solution)/shard_map/ppermute | solution.py:595
  5.3 8.6 %copy-start = (bf16[512,1024]{1,0:T(8,128)(2,1)S(1)}, bf16[512,1024]{1,0:T(8,128)(2,1)}, u32[]{:S(2)}) copy-start(bf16[512,1024]{1,0:T(8,128)(2,1)} %constant.5.clone.split_ref.refs_8_) | copy-start | bytes 3145732
  5.3 8.6 %copy-start.1 = (bf16[512,1024]{1,0:T(8,128)(2,1)S(1)}, bf16[512,1024]{1,0:T(8,128)(2,1)}, u32[]{:S(2)}) copy-start(bf16[512,1024]{1,0:T(8,128)(2,1)} %constant.4.clone.table_ref.refs_7_) | copy-start | bytes 3145732
  5.3 8.5 %copy-start.2 = (bf16[4,64,512]{2,1,0:T(8,128)(2,1)S(1)}, bf16[4,64,512]{2,1,0:T(8,128)(2,1)}, u32[]{:S(2)}) copy-start(bf16[4,64,512]{2,1,0:T(8,128)(2,1)} %t_ref.1) | copy-start | bytes 786436
  7.3 8.2 %collective-permute-start.2 = (bf16[64,512]{1,0:T(8,128)(2,1)S(1)}, bf16[64,512]{1,0:T(8,128)(2,1)S(1)}, u32[]{:S(2)}, u32[]{:S(2)}) collective-permute-start(bf16[64,512]{1,0:T(8,128)(2,1)S(1)} %shard_map.152.x_ref), channel_id=1, source_target_pairs={{0,8},{8,16},{16,24},{24,0},{1,9},{9,17},{17,25},{25,1},{2,10},{10... | collective-permute-start | bytes 196616 | tf_op jit(solution)/shard_map/ppermute | solution.py:565
  9.9 6.1 %collective-permute-start.3 = (bf16[64,512]{1,0:T(8,128)(2,1)S(1)}, bf16[64,512]{1,0:T(8,128)(2,1)S(1)}, u32[]{:S(2)}, u32[]{:S(2)}) collective-permute-start(bf16[64,512]{1,0:T(8,128)(2,1)S(1)} %shard_map.152.x_ref), channel_id=1, source_target_pairs={{0,16},{8,24},{16,0},{24,8},{1,17},{9,25},{17,1},{25,9},{2,18},{10... | collective-permute-start | bytes 196616 | tf_op jit(solution)/shard_map/ppermute | solution.py:565
  12.5 5.1 %collective-permute-start.4 = (bf16[64,512]{1,0:T(8,128)(2,1)S(1)}, bf16[64,512]{1,0:T(8,128)(2,1)S(1)}, u32[]{:S(2)}, u32[]{:S(2)}) collective-permute-start(bf16[64,512]{1,0:T(8,128)(2,1)S(1)} %shard_map.152.x_ref), channel_id=1, source_target_pairs={{0,24},{8,0},{16,8},{24,16},{1,25},{9,1},{17,9},{25,17},{2,26},{10... | collective-permute-start | bytes 196616 | tf_op jit(solution)/shard_map/ppermute | solution.py:565
  18.5 2.4 %collective-permute-start.5 = (bf16[4,16,128]{2,1,0:T(8,128)(2,1)S(1)}, bf16[4,16,128]{2,1,0:T(8,128)(2,1)S(1)}, u32[]{:S(2)}, u32[]{:S(2)}) collective-permute-start(bf16[4,16,128]{2,1,0:T(8,128)(2,1)S(1)} %get-tuple-element.61), channel_id=1, source_target_pairs={{0,2},{2,0},{4,6},{6,4},{1,3},{3,1},{5,7},{7,5},{8,10},{10,8},{12,... | collective-permute-start | bytes 49160 | tf_op jit(solution)/shard_map/ppermute | solution.py:678
  20.9 3.6 %collective-permute-start.6 = (bf16[16,128]{1,0:T(8,128)(2,1)S(1)}, bf16[16,128]{1,0:T(8,128)(2,1)S(1)}, u32[]{:S(2)}, u32[]{:S(2)}) collective-permute-start(bf16[16,128]{1,0:T(8,128)(2,1)S(1)} %get-tuple-element.63), channel_id=1, source_target_pairs={{0,1},{1,0},{2,3},{3,2},{4,5},{5,4},{6,7},{7,6},{8,9},{9,8},{10,11... | collective-permute-start | bytes 12296 | tf_op jit(solution)/shard_map/ppermute | solution.py:684
  22.4 3.6 %collective-permute-start.7 = (bf16[16,128]{1,0:T(8,128)(2,1)S(1)}, bf16[16,128]{1,0:T(8,128)(2,1)S(1)}, u32[]{:S(2)}, u32[]{:S(2)}) collective-permute-start(bf16[16,128]{1,0:T(8,128)(2,1)S(1)} %get-tuple-element.64), channel_id=1, source_target_pairs={{0,4},{1,5},{2,6},{3,7},{4,0},{5,1},{6,2},{7,3},{8,12},{9,13},{10,... | collective-permute-start | bytes 12296 | tf_op jit(solution)/shard_map/ppermute | solution.py:684
  23.9 4.5 %collective-permute-start.8 = (bf16[16,128]{1,0:T(8,128)(2,1)S(1)}, bf16[16,128]{1,0:T(8,128)(2,1)S(1)}, u32[]{:S(2)}, u32[]{:S(2)}) collective-permute-start(bf16[16,128]{1,0:T(8,128)(2,1)S(1)} %get-tuple-element.65), channel_id=1, source_target_pairs={{0,5},{1,4},{2,7},{3,6},{4,1},{5,0},{6,3},{7,2},{8,13},{9,12},{10,... | collective-permute-start | bytes 12296 | tf_op jit(solution)/shard_map/ppermute | solution.py:684
